TPU v7x, 32 devices: a whole 2x2x4 slice. The times are simulated.
32 devices in a mesh: ctx: 4 (over y, x), fsdp: 8 (over z, core).
Axes of the slice: x: 2, y: 2, z: 4, core: 2. Of those that a mesh axis runs over, the one named last changes fastest.
Arguments:
- tokens: bfloat16 [8, 1024, 2048], P('fsdp', 'ctx'), may hold values from -6 to 6
- block_ids: int32 [8, 1024], P('fsdp'), may hold values from 0 to 7, never falling along the last dimension, each value on 1 to 256 neighbouring positions
- piece_order: int32 [8], replicated, may hold values from 0 to 7, as said below
- norm1_gain: float32 [2048], replicated, may hold values from 0.5 to 1.5
- norm1_bias: float32 [2048], replicated, may hold values from -1 to 1
- w_qkv: bfloat16 [2048, 6144], P('fsdp'), may hold values from -0.125 to 0.125
- w_out: bfloat16 [2048, 2048], P('fsdp'), may hold values from -1 to 1
- norm2_gain: float32 [2048], replicated, may hold values from 0.5 to 1.5
- norm2_bias: float32 [2048], replicated, may hold values from -1 to 1
- w_up: bfloat16 [2048, 8192], P('fsdp'), may hold values from -0.125 to 0.125
- w_down: bfloat16 [2048, 8192], P('fsdp'), may hold values from -0.0625 to 0.0625
- grad_out: bfloat16 [8, 1024, 2048], P('fsdp', 'ctx'), may hold values from -6 to 6
Outputs:
- mixed: bfloat16 [8, 1024, 2048], P('fsdp', 'ctx')
- grad_tokens: bfloat16 [8, 1024, 2048], P('fsdp', 'ctx')
- grad_qkv: float32 [2048, 6144], P(('ctx', 'fsdp'))
- grad_wout: float32 [2048, 2048], P(('ctx', 'fsdp'))
- grad_up: float32 [2048, 8192], P(('ctx', 'fsdp'))
- grad_down: float32 [2048, 8192], P(('ctx', 'fsdp'))
- grad_norm1_gain: float32 [2048], replicated
- grad_norm1_bias: float32 [2048], replicated
- grad_norm2_gain: float32 [2048], replicated
- grad_norm2_bias: float32 [2048], replicated
Inputs may be any that keep to these rules, and one draw needn't show every extreme that they name: `block_ids`: within a sequence the block numbers never fall along positions; every block covers 1 to 256 positions and some block exactly 256. `piece_order`: each piece appears once; stored pieces 2c and 2c + 1 hold pieces p and 7 - p for some p.
All inputs are finite; a program needn't handle non-finite values.
Results may differ from a plain program's by a relative error of at most 0.014.
Values may be sent and summed in bfloat16 or wider, within the bound.
A program may use at most 896 MiB of HBM per device.

v0:
```python
import functools
import math

import jax
import jax.numpy as jnp
from jax import lax
from jax.sharding import PartitionSpec as P

HEADS = 16


norm_eps = 1e-05


def stored_blocks(seq_blocks, piece_order, piece_len):
    row_index = jnp.arange(seq_blocks.shape[-1], dtype=jnp.int32)
    stored_pos = piece_order[row_index // piece_len] * piece_len + row_index % piece_len
    return jnp.take(seq_blocks, stored_pos, axis=-1)


def normalize(values, norm_gain, norm_bias):
    center = values - jnp.mean(values, axis=-1, keepdims=True)
    variance = jnp.mean(center * center, axis=-1, keepdims=True)
    inv_std = lax.rsqrt(variance + norm_eps)
    unit_vals = center * inv_std
    return (unit_vals * norm_gain + norm_bias, unit_vals, inv_std)


def normalize_back(grad_normed, unit_vals, inv_std, norm_gain):
    grad_unit = grad_normed * norm_gain
    mean_first = jnp.mean(grad_unit, axis=-1, keepdims=True)
    mean_second = jnp.mean(grad_unit * unit_vals, axis=-1, keepdims=True)
    return inv_std * (grad_unit - mean_first - unit_vals * mean_second)


def contract_last(left_arr, right_arr):
    return lax.dot_general(
        left_arr, right_arr, (((1,), (1,)), ((), ())), preferred_element_type=jnp.float32
    )


def contract_first(left_arr, right_arr):
    return lax.dot_general(
        left_arr, right_arr, (((0,), (0,)), ((), ())), preferred_element_type=jnp.float32
    )


def split_heads(flat_arr):
    return flat_arr.reshape(flat_arr.shape[0], flat_arr.shape[1], HEADS, -1)


def shards(
    tokens,
    block_ids,
    piece_order,
    norm1_gain,
    norm1_bias,
    w_qkv,
    w_out,
    norm2_gain,
    norm2_bias,
    w_up,
    w_down,
    grad_out,
):
    micro_count, row_count, model_width = (tokens.shape[0], tokens.shape[1], tokens.shape[2])
    total_rows = micro_count * row_count
    head_size = model_width // HEADS
    hidden_width = w_up.shape[1]
    score_scale = 1.0 / math.sqrt(head_size)
    seq_blocks = stored_blocks(block_ids, piece_order, row_count // 2)
    query_blocks = lax.dynamic_slice_in_dim(
        seq_blocks, lax.axis_index("ctx") * row_count, row_count, 1
    )
    visible = seq_blocks[:, None, None, :] <= query_blocks[:, None, :, None]
    inputs = tokens.reshape(total_rows, model_width).astype(jnp.float32)
    normed_one, unit_one, inv_one = normalize(inputs, norm1_gain, norm1_bias)
    act_one = normed_one.astype(jnp.bfloat16)
    full_qkv, full_out = (
        lax.all_gather(w_qkv, "fsdp", axis=0, tiled=True),
        lax.all_gather(w_out, "fsdp", axis=0, tiled=True),
    )
    projected = jnp.dot(act_one, full_qkv, preferred_element_type=jnp.float32).astype(jnp.bfloat16)
    queries = projected[:, :model_width].reshape(micro_count, row_count, HEADS, head_size)
    key_local = projected[:, model_width : 2 * model_width].reshape(
        micro_count, row_count, model_width
    )
    value_local = projected[:, 2 * model_width :].reshape(micro_count, row_count, model_width)
    key_all, value_all = (
        lax.all_gather(key_local, "ctx", axis=1, tiled=True),
        lax.all_gather(value_local, "ctx", axis=1, tiled=True),
    )
    seq_len = key_all.shape[1]

    def scores_of(key_source):
        raw_scores = jnp.einsum(
            "mqhd,mkhd->mhqk", queries, split_heads(key_source), preferred_element_type=jnp.float32
        )
        return jnp.where(visible, raw_scores * score_scale, -jnp.inf)

    scores = scores_of(key_all)
    row_max = jnp.max(scores, axis=-1, keepdims=True)
    exp_scores = jnp.exp(scores - row_max)
    row_total = jnp.sum(exp_scores, axis=-1, keepdims=True)
    attn_prob = (exp_scores / row_total).astype(jnp.bfloat16)
    log_total = row_max + jnp.log(row_total)
    attended = jnp.einsum(
        "mhqk,mkhd->mqhd", attn_prob, split_heads(value_all), preferred_element_type=jnp.float32
    )
    attended = attended.reshape(total_rows, model_width).astype(jnp.bfloat16)
    residual = inputs + jnp.dot(attended, full_out, preferred_element_type=jnp.float32)
    normed_two, unit_two, inv_two = normalize(residual, norm2_gain, norm2_bias)
    act_two = normed_two.astype(jnp.bfloat16)
    full_up, full_down = (
        lax.all_gather(w_up, "fsdp", axis=0, tiled=True),
        lax.all_gather(w_down, "fsdp", axis=0, tiled=True),
    )
    pre_act = jnp.dot(act_two, full_up, preferred_element_type=jnp.float32)
    gelu_tanh = functools.partial(jax.nn.gelu, approximate=True)
    hidden_full, gelu_pull = jax.vjp(gelu_tanh, pre_act)
    hidden = hidden_full.astype(jnp.bfloat16)
    mixed = residual + contract_last(hidden, full_down)
    grad_y = grad_out.reshape(total_rows, model_width)
    grad_hidden = jnp.dot(grad_y, full_down, preferred_element_type=jnp.float32)
    grad_pre = gelu_pull(grad_hidden)[0].astype(jnp.bfloat16)
    grad_act_two = contract_last(grad_pre, full_up)
    grad_res = grad_y.astype(jnp.float32) + normalize_back(
        grad_act_two, unit_two, inv_two, norm2_gain
    )
    act_rows = act_two
    up_part = contract_first(act_rows, grad_pre)
    down_part = contract_first(grad_y, hidden)
    grad_mlp = lax.psum_scatter(
        jnp.concatenate([up_part, down_part], axis=1),
        ("ctx", "fsdp"),
        scatter_dimension=0,
        tiled=True,
    )
    back_qkv, back_out = (
        lax.all_gather(w_qkv, "fsdp", axis=0, tiled=True),
        lax.all_gather(w_out, "fsdp", axis=0, tiled=True),
    )
    grad_res_low = grad_res.astype(jnp.bfloat16)
    grad_attended = contract_last(grad_res_low, back_out).astype(jnp.bfloat16)
    grad_heads = grad_attended.reshape(micro_count, row_count, HEADS, head_size)
    back_keys, back_values = (key_all, value_all)
    prob_full = jnp.exp(scores_of(back_keys) - log_total)
    prob_low = prob_full.astype(jnp.bfloat16)
    grad_prob = jnp.einsum(
        "mqhd,mkhd->mhqk", grad_heads, split_heads(back_values), preferred_element_type=jnp.float32
    )
    row_dot = jnp.sum(prob_full * grad_prob, axis=-1, keepdims=True)
    grad_raw = (prob_full * (grad_prob - row_dot) * score_scale).astype(jnp.bfloat16)
    grad_query = jnp.einsum(
        "mhqk,mkhd->mqhd", grad_raw, split_heads(back_keys), preferred_element_type=jnp.float32
    )
    grad_query = grad_query.reshape(total_rows, model_width).astype(jnp.bfloat16)
    key_terms = jnp.einsum(
        "mhqk,mqhd->mkhd", grad_raw, queries, preferred_element_type=jnp.float32
    ).reshape(micro_count, seq_len, model_width)
    value_terms = jnp.einsum(
        "mhqk,mqhd->mkhd", prob_low, grad_heads, preferred_element_type=jnp.float32
    ).reshape(micro_count, seq_len, model_width)
    grad_keys, grad_values = (
        lax.psum_scatter(
            key_terms.astype(jnp.bfloat16), "ctx", scatter_dimension=1, tiled=True
        ).astype(jnp.float32),
        lax.psum_scatter(
            value_terms.astype(jnp.bfloat16), "ctx", scatter_dimension=1, tiled=True
        ).astype(jnp.float32),
    )
    grad_proj = jnp.concatenate(
        [
            grad_query,
            grad_keys.reshape(total_rows, model_width).astype(jnp.bfloat16),
            grad_values.reshape(total_rows, model_width).astype(jnp.bfloat16),
        ],
        axis=1,
    )
    grad_act_one = contract_last(grad_proj, back_qkv)
    grad_inputs = grad_res + normalize_back(grad_act_one, unit_one, inv_one, norm1_gain)
    act_rows = act_one
    proj_part = contract_first(act_rows, grad_proj)
    out_part = contract_first(attended, grad_res_low)
    grad_attn_all = lax.psum_scatter(
        jnp.concatenate([proj_part, out_part], axis=1),
        ("ctx", "fsdp"),
        scatter_dimension=0,
        tiled=True,
    )
    norm_sums = (
        jnp.sum(grad_act_one * unit_one, axis=0),
        jnp.sum(grad_act_one, axis=0),
        jnp.sum(grad_act_two * unit_two, axis=0),
        jnp.sum(grad_act_two, axis=0),
    )
    gain_one_sum, bias_one_sum, gain_two_sum, bias_two_sum = lax.psum(
        (norm_sums[0], norm_sums[1], norm_sums[2], norm_sums[3]), ("ctx", "fsdp")
    )
    out_shape = (micro_count, row_count, model_width)
    return (
        mixed.reshape(out_shape).astype(jnp.bfloat16),
        grad_inputs.reshape(out_shape).astype(jnp.bfloat16),
        grad_attn_all[:, : 3 * model_width],
        grad_attn_all[:, 3 * model_width :],
        grad_mlp[:, :hidden_width],
        grad_mlp[:, hidden_width:],
        gain_one_sum,
        bias_one_sum,
        gain_two_sum,
        bias_two_sum,
    )


def solution(mesh):
    return jax.shard_map(
        shards,
        mesh=mesh,
        in_specs=(
            P("fsdp", "ctx", None),
            P("fsdp", None),
            P(),
            P(),
            P(),
            P("fsdp", None),
            P("fsdp", None),
            P(),
            P(),
            P("fsdp", None),
            P("fsdp", None),
            P("fsdp", "ctx", None),
        ),
        out_specs=(
            P("fsdp", "ctx", None),
            P("fsdp", "ctx", None),
            P(("ctx", "fsdp"), None),
            P(("ctx", "fsdp"), None),
            P(("ctx", "fsdp"), None),
            P(("ctx", "fsdp"), None),
            P(),
            P(),
            P(),
            P(),
        ),
        check_vma=False,
    )
```

profile of v0, /device:TPU:0, one launch (start us, length us, event | category | flops | bytes accessed | tf_op | source)
XLA Modules:
  0.0 3859.2 jit_solution(6889009653711367241)
XLA Ops:
  11.1 221.2 %all-gather.9.cloned.1.call-done = bf16[2048,6144]{1,0:T(8,128)(2,1)} async-done(((bf16[256,6144]{1,0:T(8,128)(2,1)}), bf16[2048,6144]{1,0:T(8,128)(2,1)}) %all-gather.9.cloned.1.call-update) | async-done | bytes 25165840 | tf_op jit(solution)/shard_map/all_gather | solution.py:80
  232.3 12.1 convolution_convert_fusion
  260.0 37.0 all-gather.19.cloned.1.call-done
  297.0 6.4 copy.55
  303.4 5.3 fusion.89
  308.7 5.7 copy-done.2
  318.2 34.0 all-gather.17.cloned.1.call-done
  352.1 10.6 fusion.57
  362.8 72.9 %all-gather.11.cloned.1.call-done = bf16[2048,2048]{1,0:T(8,128)(2,1)} async-done(((bf16[256,2048]{1,0:T(8,128)(2,1)}), bf16[2048,2048]{1,0:T(8,128)(2,1)}) %all-gather.11.cloned.1.call-update) | async-done | bytes 8388624 | tf_op jit(solution)/shard_map/all_gather | solution.py:81
  435.7 6.2 fusion.90
  442.3 282.0 %all-gather.13.cloned.1.call-done = bf16[2048,8192]{1,0:T(8,128)(2,1)} async-done(((bf16[256,8192]{1,0:T(8,128)(2,1)}), bf16[2048,8192]{1,0:T(8,128)(2,1)}) %all-gather.13.cloned.1.call-update) | async-done | bytes 33554448 | tf_op jit(solution)/shard_map/all_gather | solution.py:115
  724.3 21.3 fusion.85
  745.6 267.0 %all-gather.15.cloned.1.call-done = bf16[2048,8192]{1,0:T(8,128)(2,1)} async-done(((bf16[256,8192]{1,0:T(8,128)(2,1)}), bf16[2048,8192]{1,0:T(8,128)(2,1)}) %all-gather.15.cloned.1.call-update) | async-done | bytes 33554448 | tf_op jit(solution)/shard_map/all_gather | solution.py:116
  1012.6 21.4 fusion.12
  1034.1 18.7 multiply_reduce_fusion.1
  1056.7 6.7 convolution_convert_fusion.1
  1064.9 8.8 fusion.32
  1073.8 10.3 fusion.25
  1084.1 32.6 fusion.29
  1116.7 25.6 fusion.84
  1142.4 28.7 convolution_bitcast_fusion
  1171.1 87.9 %pad_maximum_fusion = f32[2048,16384]{1,0:T(8,128)} fusion(f32[2048,8192]{1,0:T(8,128)} %convolution_bitcast_fusion, f32[2048,8192]{1,0:T(8,128)} %fusion.84), kind=kLoop, calls=%fused_computation.2 | loop fusion | flops 33554432 | bytes 268435456 | tf_op jit(solution)/shard_map/concatenate | solution.py:134
  1259.8 32.8 fusion.54
  1292.7 9.4 fusion.68
  1302.1 22.1 fusion.60
  1324.2 45.9 %pad_maximum_fusion.1 = f32[2048,8192]{1,0:T(8,128)} fusion(f32[2048,2048]{1,0:T(8,128)} %fusion.68, f32[2048,6144]{1,0:T(8,128)} %fusion.60), kind=kLoop, calls=%fused_computation.3 | loop fusion | flops 16777216 | bytes 134217728 | tf_op jit(solution)/shard_map/concatenate | solution.py:186
  1371.7 18.7 fusion.44
  1390.4 15.0 fusion.52
  1405.4 40.4 %all-reduce.1 = (f32[2048]{0:T(1024)}, f32[2048]{0:T(1024)}, f32[2048]{0:T(1024)}, f32[2048]{0:T(1024)}) all-reduce(f32[2048]{0:T(1024)S(1)} %get-tuple-element.12, f32[2048]{0:T(1024)S(1)} %get-tuple-element.17, f32[2048]{0:T(1024)S(1)} %copy-done.24, f32[2048]{0:T(1024)S(1)} %copy-done.25), channel_id=1, replica_groups=mesh['ctx'=4,'fsdp'=8] {'ctx','fsdp'}, use_global_device_ids=true, to_apply=%region_16.17 | all-reduce | flops 8192 | bytes 65536 | tf_op jit(solution)/shard_map/psum | solution.py:197
  1449.3 1687.3 %all-reduce.4.cloned.1.call-done = f32[2048,16384]{1,0:T(8,128)} async-done(((f32[2048,16384]{1,0:T(8,128)}), f32[2048,16384]{1,0:T(8,128)}) %all-reduce.4.cloned.1.call-update) | async-done | bytes 134217744
  3136.6 4.9 fusion.86
  3141.5 706.0 %reduce-scatter.8.cloned.1.call-done = f32[64,8192]{1,0:T(8,128)} async-done(((f32[2048,8192]{1,0:T(8,128)}), f32[64,8192]{1,0:T(8,128)}) %reduce-scatter.8.cloned.1.call-update) | async-done | bytes 2097168 | tf_op jit(solution)/shard_map/reduce_scatter | solution.py:185
  (103 shorter events, 39.2 us)
Async XLA Ops:
  7.2 247.5 %copy-start = (s32[1,1024]{1,0:T(1,128)S(1)}, s32[1,1024]{1,0:T(1,128)}, u32[]{:S(2)}) copy-start(s32[1,1024]{1,0:T(1,128)} %param.13) | copy-start | bytes 12292
  7.2 225.1 %all-gather.9.cloned.1.call-start = ((), (), s32[]{:S(2)}) async-start(), calls=%async_computation.3 | async-start | bytes 28311552 | tf_op jit(solution)/shard_map/all_gather | solution.py:80
  7.9 289.1 %all-gather.19.cloned.1.call-start = ((), (), s32[]{:S(2)}) async-start(), calls=%async_computation.11 | async-start | bytes 5242880 | tf_op jit(solution)/shard_map/all_gather | solution.py:90
  9.4 234.9 %copy-start.17 = (f32[256]{0:T(256)}, f32[256]{0:T(256)S(1)}, u32[]{:S(2)}) copy-start(f32[256]{0:T(256)S(1)} %broadcast_multiply_fusion.5) | copy-start | bytes 3076
  11.1 233.3 %copy-start.19 = (f32[256]{0:T(256)}, f32[256]{0:T(256)S(1)}, u32[]{:S(2)}) copy-start(f32[256]{0:T(256)S(1)} %add_rsqrt_fusion.1) | copy-start | bytes 3076
  245.9 106.2 %all-gather.17.cloned.1.call-start = ((), (), s32[]{:S(2)}) async-start(), calls=%async_computation.10 | async-start | bytes 5242880 | tf_op jit(solution)/shard_map/all_gather | solution.py:91
  246.7 189.0 %all-gather.11.cloned.1.call-start = ((), (), s32[]{:S(2)}) async-start(), calls=%async_computation.4 | async-start | bytes 9437184 | tf_op jit(solution)/shard_map/all_gather | solution.py:81
  247.2 477.1 %all-gather.13.cloned.1.call-start = ((), (), s32[]{:S(2)}) async-start(), calls=%async_computation.5 | async-start | bytes 37748736 | tf_op jit(solution)/shard_map/all_gather | solution.py:115
  247.8 764.8 %all-gather.15.cloned.1.call-start = ((), (), s32[]{:S(2)}) async-start(), calls=%async_computation.6 | async-start | bytes 37748736 | tf_op jit(solution)/shard_map/all_gather | solution.py:116
  248.4 1053.7 %reduce-scatter.6.cloned.1.call-start = ((), (), s32[]{:S(2)}) async-start(), calls=%async_computation.8 | async-start | bytes 5242880 | tf_op jit(solution)/shard_map/reduce_scatter | solution.py:168
  260.0 48.7 %copy-start.12 = (bf16[256,2048]{0,1:T(8,128)(2,1)}, bf16[256,2048]{0,1:T(8,128)(2,1)S(1)}, u32[]{:S(2)}) copy-start(bf16[256,2048]{0,1:T(8,128)(2,1)S(1)} %copy.54) | copy-start | bytes 3145732
  308.7 5.7 copy-start.2
  318.2 117.5 %copy-start.5 = (bf16[1,256,2048]{2,1,0:T(8,128)(2,1)S(1)}, bf16[1,256,2048]{2,1,0:T(8,128)(2,1)}, u32[]{:S(2)}) copy-start(bf16[1,256,2048]{2,1,0:T(8,128)(2,1)} %param.12) | copy-start | bytes 3145732
  435.7 288.6 %copy-start.15 = (f32[2048]{0:T(1024)S(1)}, f32[2048]{0:T(1024)}, u32[]{:S(2)}) copy-start(f32[2048]{0:T(1024)} %param.19) | copy-start | bytes 24580
  435.7 288.6 %copy-start.16 = (f32[2048]{0:T(1024)S(1)}, f32[2048]{0:T(1024)}, u32[]{:S(2)}) copy-start(f32[2048]{0:T(1024)} %param.20) | copy-start | bytes 24580
  441.9 674.8 %copy-start.3 = (f32[256,2048]{1,0:T(8,128)}, f32[256,2048]{1,0:T(8,128)S(1)}, u32[]{:S(2)}) copy-start(f32[256,2048]{1,0:T(8,128)S(1)} %get-tuple-element.38) | copy-start | bytes 6291460
  442.3 641.8 %copy-start.21 = (f32[16,256]{1,0:T(8,128)}, f32[16,256]{1,0:T(8,128)S(1)}, u32[]{:S(2)}) copy-start(f32[16,256]{1,0:T(8,128)S(1)} %log_add_fusion) | copy-start | bytes 49156
  442.3 570.3 %copy-start.10 = (bf16[1,256,2048]{2,1,0:T(8,128)(2,1)S(1)}, bf16[1,256,2048]{2,1,0:T(8,128)(2,1)}, u32[]{:S(2)}) copy-start(bf16[1,256,2048]{2,1,0:T(8,128)(2,1)} %param.23) | copy-start | bytes 3145732
  1073.7 228.4 %reduce-scatter.4.cloned.1.call-start = ((), (), s32[]{:S(2)}) async-start(), calls=%async_computation.7 | async-start | bytes 5242880 | tf_op jit(solution)/shard_map/reduce_scatter | solution.py:165
  1116.7 25.7 copy-start.11
  1142.3 1994.3 %all-reduce.4.cloned.1.call-start = ((), (), s32[]{:S(2)}) async-start(), calls=%async_computation.12 | async-start | bytes 268435456
  1259.1 33.5 copy-start.8
  1259.1 2588.5 %reduce-scatter.8.cloned.1.call-start = ((), (), s32[]{:S(2)}) async-start(), calls=%async_computation.9 | async-start | bytes 69206016 | tf_op jit(solution)/shard_map/reduce_scatter | solution.py:185
  1292.6 9.5 copy-start.6
  1292.6 9.5 copy-start.13
  1292.6 9.5 copy-start.14
  1292.6 9.5 copy-start.18
  1292.7 9.5 copy-start.20
  1390.4 15.0 copy-start.24
  1390.4 15.0 copy-start.25
  1390.4 55.4 %copy-start.9 = (f32[256,2048]{1,0:T(8,128)S(1)}, f32[256,2048]{1,0:T(8,128)}, u32[]{:S(2)}) copy-start(f32[256,2048]{1,0:T(8,128)} %copy-done.7) | copy-start | bytes 6291460
  1445.8 2406.2 %copy-start.1 = (s32[1,1024]{1,0:T(1,128)S(1)}, s32[1,1024]{1,0:T(1,128)}, u32[]{:S(2)}) copy-start(s32[1,1024]{1,0:T(1,128)} %param.13) | copy-start | bytes 12292
  (4 other events, 6.4 us)
Sparse Core Ops, SparseCore 0:
  9.7 222.5 all-gather.8
  246.1 50.8 all-gather.18
  299.4 52.6 all-gather.16
  353.6 82.0 all-gather.10
  437.1 287.1 all-gather.12
  725.8 286.8 all-gather.14
  1073.8 50.8 reduce-scatter.5
  1142.5 51.5 reduce-scatter.3
  1259.2 1877.3 all-reduce.3
  3138.8 708.6 reduce-scatter.7
where the time goes:
time: 3860 us
  waiting for transfers between devices  3310 us (86%)
  matrix products  306 us (8%)
  other arithmetic  153 us (4%)
  blocking collectives  40.4 us (1%)
    unnamed x11, waiting for transfers between devices  1690 us
    reduce_scatter x1, waiting for transfers between devices, shards(): lax.psum_scatter(jnp.concatenate([proj_part, out_part], axis=1), ('ctx',...  706 us
    all_gather x1, waiting for transfers between devices, shards(): lax.all_gather(w_up, 'fsdp', axis=0, tiled=True)  282 us
    all_gather x1, waiting for transfers between devices, shards(): lax.all_gather(w_down, 'fsdp', axis=0, tiled=True)  267 us
    all_gather x1, waiting for transfers between devices, shards(): lax.all_gather(w_qkv, 'fsdp', axis=0, tiled=True)  221 us
    concatenate x1, other arithmetic, shards(): jnp.concatenate([up_part, down_part], axis=1)  87.9 us
    dot_general x4, matrix products, contract_first(): lax.dot_general(left_arr, right_arr, (((0,), (0,)), ((), ())), preferred_...  85.8 us
  transfers between devices with their start and end apart: 10, of which 8 were waited for; matrix products, arithmetic and copies ran while one was open for 11% of the time, Pallas kernels for 0%

commit v1 on v0

v1 whole, which is shorter than its diff:
```python
import functools
import math

import jax
import jax.numpy as jnp
import numpy as np
from jax import lax
from jax.experimental import pallas as pl
from jax.experimental.pallas import tpu as pltpu
from jax.sharding import Mesh, PartitionSpec as P

HEADS = 16
CORES = 2
LANES = 2
MESH = pl.DeviceIdType.MESH
VMEM_LIMIT = 56 << 20
norm_eps = 1e-05
F32 = jnp.float32
BF16 = jnp.bfloat16


def stored_blocks(seq_blocks, piece_order, piece_len):
    pieces = seq_blocks.reshape(seq_blocks.shape[0], -1, piece_len)
    return jnp.take(pieces, piece_order, axis=1).reshape(seq_blocks.shape)


def normalize(values, norm_gain, norm_bias):
    center = values - jnp.mean(values, axis=-1, keepdims=True)
    variance = jnp.mean(center * center, axis=-1, keepdims=True)
    inv_std = lax.rsqrt(variance + norm_eps)
    unit_vals = center * inv_std
    return (unit_vals * norm_gain + norm_bias, unit_vals, inv_std)


def normalize_back(grad_normed, unit_vals, inv_std, norm_gain):
    grad_unit = grad_normed * norm_gain
    mean_first = jnp.mean(grad_unit, axis=-1, keepdims=True)
    mean_second = jnp.mean(grad_unit * unit_vals, axis=-1, keepdims=True)
    return inv_std * (grad_unit - mean_first - unit_vals * mean_second)


def contract_last(left_arr, right_arr):
    return lax.dot_general(
        left_arr, right_arr, (((1,), (1,)), ((), ())), preferred_element_type=F32
    )


def contract_first(left_arr, right_arr):
    return lax.dot_general(
        left_arr, right_arr, (((0,), (0,)), ((), ())), preferred_element_type=F32
    )


def chip_bits(chips):
    return [1 << i for i in range(chips.bit_length() - 1)]


def lane_orders(chips):
    bits = chip_bits(chips)
    return [bits[lane:] + bits[:lane] for lane in range(LANES)]


def greet(chips, me_chip, me_core):
    barrier = pltpu.get_barrier_semaphore()
    bits = chip_bits(chips)
    for bit in bits:
        pl.semaphore_signal(barrier, inc=1, device_id={"ctx": me_chip ^ bit}, device_id_type=MESH)
    pl.semaphore_signal(barrier, inc=1, device_id={"core": 1 - me_core}, device_id_type=MESH)
    pl.semaphore_wait(barrier, len(bits) + 1)


def gather_kernel(chips, pieces, x_ref, o_ref, own_sem, send_sem, recv_sem):
    c, k = lax.axis_index("ctx"), lax.axis_index("core")
    rows = x_ref.shape[0]
    piece_rows = rows // (LANES * pieces)
    bits, orders = chip_bits(chips), lane_orders(chips)

    def place(core, chip, lane, piece):
        return pl.ds((core * chips + chip) * rows + (lane * pieces + piece) * piece_rows, piece_rows)

    local = pltpu.make_async_copy(x_ref, o_ref.at[pl.ds((k * chips + c) * rows, rows)], own_sem)
    local.start()
    greet(chips, c, k)
    started = []

    def send(source, m, lane, piece, step):
        if step < len(bits):
            bit = orders[lane][step]
            device, kind, landing = {"ctx": c ^ bit}, 0, m ^ bit
        else:
            device, kind, landing = {"core": 1 - k}, 1, m
        copy = pltpu.make_async_remote_copy(
            src_ref=source,
            dst_ref=o_ref.at[place(k, c ^ m, lane, piece)],
            send_sem=send_sem.at[step, m, lane, piece],
            recv_sem=recv_sem.at[kind, landing, lane, piece],
            device_id=device,
            device_id_type=MESH,
        )
        copy.start()
        started.append(copy)

    def arrived(kind, m, lane, piece):
        ref = o_ref.at[place(k if kind == 0 else 1 - k, c ^ m, lane, piece)]
        pltpu.make_async_remote_copy(
            src_ref=ref,
            dst_ref=ref,
            send_sem=send_sem.at[0, m, lane, piece],
            recv_sem=recv_sem.at[kind, m, lane, piece],
            device_id={"core": 1 - k},
            device_id_type=MESH,
        ).wait_recv()

    own = [(p, l) for p in range(pieces) for l in range(LANES)]
    for piece, lane in own:
        source = x_ref.at[pl.ds((lane * pieces + piece) * piece_rows, piece_rows)]
        for step in range(len(bits)):
            send(source, 0, lane, piece, step)
    for piece, lane in own:
        source = x_ref.at[pl.ds((lane * pieces + piece) * piece_rows, piece_rows)]
        send(source, 0, lane, piece, len(bits))
    items = sorted(
        (max(i for i, b in enumerate(orders[lane]) if m & b), piece, lane, m)
        for m in range(1, chips)
        for piece, lane in own
    )
    for step, piece, lane, m in items:
        arrived(0, m, lane, piece)
        source = o_ref.at[place(k, c ^ m, lane, piece)]
        for later in range(step + 1, len(bits) + 1):
            send(source, m, lane, piece, later)
    for m in range(chips):
        for piece, lane in own:
            arrived(1, m, lane, piece)
    for copy in started:
        copy.wait_send()
    local.wait()


def plane_gather(x, chips, ident, pieces=2):
    rows, cols = x.shape
    bits = len(chip_bits(chips))
    return pl.pallas_call(
        functools.partial(gather_kernel, chips, pieces),
        name="plane_gather",
        out_shape=jax.ShapeDtypeStruct((CORES * chips * rows, cols), x.dtype),
        in_specs=[pl.BlockSpec(memory_space=pl.ANY)],
        out_specs=pl.BlockSpec(memory_space=pl.ANY),
        scratch_shapes=[
            pltpu.SemaphoreType.DMA,
            pltpu.SemaphoreType.DMA((bits + 1, chips, LANES, pieces)),
            pltpu.SemaphoreType.DMA((2, chips, LANES, pieces)),
        ],
        cost_estimate=pl.CostEstimate(flops=40_000_000_000, bytes_accessed=0, transcendentals=0),
        compiler_params=pltpu.CompilerParams(collective_id=ident, has_side_effects=True),
    )(x)


def scatter_plan(chips):
    orders = lane_orders(chips)
    slots, sends = {}, {}
    for lane in range(LANES):
        count = 0
        for step, bit in enumerate(orders[lane]):
            gone = sum(orders[lane][: step + 1])
            for m in range(chips):
                if m & gone == 0:
                    slots[lane, step, m] = count
                    count += 1
        for m in range(1, chips):
            sends[m, lane] = min(i for i, b in enumerate(orders[lane]) if m & b)
    units = sorted(
        ((m, lane) for m in range(chips) for lane in range(LANES)),
        key=lambda u: (sends.get(u, len(orders[0])), -bin(u[0]).count("1"), u[1], u[0]),
    )
    return orders, slots, sends, units


def product_scatter_kernel(
    chips, transposed, tile, h_ref, w_ref, o_ref, h_v, w_v, own, theirs, from_core, from_chip,
    load_sem, core_send, core_recv, chip_send, chip_recv,
):
    c, k = lax.axis_index("ctx"), lax.axis_index("core")
    rows, cols = o_ref.shape
    half = rows // LANES
    orders, slots, sends, units = scatter_plan(chips)
    w_load = pltpu.make_async_copy(w_ref, w_v, load_sem.at[0])
    h_load = pltpu.make_async_copy(h_ref, h_v, load_sem.at[1])
    w_load.start()
    h_load.start()
    greet(chips, c, k)
    w_load.wait()
    h_load.wait()
    waits = []

    def lane_rows(lane):
        return pl.ds(lane * half, half)

    def compute(m, lane):
        def rows_for(core):
            start = (core * chips + (c ^ m)) * rows + lane * half
            return h_v[pl.ds(pl.multiple_of(start, half), half), :]

        left = jnp.concatenate([rows_for(k), rows_for(1 - k)], axis=0)

        def body(i, carry):
            span = pl.ds(pl.multiple_of(i * tile, tile), tile)
            if transposed:
                part = contract_last(left, w_v[span, :])
            else:
                part = jnp.dot(left, w_v[:, span], preferred_element_type=F32)
            own[m, lane_rows(lane), span] = part[:half].astype(BF16)
            theirs[m, lane_rows(lane), span] = part[half:].astype(BF16)
            return carry

        lax.fori_loop(0, cols // tile, body, 0)
        copy = pltpu.make_async_remote_copy(
            src_ref=theirs.at[m, lane_rows(lane)],
            dst_ref=from_core.at[m, lane_rows(lane)],
            send_sem=core_send.at[m, lane],
            recv_sem=core_recv.at[m, lane],
            device_id={"core": 1 - k},
            device_id_type=MESH,
        )
        copy.start()
        waits.append(copy)
        return copy

    def combine(m, lane, core_copy):
        core_copy.wait_recv()
        total = own[m, lane_rows(lane), :].astype(F32) + from_core[m, lane_rows(lane), :].astype(F32)
        last = sends.get((m, lane), len(orders[lane]))
        for step in range(last):
            slot = slots[lane, step, m]
            landed = from_chip.at[lane, slot]
            pltpu.make_async_remote_copy(
                src_ref=landed,
                dst_ref=landed,
                send_sem=chip_send.at[lane, slot],
                recv_sem=chip_recv.at[lane, slot],
                device_id={"core": 1 - k},
                device_id_type=MESH,
            ).wait_recv()
            total = total + from_chip[lane, slot].astype(F32)
        if m == 0:
            o_ref[lane_rows(lane), :] = total.astype(o_ref.dtype)
            return
        own[m, lane_rows(lane), :] = total.astype(BF16)
        bit = orders[lane][last]
        slot = slots[lane, last, m ^ bit]
        copy = pltpu.make_async_remote_copy(
            src_ref=own.at[m, lane_rows(lane)],
            dst_ref=from_chip.at[lane, slot],
            send_sem=chip_send.at[lane, slot],
            recv_sem=chip_recv.at[lane, slot],
            device_id={"ctx": c ^ bit},
            device_id_type=MESH,
        )
        copy.start()
        waits.append(copy)

    pending = []
    for m, lane in units:
        pending.append((m, lane, compute(m, lane)))
        if len(pending) > 1:
            combine(*pending.pop(0))
    while pending:
        combine(*pending.pop(0))
    for copy in waits:
        copy.wait_send()


def product_scatter(h, w, chips, ident, transposed):
    depth = h.shape[1]
    cols = w.shape[0] if transposed else w.shape[1]
    rows = h.shape[0] // (CORES * chips)
    half = rows // LANES
    return pl.pallas_call(
        functools.partial(product_scatter_kernel, chips, transposed, 512),
        name="product_scatter",
        out_shape=jax.ShapeDtypeStruct((rows, cols), F32),
        in_specs=[pl.BlockSpec(memory_space=pl.ANY)] * 2,
        out_specs=pl.BlockSpec(memory_space=pltpu.VMEM),
        scratch_shapes=[
            pltpu.VMEM(h.shape, BF16),
            pltpu.VMEM(w.shape, BF16),
            pltpu.VMEM((chips, rows, cols), BF16),
            pltpu.VMEM((chips, rows, cols), BF16),
            pltpu.VMEM((chips, rows, cols), BF16),
            pltpu.VMEM((LANES, chips - 1, half, cols), BF16),
            pltpu.SemaphoreType.DMA((2,)),
            pltpu.SemaphoreType.DMA((chips, LANES)),
            pltpu.SemaphoreType.DMA((chips, LANES)),
            pltpu.SemaphoreType.DMA((LANES, chips - 1)),
            pltpu.SemaphoreType.DMA((LANES, chips - 1)),
        ],
        cost_estimate=pl.CostEstimate(flops=45_000_000_000, bytes_accessed=0, transcendentals=0),
        compiler_params=pltpu.CompilerParams(
            collective_id=ident, has_side_effects=True, vmem_limit_bytes=VMEM_LIMIT
        ),
    )(h, w)


def attend_kernel(heads, size, step, p_ref, key_blk, query_blk, o_ref, log_ref):
    length = p_ref.shape[0]
    scale = 1.0 / math.sqrt(size)
    key_block = key_blk[0]
    for head in range(heads):
        keys = p_ref[:, (heads + head) * size : (heads + head + 1) * size]
        values = p_ref[:, (2 * heads + head) * size : (2 * heads + head + 1) * size]
        values_t = values.T
        for first in range(0, length, step):
            span = slice(first, first + step)
            queries = p_ref[span, head * size : (head + 1) * size]
            scores = contract_last(keys, queries) * scale
            scores = jnp.where(key_block <= query_blk[0, :, span], scores, -jnp.inf)
            top = jnp.max(scores, axis=0, keepdims=True)
            weights = jnp.exp(scores - top)
            total = jnp.sum(weights, axis=0, keepdims=True)
            prob = (weights * (1.0 / total)).astype(BF16)
            out_t = jnp.dot(values_t, prob, preferred_element_type=F32)
            o_ref[span, head * size : (head + 1) * size] = out_t.T.astype(BF16)
            log_ref[0, head : head + 1, span] = top + jnp.log(total)


def attend_back_kernel(heads, size, step, p_ref, g_ref, key_blk, query_blk, log_ref, d_ref, dk, dv):
    length = p_ref.shape[0]
    scale = 1.0 / math.sqrt(size)
    key_block = key_blk[0]
    for head in range(heads):
        keys = p_ref[:, (heads + head) * size : (heads + head + 1) * size]
        values = p_ref[:, (2 * heads + head) * size : (2 * heads + head + 1) * size]
        keys_t = keys.T
        for first in range(0, length, step):
            span = slice(first, first + step)
            queries = p_ref[span, head * size : (head + 1) * size]
            grads = g_ref[span, head * size : (head + 1) * size]
            scores = contract_last(keys, queries) * scale
            shifted = jnp.where(
                key_block <= query_blk[0, :, span], scores - log_ref[0, head : head + 1, span], -jnp.inf
            )
            prob = jnp.exp(shifted)
            grad_prob = contract_last(values, grads)
            row_dot = jnp.sum(prob * grad_prob, axis=0, keepdims=True)
            grad_raw = (prob * (grad_prob - row_dot) * scale).astype(BF16)
            dk_part = jnp.dot(grad_raw, queries, preferred_element_type=F32)
            dv_part = jnp.dot(prob.astype(BF16), grads, preferred_element_type=F32)
            if first == 0:
                dk[...] = dk_part
                dv[...] = dv_part
            else:
                dk[...] += dk_part
                dv[...] += dv_part
            dq_t = jnp.dot(keys_t, grad_raw, preferred_element_type=F32)
            d_ref[span, head * size : (head + 1) * size] = dq_t.T.astype(BF16)
        d_ref[:, (heads + head) * size : (heads + head + 1) * size] = dk[...].astype(BF16)
        d_ref[:, (2 * heads + head) * size : (2 * heads + head + 1) * size] = dv[...].astype(BF16)


def attention_specs(length, width, heads):
    wide = pl.BlockSpec((length, 3 * width), lambda s: (s, 0))
    narrow = pl.BlockSpec((length, width), lambda s: (s, 0))
    column = pl.BlockSpec((1, length, 1), lambda s: (s, 0, 0))
    row = pl.BlockSpec((1, 1, length), lambda s: (s, 0, 0))
    logs = pl.BlockSpec((1, heads, length), lambda s: (s, 0, 0))
    return wide, narrow, column, row, logs


def attend(proj, blocks, heads, size):
    length = blocks.shape[1]
    width = heads * size
    wide, narrow, column, row, logs = attention_specs(length, width, heads)
    return pl.pallas_call(
        functools.partial(attend_kernel, heads, size, 256),
        name="attend",
        grid=(blocks.shape[0],),
        out_shape=(
            jax.ShapeDtypeStruct((proj.shape[0], width), BF16),
            jax.ShapeDtypeStruct((blocks.shape[0], heads, length), F32),
        ),
        in_specs=[wide, column, row],
        out_specs=(narrow, logs),
        cost_estimate=pl.CostEstimate(flops=15_000_000_000, bytes_accessed=0, transcendentals=0),
        compiler_params=pltpu.CompilerParams(vmem_limit_bytes=VMEM_LIMIT),
    )(proj, blocks[:, :, None], blocks[:, None, :])


def attend_back(proj, grads, blocks, logsums, heads, size):
    length = blocks.shape[1]
    width = heads * size
    wide, narrow, column, row, logs = attention_specs(length, width, heads)
    return pl.pallas_call(
        functools.partial(attend_back_kernel, heads, size, 256),
        name="attend_back",
        grid=(blocks.shape[0],),
        out_shape=jax.ShapeDtypeStruct(proj.shape, BF16),
        in_specs=[wide, narrow, column, row, logs],
        out_specs=wide,
        scratch_shapes=[pltpu.VMEM((length, size), F32)] * 2,
        cost_estimate=pl.CostEstimate(flops=30_000_000_000, bytes_accessed=0, transcendentals=0),
        compiler_params=pltpu.CompilerParams(vmem_limit_bytes=VMEM_LIMIT),
    )(proj, grads, blocks[:, :, None], blocks[:, None, :], logsums)


def shards(
    tokens,
    block_ids,
    piece_order,
    norm1_gain,
    norm1_bias,
    w_qkv,
    w_out,
    norm2_gain,
    norm2_bias,
    w_up,
    w_down,
    grad_out,
):
    chips, depth = lax.axis_size("ctx"), lax.axis_size("z")
    c, k = lax.axis_index("ctx"), lax.axis_index("core")
    row_count, model_width = tokens.shape[1:]
    hidden_width = w_up.shape[1]
    size = model_width // HEADS
    team = CORES * chips
    heads = HEADS // team
    head_cols = heads * size
    ff_cols = hidden_width // team
    fsdp = ("z", "core")

    def chip_cols(w, width):
        return lax.dynamic_slice_in_dim(w, c * (CORES * width), CORES * width, 1)

    def own_slice(w, width):
        parts = w.reshape(w.shape[0], -1, CORES, width).transpose(2, 0, 1, 3)
        parts = parts.reshape(CORES, w.shape[0], -1)
        full = lax.all_gather(parts, fsdp, axis=0, tiled=False)
        mine = lax.dynamic_index_in_dim(full, k, 1, keepdims=False)
        return mine.reshape(model_width, -1)

    qkv_cols = jnp.concatenate(
        [chip_cols(part, head_cols) for part in jnp.split(w_qkv, 3, axis=1)], axis=1
    )
    my_qkv = own_slice(qkv_cols, head_cols)
    out_cols = model_width // chips
    out_gathered = lax.all_gather(
        lax.dynamic_slice_in_dim(w_out, c * out_cols, out_cols, 1), fsdp, axis=0, tiled=True
    )
    out_rows = lax.all_to_all(out_gathered, "ctx", split_axis=0, concat_axis=1, tiled=True)
    my_out = lax.dynamic_slice_in_dim(out_rows, k * head_cols, head_cols, 0)
    my_up = own_slice(chip_cols(w_up, ff_cols), ff_cols)
    my_down = own_slice(chip_cols(w_down, ff_cols), ff_cols)

    blocks = stored_blocks(block_ids, piece_order, row_count // 2)
    blocks = lax.all_gather(blocks, "core", axis=0, tiled=True)

    inputs = tokens.reshape(row_count, model_width).astype(F32)
    grad_y = grad_out.reshape(row_count, model_width)
    normed_one, unit_one, inv_one = normalize(inputs, norm1_gain, norm1_bias)
    acts_one = plane_gather(normed_one.astype(BF16), chips, 1)
    grads_y = plane_gather(grad_y, chips, 1)
    proj = jnp.dot(acts_one, my_qkv, preferred_element_type=F32).astype(BF16)
    attended, logsums = attend(proj, blocks, heads, size)
    residual = inputs + product_scatter(attended, my_out, chips, 2, False)
    normed_two, unit_two, inv_two = normalize(residual, norm2_gain, norm2_bias)
    acts_two = plane_gather(normed_two.astype(BF16), chips, 1)
    pre_act = jnp.dot(acts_two, my_up, preferred_element_type=F32)
    gelu_tanh = functools.partial(jax.nn.gelu, approximate=True)
    hidden_full, gelu_pull = jax.vjp(gelu_tanh, pre_act)
    hidden = hidden_full.astype(BF16)

    def spread_rows(grad):
        rounded = grad.astype(BF16).reshape(chips, -1, grad.shape[1])
        summed = lax.psum_scatter(rounded, "z", scatter_dimension=1, tiled=True)
        summed = summed.reshape(team, -1, grad.shape[1])
        return lax.all_to_all(summed, ("ctx", "core"), split_axis=0, concat_axis=0, tiled=True)

    def whole_columns(parts, width):
        count = parts.shape[1]
        return (
            parts.reshape(team, count, -1, width)
            .transpose(1, 2, 0, 3)
            .reshape(count, -1)
            .astype(F32)
        )

    grad_down = whole_columns(spread_rows(contract_first(grads_y, hidden)), ff_cols)
    grad_hidden = jnp.dot(grads_y, my_down, preferred_element_type=F32)
    grad_pre = gelu_pull(grad_hidden)[0].astype(BF16)
    grad_up = whole_columns(spread_rows(contract_first(acts_two, grad_pre)), ff_cols)
    grad_act_two = product_scatter(grad_pre, my_up, chips, 3, True)
    grad_res = grad_y.astype(F32) + normalize_back(grad_act_two, unit_two, inv_two, norm2_gain)
    grads_res = plane_gather(grad_res.astype(BF16), chips, 1)
    grad_attended = contract_last(grads_res, my_out).astype(BF16)
    grad_proj = attend_back(proj, grad_attended, blocks, logsums, heads, size)
    grad_qkv = whole_columns(spread_rows(contract_first(acts_one, grad_proj)), head_cols)
    out_part = lax.psum_scatter(
        contract_first(attended, grads_res).astype(BF16), "z", scatter_dimension=0, tiled=True
    )
    moves = [(z * CORES + core, core * depth + z) for z in range(depth) for core in range(CORES)]
    grad_wout = lax.ppermute(out_part, fsdp, moves).astype(F32)
    mixed = residual + product_scatter(hidden, my_down, chips, 3, True)
    grad_act_one = product_scatter(grad_proj, my_qkv, chips, 4, True)
    grad_inputs = grad_res + normalize_back(grad_act_one, unit_one, inv_one, norm1_gain)
    norm_sums = lax.psum(
        (
            jnp.sum(grad_act_one * unit_one, axis=0),
            jnp.sum(grad_act_one, axis=0),
            jnp.sum(grad_act_two * unit_two, axis=0),
            jnp.sum(grad_act_two, axis=0),
        ),
        ("ctx", "z", "core"),
    )
    out_shape = (1, row_count, model_width)
    return (
        mixed.reshape(out_shape).astype(BF16),
        grad_inputs.reshape(out_shape).astype(BF16),
        grad_qkv,
        grad_wout,
        grad_up,
        grad_down,
        *norm_sums,
    )


def solution(mesh):
    chips, across = mesh.shape["ctx"], mesh.shape["fsdp"]
    devices = np.asarray(mesh.devices).reshape(chips, across // CORES, CORES)
    cube = Mesh(devices, ("ctx", "z", "core"))
    fsdp = ("z", "core")
    rows = P(fsdp, "ctx", None)
    weight = P(fsdp, None)
    grad = P(("ctx", "z", "core"), None)
    return jax.shard_map(
        shards,
        mesh=cube,
        in_specs=(rows, weight, P(), P(), P(), weight, weight, P(), P(), weight, weight, rows),
        out_specs=(rows, rows, grad, grad, grad, grad, P(), P(), P(), P()),
        check_vma=False,
    )
```

time: 3860 us -> 806 us (0.21)
  waiting for transfers between devices: 3310 us -> 158 us
  Pallas kernels: 0 us -> 406 us
  matrix products: 306 us -> 95.8 us
  other arithmetic: 153 us -> 22.3 us
    unnamed x11 -> x8, waiting for transfers between devices: 1690 us -> 0.13 us
    all_gather x6 -> x4, waiting for transfers between devices: 914 us -> 18.4 us  [the longest x3 18.4 us: own_slice(): full = lax.all_gather(parts, fsdp, axis=0, tiled=False)]
    reduce_scatter x3 -> x4, waiting for transfers between devices: 706 us -> 134 us  [the longest x3 108 us: spread_rows(): summed = lax.psum_scatter(rounded, 'z', scatter_dimension=1, tiled=True)]
    pallas_call x0 -> x10, Pallas kernels: none -> 406 us  [the longest x4 189 us: product_scatter(): pl.pallas_call(functools.partial(product_scatter_kernel, chips, transpose...]
    concatenate x2 -> x1, other arithmetic: 134 us -> 0.05 us  [shards(): jnp.concatenate([chip_cols(part, head_cols) for part in jnp.split(w_qkv,...]
    dot_general x10 -> x3, matrix products: 161 us -> 42.4 us  [the longest x1 19.3 us: shards(): grad_hidden = jnp.dot(grads_y, my_down, preferred_element_type=F32)]
    dot_general x4 -> x1, matrix products: 59.2 us -> 6.74 us  [contract_last(): lax.dot_general(left_arr, right_arr, (((1,), (1,)), ((), ())), preferred_...]
    dot_general x4, matrix products: 85.8 us -> 46.6 us  [contract_first(): lax.dot_general(left_arr, right_arr, (((0,), (0,)), ((), ())), preferred_...]
  transfers between devices with their start and end apart: 10 -> 13, of which waited for: 8 -> 6; matrix products, arithmetic and copies ran while one was open for 11% -> 11% of each run, Pallas kernels for 0% -> 32%
where the time goes in v1:
time: 806 us; the launch traced here: 801 us
  Pallas kernels  406 us (50%)
  waiting for transfers between devices  158 us (20%)
  matrix products  95.8 us (12%)
  blocking collectives  43.3 us (5%)
  local copies, waits for them, and re-layouts  42.3 us (5%)
  other arithmetic  22.3 us (3%)
  starting transfers between devices  17.9 us (2%)
  between operations  15 us (2%)
    pallas_call x4, Pallas kernels, product_scatter(): pl.pallas_call(functools.partial(product_scatter_kernel, chips, transpose...  189 us
    pallas_call x4, Pallas kernels, plane_gather(): pl.pallas_call(functools.partial(gather_kernel, chips, pieces), name='pla...  185 us
    reduce_scatter x3, waiting for transfers between devices, spread_rows(): summed = lax.psum_scatter(rounded, 'z', scatter_dimension=1, tiled=True)  108 us
    dot_general x4, matrix products, contract_first(): lax.dot_general(left_arr, right_arr, (((0,), (0,)), ((), ())), preferred_...  46.6 us
    psum x1, blocking collectives, shards(): lax.psum((jnp.sum(grad_act_one * unit_one, axis=0), jnp.sum(grad_act_one,...  41.2 us
    reduce_scatter x1, waiting for transfers between devices, shards(): lax.psum_scatter(contract_first(attended, grads_res).astype(BF16), 'z', s...  26.2 us
    dot_general x1, matrix products, shards(): grad_hidden = jnp.dot(grads_y, my_down, preferred_element_type=F32)  19.3 us
    all_gather x3, waiting for transfers between devices, own_slice(): full = lax.all_gather(parts, fsdp, axis=0, tiled=False)  18.4 us
  transfers between devices with their start and end apart: 13, of which 6 were waited for; matrix products, arithmetic and copies ran while one was open for 11% of the time, Pallas kernels for 32%

profile of v1, /device:TPU:0, one launch (start us, length us, event | category | flops | bytes accessed | tf_op | source)
XLA Modules:
  0.0 801.3 jit_solution(4672395830952422240)
XLA Ops:
  22.6 42.0 %plane_gather.4 = bf16[2048,2048]{1,0:T(8,128)(2,1)} custom-call(bf16[256,2048]{1,0:T(8,128)(2,1)} %fusion.19.x_ref), custom_call_target="tpu_custom_call" | custom-call | flops 40000000000 | tf_op jit(solution)/shard_map/plane_gather/pallas_call | solution.py:143
  64.7 3.6 all-to-all-start
  68.4 62.5 %plane_gather.6 = bf16[2048,2048]{1,0:T(8,128)(2,1)} custom-call(bf16[256,2048]{1,0:T(8,128)(2,1)} %bitcast.170), custom_call_target="tpu_custom_call" | custom-call | flops 40000000000 | tf_op jit(solution)/shard_map/plane_gather/pallas_call | solution.py:143
  140.2 10.3 %convolution_convert_fusion.1.p_ref = bf16[2048,768]{1,0:T(8,128)(2,1)} fusion(bf16[2048,2048]{1,0:T(8,128)(2,1)} %plane_gather.4, bf16[2048,768]{1,0:T(8,128)(2,1)S(1)} %bitcast.159), kind=kOutput, calls=%fused_computation.18 | convolution fusion | flops 6444023808 | bytes 14680064 | tf_op jit(solution)/shard_map/dot_general | solution.py:461
  150.5 16.2 %attend.1 = (bf16[2048,256]{1,0:T(8,128)(2,1)}, f32[2,2,1024]{2,1,0:T(2,128)}) custom-call(bf16[2048,768]{1,0:T(8,128)(2,1)} %convolution_convert_fusion.1.p_ref, s32[2,1024,1]{2,1,0:T(8,128)} %broadcast_in_dim.42.key_blk, s32[2,1,1024]{2,1,0:T(1,128)} %copy-done.24), custom_call_target="tpu_custom_call" | custom-call | flops 15000000512 | tf_op jit(solution)/shard_map/attend/pallas_call | solution.py:373
  166.7 43.3 %product_scatter.4 = f32[256,2048]{1,0:T(8,128)} custom-call(bf16[2048,256]{1,0:T(8,128)(2,1)} %get-tuple-element.12.h_ref, bf16[256,2048]{1,0:T(8,128)(2,1)} %constant_dynamic-slice_fusion.4.w_ref), custom_call_target="tpu_custom_call" | custom-call | flops 44999999488 | tf_op jit(solution)/shard_map/product_scatter/pallas_call | solution.py:278
  214.8 40.1 %plane_gather.5 = bf16[2048,2048]{1,0:T(8,128)(2,1)} custom-call(bf16[256,2048]{1,0:T(8,128)(2,1)} %add_convert_fusion.1.x_ref), custom_call_target="tpu_custom_call" | custom-call | flops 40000000000 | tf_op jit(solution)/shard_map/plane_gather/pallas_call | solution.py:143
  255.0 18.3 %all-gather.14.cloned.1.call-done = bf16[16,256,1,1024]{3,1,2,0:T(8,128)(2,1)} async-done(((bf16[2,256,1,1024]{3,1,2,0:T(8,128)(2,1)}), bf16[16,256,1,1024]{3,1,2,0:T(8,128)(2,1)}) %all-gather.14.cloned.1.call-update) | async-done | bytes 8388624 | tf_op jit(solution)/shard_map/all_gather | solution.py:436
  273.3 6.9 constant_dynamic-slice_fusion
  280.2 12.9 %multiply_convert_fusion = (bf16[2048,1024]{1,0:T(8,128)(2,1)}, f32[2048,1024]{1,0:T(8,128)}) fusion(bf16[2048,2048]{1,0:T(8,128)(2,1)S(1)} %copy-done.36, bf16[2048,1024]{1,0:T(8,128)(2,1)S(1)} %bitcast.152), kind=kOutput, calls=%fused_computation.15 | convolution fusion | flops 8608808960 | bytes 25165824 | tf_op jit(solution)/shard_map/dot_general | solution.py:466
  293.1 48.1 %product_scatter.5 = f32[256,2048]{1,0:T(8,128)} custom-call(bf16[2048,1024]{1,0:T(8,128)(2,1)} %get-tuple-element.34.h_ref, bf16[2048,1024]{1,0:T(8,128)(2,1)} %bitcast.154), custom_call_target="tpu_custom_call" | custom-call | flops 44999999488 | tf_op jit(solution)/shard_map/product_scatter/pallas_call | solution.py:278
  341.3 19.3 %fusion.6.h_ref = bf16[2048,1024]{1,0:T(8,128)(2,1)} fusion(f32[2048,1024]{1,0:T(8,128)} %get-tuple-element.35, bf16[2048,2048]{1,0:T(8,128)(2,1)} %plane_gather.6, bf16[2048,1024]{1,0:T(8,128)(2,1)S(1)} %bitcast.155), kind=kOutput, calls=%fused_computation.9 | convolution fusion | flops 8631877632 | bytes 25165824 | tf_op jit(solution)/shard_map/dot_general | solution.py:487
  360.6 46.8 %product_scatter.6 = f32[256,2048]{1,0:T(8,128)} custom-call(bf16[2048,1024]{1,0:T(8,128)(2,1)} %fusion.6.h_ref, bf16[2048,1024]{1,0:T(8,128)(2,1)} %bitcast.153), custom_call_target="tpu_custom_call" | custom-call | flops 44999999488 | tf_op jit(solution)/shard_map/product_scatter/pallas_call | solution.py:278
  413.9 40.0 %plane_gather.7 = bf16[2048,2048]{1,0:T(8,128)(2,1)} custom-call(bf16[256,2048]{1,0:T(8,128)(2,1)} %get-tuple-element.26.x_ref), custom_call_target="tpu_custom_call" | custom-call | flops 40000000000 | tf_op jit(solution)/shard_map/plane_gather/pallas_call | solution.py:143
  454.0 6.7 convolution_convert_fusion.4.g_ref
  460.7 16.9 %attend_back.1.h_ref = bf16[2048,768]{1,0:T(8,128)(2,1)} custom-call(bf16[2048,768]{1,0:T(8,128)(2,1)} %convolution_convert_fusion.1.p_ref, bf16[2048,256]{1,0:T(8,128)(2,1)} %convolution_convert_fusion.4.g_ref, s32[2,1024,1]{2,1,0:T(8,128)} %broadcast_in_dim.42.key_blk, s32[2,1,1024]{2,1,0:T(1,128)} %copy-done.24, f32[2,2,1024]{2,1,0:T(2,128)} %get-tuple-element.13.log_ref), custom_call_target="tpu_custom_call" | custom-call | flops 30000001024 | tf_op jit(solution)/shard_map/attend_back/pallas_call | solution.py:392
  477.6 11.4 %convolution_convert_fusion.2 = bf16[2048,768]{1,0:T(8,128)(2,1)} fusion(bf16[2048,2048]{1,0:T(8,128)(2,1)} %plane_gather.4, bf16[2048,768]{1,0:T(8,128)(2,1)} %attend_back.1.h_ref), kind=kOutput, calls=%fused_computation.19 | convolution fusion | flops 6444023808 | bytes 14680064 | tf_op jit(solution)/shard_map/dot_general | solution.py:49
  489.1 14.6 %convert_bitcast_fusion = bf16[2048,1024]{0,1:T(8,128)(2,1)} fusion(bf16[2048,1024]{1,0:T(8,128)(2,1)} %get-tuple-element.34.h_ref, bf16[2048,2048]{1,0:T(8,128)(2,1)} %plane_gather.6), kind=kOutput, calls=%fused_computation.16 | convolution fusion | flops 8592031744 | bytes 16777216 | tf_op jit(solution)/shard_map/dot_general | solution.py:49
  503.7 6.5 copy.85
  510.2 14.0 %convolution_convert_fusion = bf16[2048,1024]{1,0:T(8,128)(2,1)} fusion(bf16[2048,2048]{1,0:T(8,128)(2,1)} %plane_gather.5, bf16[2048,1024]{1,0:T(8,128)(2,1)} %fusion.6.h_ref), kind=kOutput, calls=%fused_computation.17 | convolution fusion | flops 8592031744 | bytes 16777216 | tf_op jit(solution)/shard_map/dot_general | solution.py:49
  524.2 22.9 %reduce-scatter.5.cloned.1.call-done = bf16[4,128,768]{2,1,0:T(8,128)(2,1)} async-done(((bf16[4,512,768]{2,1,0:T(8,128)(2,1)}), bf16[4,128,768]{2,1,0:T(8,128)(2,1)}) %reduce-scatter.5.cloned.1.call-update) | async-done | bytes 786448 | tf_op jit(solution)/shard_map/reduce_scatter | solution.py:473
  547.1 3.7 all-to-all-start.1
  550.8 6.7 convolution_convert_fusion.3
  557.6 5.8 all-to-all-done.1
  563.4 62.7 %reduce-scatter.11.cloned.1.call-done = bf16[4,128,1024]{2,1,0:T(8,128)(2,1)} async-done(((bf16[4,512,1024]{2,1,0:T(8,128)(2,1)}), bf16[4,128,1024]{2,1,0:T(8,128)(2,1)}) %reduce-scatter.11.cloned.1.call-update) | async-done | bytes 1048592 | tf_op jit(solution)/shard_map/reduce_scatter | solution.py:473
  626.1 4.4 all-to-all-start.3
  630.5 50.2 %product_scatter.7 = f32[256,2048]{1,0:T(8,128)} custom-call(bf16[2048,768]{1,0:T(8,128)(2,1)} %attend_back.1.h_ref, bf16[2048,768]{1,0:T(8,128)(2,1)} %bitcast.160), custom_call_target="tpu_custom_call" | custom-call | flops 44999999488 | tf_op jit(solution)/shard_map/product_scatter/pallas_call | solution.py:278
  683.5 22.2 %reduce-scatter.9.cloned.1.call-done = bf16[4,128,1024]{2,1,0:T(8,128)(2,1)} async-done(((bf16[4,512,1024]{2,1,0:T(8,128)(2,1)}), bf16[4,128,1024]{2,1,0:T(8,128)(2,1)}) %reduce-scatter.9.cloned.1.call-update) | async-done | bytes 1048592 | tf_op jit(solution)/shard_map/reduce_scatter | solution.py:473
  705.8 4.2 all-to-all-start.2
  710.0 26.2 %reduce-scatter.7.cloned.1.call-done = bf16[64,2048]{1,0:T(8,128)(2,1)} async-done(((bf16[256,2048]{1,0:T(8,128)(2,1)}), bf16[64,2048]{1,0:T(8,128)(2,1)}) %reduce-scatter.7.cloned.1.call-update) | async-done | bytes 262160 | tf_op jit(solution)/shard_map/reduce_scatter | solution.py:496
  737.9 3.4 fusion.28
  741.3 41.2 %all-reduce = (f32[2048]{0:T(1024)}, f32[2048]{0:T(1024)}, f32[2048]{0:T(1024)}, f32[2048]{0:T(1024)}) all-reduce(f32[2048]{0:T(1024)S(1)} %get-tuple-element.16, f32[2048]{0:T(1024)S(1)} %get-tuple-element.21, f32[2048]{0:T(1024)S(1)} %copy-done.22, f32[2048]{0:T(1024)S(1)} %copy-done.23), channel_id=1, replica_groups=mesh['ctx'=4,'z'=4,'core'=2] {'ctx','z','core'}, use_global_device_ids=true, to_apply=%region_13.14 | all-reduce | flops 8192 | bytes 65536 | tf_op jit(solution)/shard_map/psum | solution.py:504
  (151 shorter events, 52.0 us)
Async XLA Ops:
  7.2 57.5 %all-gather.10.cloned.1.call-start = ((), (), s32[]{:S(2)}) async-start(), calls=%async_computation.9 | async-start | bytes 2359296 | tf_op jit(solution)/shard_map/all_gather | solution.py:445
  9.2 127.3 %all-gather.8.cloned.1.call-start = ((), (), s32[]{:S(2)}) async-start(), calls=%async_computation.8 | async-start | bytes 7077888 | tf_op jit(solution)/shard_map/all_gather | solution.py:436
  13.3 241.7 %all-gather.12.cloned.1.call-start = ((), (), s32[]{:S(2)}) async-start(), calls=%async_computation.14 | async-start | bytes 9437184 | tf_op jit(solution)/shard_map/all_gather | solution.py:436
  16.5 256.8 %all-gather.14.cloned.1.call-start = ((), (), s32[]{:S(2)}) async-start(), calls=%async_computation.15 | async-start | bytes 9437184 | tf_op jit(solution)/shard_map/all_gather | solution.py:436
  64.7 70.4 %all-to-all-start = ((bf16[4,512,512]{2,1,0:T(8,128)(2,1)}), bf16[4,512,512]{2,1,0:T(8,128)(2,1)S(1)}, u32[]{:S(2)}, u32[]{:S(2)}) async-start(bf16[4,512,512]{2,1,0:T(8,128)(2,1)} %bitcast.166), calls=%async_computation | async-start | bytes 4194304 | tf_op jit(solution)/shard_map/all_to_all | solution.py:448
  68.3 478.8 %reduce-scatter.5.cloned.1.call-start = ((), (), s32[]{:S(2)}) async-start(), calls=%async_computation.10 | async-start | bytes 3932160 | tf_op jit(solution)/shard_map/reduce_scatter | solution.py:473
  68.4 62.6 %copy-start.35 = (s32[8]{0:T(128)S(1)}, s32[8]{0:T(128)}, u32[]{:S(2)}) copy-start(s32[8]{0:T(128)} %param.14) | copy-start | bytes 100
  68.4 62.6 %copy-start.17 = (s32[1,1024]{1,0:T(1,128)S(1)}, s32[1,1024]{1,0:T(1,128)}, u32[]{:S(2)}) copy-start(s32[1,1024]{1,0:T(1,128)} %param.13) | copy-start | bytes 12292
  166.7 43.3 %copy-start.5 = (bf16[1,256,2048]{2,1,0:T(8,128)(2,1)S(1)}, bf16[1,256,2048]{2,1,0:T(8,128)(2,1)}, u32[]{:S(2)}) copy-start(bf16[1,256,2048]{2,1,0:T(8,128)(2,1)} %param.12) | copy-start | bytes 3145732
  212.1 42.8 %copy-start.25 = (f32[256]{0:T(256)}, f32[256]{0:T(256)S(1)}, u32[]{:S(2)}) copy-start(f32[256]{0:T(256)S(1)} %broadcast_multiply_fusion.4) | copy-start | bytes 3076
  213.4 41.6 %copy-start.29 = (f32[256]{0:T(256)}, f32[256]{0:T(256)S(1)}, u32[]{:S(2)}) copy-start(f32[256]{0:T(256)S(1)} %add_rsqrt_fusion) | copy-start | bytes 3076
  293.1 48.2 %copy-start.10 = (bf16[8,1,256,1024]{3,2,1,0:T(8,128)(2,1)S(1)}, bf16[8,1,256,1024]{3,2,1,0:T(8,128)(2,1)}, u32[]{:S(2)}) copy-start(bf16[8,1,256,1024]{3,2,1,0:T(8,128)(2,1)} %get-tuple-element.38) | copy-start | bytes 12582916
  360.5 46.9 %copy-start.3 = (f32[256,2048]{1,0:T(8,128)S(1)}, f32[256,2048]{1,0:T(8,128)}, u32[]{:S(2)}) copy-start(f32[256,2048]{1,0:T(8,128)} %copy-done.2) | copy-start | bytes 6291460
  360.5 46.9 %copy-start.19 = (f32[2048]{0:T(1024)S(1)}, f32[2048]{0:T(1024)}, u32[]{:S(2)}) copy-start(f32[2048]{0:T(1024)} %param.19) | copy-start | bytes 24580
  360.5 46.9 %copy-start.26 = (f32[256]{0:T(256)S(1)}, f32[256]{0:T(256)}, u32[]{:S(2)}) copy-start(f32[256]{0:T(256)} %copy-done.25) | copy-start | bytes 3076
  360.5 46.9 %copy-start.30 = (f32[256]{0:T(256)S(1)}, f32[256]{0:T(256)}, u32[]{:S(2)}) copy-start(f32[256]{0:T(256)} %copy-done.29) | copy-start | bytes 3076
  360.5 50.2 %copy-start.15 = (bf16[1,256,2048]{2,1,0:T(8,128)(2,1)S(1)}, bf16[1,256,2048]{2,1,0:T(8,128)(2,1)}, u32[]{:S(2)}) copy-start(bf16[1,256,2048]{2,1,0:T(8,128)(2,1)} %param.23) | copy-start | bytes 3145732
  413.9 40.0 %copy-start.16 = (bf16[256,2048]{1,0:T(8,128)(2,1)S(1)}, bf16[256,2048]{1,0:T(8,128)(2,1)}, u32[]{:S(2)}) copy-start(bf16[256,2048]{1,0:T(8,128)(2,1)} %constant_dynamic-slice_fusion.4.w_ref) | copy-start | bytes 3145732
  489.0 137.0 %reduce-scatter.11.cloned.1.call-start = ((), (), s32[]{:S(2)}) async-start(), calls=%async_computation.13 | async-start | bytes 5242880 | tf_op jit(solution)/shard_map/reduce_scatter | solution.py:473
  510.2 195.6 %reduce-scatter.9.cloned.1.call-start = ((), (), s32[]{:S(2)}) async-start(), calls=%async_computation.12 | async-start | bytes 5242880 | tf_op jit(solution)/shard_map/reduce_scatter | solution.py:473
  524.2 26.6 %copy-start.13 = (bf16[2048,256]{1,0:T(8,128)(2,1)S(1)}, bf16[2048,256]{1,0:T(8,128)(2,1)}, u32[]{:S(2)}) copy-start(bf16[2048,256]{1,0:T(8,128)(2,1)} %get-tuple-element.12.h_ref) | copy-start | bytes 3145732
  547.1 16.3 %all-to-all-start.1 = ((bf16[8,64,768]{2,1,0:T(8,128)(2,1)}), bf16[8,64,768]{2,1,0:T(8,128)(2,1)S(1)}, u32[]{:S(2)}, u32[]{:S(2)}) async-start(bf16[8,64,768]{2,1,0:T(8,128)(2,1)} %bitcast.173), calls=%async_computation.2 | async-start | bytes 1572864 | tf_op jit(solution)/shard_map/all_to_all | solution.py:475
  550.8 185.5 %reduce-scatter.7.cloned.1.call-start = ((), (), s32[]{:S(2)}) async-start(), calls=%async_computation.11 | async-start | bytes 1310720 | tf_op jit(solution)/shard_map/reduce_scatter | solution.py:496
  563.4 62.7 %copy-start.12 = (bf16[8,64,768]{2,1,0:T(8,128)(2,1)}, bf16[8,64,768]{2,1,0:T(8,128)(2,1)S(1)}, u32[]{:S(2)}) copy-start(bf16[8,64,768]{2,1,0:T(8,128)(2,1)S(1)} %all-to-all-done.1) | copy-start | bytes 2359300
  626.1 79.7 %all-to-all-start.3 = ((bf16[8,64,1024]{2,1,0:T(8,128)(2,1)}), bf16[8,64,1024]{2,1,0:T(8,128)(2,1)}, u32[]{:S(2)}, u32[]{:S(2)}) async-start(bf16[8,64,1024]{2,1,0:T(8,128)(2,1)} %bitcast.172), calls=%async_computation.7 | async-start | bytes 2097152 | tf_op jit(solution)/shard_map/all_to_all | solution.py:475
  630.5 50.3 %copy-start.6 = (bf16[1,256,2048]{2,1,0:T(8,128)(2,1)S(1)}, bf16[1,256,2048]{2,1,0:T(8,128)(2,1)}, u32[]{:S(2)}) copy-start(bf16[1,256,2048]{2,1,0:T(8,128)(2,1)} %param.12) | copy-start | bytes 3145732
  630.5 50.3 %copy-start.21 = (f32[2048]{0:T(1024)S(1)}, f32[2048]{0:T(1024)}, u32[]{:S(2)}) copy-start(f32[2048]{0:T(1024)} %param.15) | copy-start | bytes 24580
  630.5 50.3 %copy-start.28 = (f32[256]{0:T(256)S(1)}, f32[256]{0:T(256)}, u32[]{:S(2)}) copy-start(f32[256]{0:T(256)} %copy-done.27) | copy-start | bytes 3076
  630.5 50.3 %copy-start.32 = (f32[256]{0:T(256)S(1)}, f32[256]{0:T(256)}, u32[]{:S(2)}) copy-start(f32[256]{0:T(256)} %copy-done.31) | copy-start | bytes 3076
  680.8 57.1 %copy-start.7 = (f32[256,2048]{1,0:T(8,128)S(1)}, f32[256,2048]{1,0:T(8,128)}, u32[]{:S(2)}) copy-start(f32[256,2048]{1,0:T(8,128)} %product_scatter.7) | copy-start | bytes 6291460
  705.8 85.6 %all-to-all-start.2 = ((bf16[8,64,1024]{2,1,0:T(8,128)(2,1)}), bf16[8,64,1024]{2,1,0:T(8,128)(2,1)}, u32[]{:S(2)}, u32[]{:S(2)}) async-start(bf16[8,64,1024]{2,1,0:T(8,128)(2,1)} %bitcast.171), calls=%async_computation.5 | async-start | bytes 2097152 | tf_op jit(solution)/shard_map/all_to_all | solution.py:475
  736.3 46.2 %collective-permute-start = (bf16[64,2048]{1,0:T(8,128)(2,1)}, bf16[64,2048]{1,0:T(8,128)(2,1)S(1)}, u32[]{:S(2)}, u32[]{:S(2)}) collective-permute-start(bf16[64,2048]{1,0:T(8,128)(2,1)} %reduce-scatter.7.cloned.1.call-done), channel_id=1, source_target_pairs={{0,0},{1,4},{2,1},{3,5},{4,2},{5,6},{6,3},{7,7},{8,8},{9,12},{10,9... | collective-permute-start | bytes 786440 | tf_op jit(solution)/shard_map/ppermute | solution.py:500
  (18 other events, 59.6 us)
Sparse Core Ops, SparseCore 0:
  10.2 31.7 all-gather.9
  44.2 64.2 all-gather.7
  110.1 80.6 all-gather.11
  192.3 80.9 all-gather.13
  489.2 57.8 reduce-scatter.4
  549.3 76.7 reduce-scatter.10
  628.4 77.2 reduce-scatter.8
  708.6 27.6 reduce-scatter.6

commit v2 on v1

--- a/solution.py
+++ b/solution.py
@@ -60,13 +60,13 @@
     return [bits[lane:] + bits[:lane] for lane in range(LANES)]
 
 
-def greet(chips, me_chip, me_core):
+def greet(chips, me_chip, me_core, others=()):
     barrier = pltpu.get_barrier_semaphore()
-    bits = chip_bits(chips)
-    for bit in bits:
-        pl.semaphore_signal(barrier, inc=1, device_id={"ctx": me_chip ^ bit}, device_id_type=MESH)
-    pl.semaphore_signal(barrier, inc=1, device_id={"core": 1 - me_core}, device_id_type=MESH)
-    pl.semaphore_wait(barrier, len(bits) + 1)
+    friends = [{"ctx": me_chip ^ bit} for bit in chip_bits(chips)] + [{"core": 1 - me_core}]
+    friends += others
+    for friend in friends:
+        pl.semaphore_signal(barrier, inc=1, device_id=friend, device_id_type=MESH)
+    pl.semaphore_wait(barrier, len(friends))
 
 
 def gather_kernel(chips, pieces, x_ref, o_ref, own_sem, send_sem, recv_sem):
@@ -151,9 +151,53 @@
             pltpu.SemaphoreType.DMA((bits + 1, chips, LANES, pieces)),
             pltpu.SemaphoreType.DMA((2, chips, LANES, pieces)),
         ],
-        cost_estimate=pl.CostEstimate(flops=40_000_000_000, bytes_accessed=0, transcendentals=0),
+        cost_estimate=pl.CostEstimate(flops=1_000_000_000, bytes_accessed=0, transcendentals=0),
         compiler_params=pltpu.CompilerParams(collective_id=ident, has_side_effects=True),
     )(x)
+
+
+def pick_kernel(head_cols, ff_cols, q_ref, o_ref, u_ref, d_ref, attn_ref, up_ref, down_ref, sem):
+    c = lax.axis_index("ctx")
+    width = o_ref.shape[1]
+    copies = []
+
+    def move(source, first, target, landing, count):
+        first = pl.multiple_of(first, 128)
+        copy = pltpu.make_async_copy(
+            source.at[:, pl.ds(first, count)],
+            target.at[:, pl.ds(landing, count)],
+            sem.at[len(copies)],
+        )
+        copy.start()
+        copies.append(copy)
+
+    for core in range(CORES):
+        first = (c * CORES + core) * head_cols
+        for part in range(3):
+            landing = (core * 4 + part) * head_cols
+            move(q_ref, part * width + first, attn_ref, landing, head_cols)
+        move(o_ref, first, attn_ref, (core * 4 + 3) * head_cols, head_cols)
+    for source, target in ((u_ref, up_ref), (d_ref, down_ref)):
+        move(source, c * (CORES * ff_cols), target, 0, CORES * ff_cols)
+    for copy in copies:
+        copy.wait()
+
+
+def pick_columns(w_qkv, w_out, w_up, w_down, head_cols, ff_cols):
+    rows = w_qkv.shape[0]
+    in_place = pl.BlockSpec(memory_space=pl.ANY)
+    in_vmem = pl.BlockSpec(memory_space=pltpu.VMEM)
+    return pl.pallas_call(
+        functools.partial(pick_kernel, head_cols, ff_cols),
+        name="pick_columns",
+        out_shape=[
+            jax.ShapeDtypeStruct((rows, CORES * count), BF16)
+            for count in (4 * head_cols, ff_cols, ff_cols)
+        ],
+        in_specs=[in_place] * 4,
+        out_specs=[in_vmem] * 3,
+        scratch_shapes=[pltpu.SemaphoreType.DMA((4 * CORES + 2,))],
+    )(w_qkv, w_out, w_up, w_down)
 
 
 def scatter_plan(chips):
@@ -176,47 +220,32 @@
     return orders, slots, sends, units
 
 
-def product_scatter_kernel(
-    chips, transposed, tile, h_ref, w_ref, o_ref, h_v, w_v, own, theirs, from_core, from_chip,
-    load_sem, core_send, core_recv, chip_send, chip_recv,
-):
+def exchange_scratch(chips, rows, cols):
+    half = rows // LANES
+    return [
+        pltpu.VMEM((chips, rows, cols), BF16),
+        pltpu.VMEM((chips, rows, cols), BF16),
+        pltpu.VMEM((chips, rows, cols), BF16),
+        pltpu.VMEM((LANES, chips - 1, half, cols), BF16),
+        pltpu.SemaphoreType.DMA((chips, LANES)),
+        pltpu.SemaphoreType.DMA((chips, LANES)),
+        pltpu.SemaphoreType.DMA((LANES, chips - 1)),
+        pltpu.SemaphoreType.DMA((LANES, chips - 1)),
+    ]
+
+
+def exchange(chips, scratch, o_ref, compute, fillers=()):
+    own, theirs, from_core, from_chip, core_send, core_recv, chip_send, chip_recv = scratch
     c, k = lax.axis_index("ctx"), lax.axis_index("core")
-    rows, cols = o_ref.shape
-    half = rows // LANES
+    half = o_ref.shape[0] // LANES
     orders, slots, sends, units = scatter_plan(chips)
-    w_load = pltpu.make_async_copy(w_ref, w_v, load_sem.at[0])
-    h_load = pltpu.make_async_copy(h_ref, h_v, load_sem.at[1])
-    w_load.start()
-    h_load.start()
-    greet(chips, c, k)
-    w_load.wait()
-    h_load.wait()
     waits = []
 
-    def lane_rows(lane):
-        return pl.ds(lane * half, half)
-
-    def compute(m, lane):
-        def rows_for(core):
-            start = (core * chips + (c ^ m)) * rows + lane * half
-            return h_v[pl.ds(pl.multiple_of(start, half), half), :]
-
-        left = jnp.concatenate([rows_for(k), rows_for(1 - k)], axis=0)
-
-        def body(i, carry):
-            span = pl.ds(pl.multiple_of(i * tile, tile), tile)
-            if transposed:
-                part = contract_last(left, w_v[span, :])
-            else:
-                part = jnp.dot(left, w_v[:, span], preferred_element_type=F32)
-            own[m, lane_rows(lane), span] = part[:half].astype(BF16)
-            theirs[m, lane_rows(lane), span] = part[half:].astype(BF16)
-            return carry
-
-        lax.fori_loop(0, cols // tile, body, 0)
+    def share(m, lane):
+        rows = pl.ds(lane * half, half)
         copy = pltpu.make_async_remote_copy(
-            src_ref=theirs.at[m, lane_rows(lane)],
-            dst_ref=from_core.at[m, lane_rows(lane)],
+            src_ref=theirs.at[m, rows],
+            dst_ref=from_core.at[m, rows],
             send_sem=core_send.at[m, lane],
             recv_sem=core_recv.at[m, lane],
             device_id={"core": 1 - k},
@@ -227,8 +256,9 @@
         return copy
 
     def combine(m, lane, core_copy):
+        rows = pl.ds(lane * half, half)
         core_copy.wait_recv()
-        total = own[m, lane_rows(lane), :].astype(F32) + from_core[m, lane_rows(lane), :].astype(F32)
+        total = own[m, rows, :].astype(F32) + from_core[m, rows, :].astype(F32)
         last = sends.get((m, lane), len(orders[lane]))
         for step in range(last):
             slot = slots[lane, step, m]
@@ -243,13 +273,13 @@
             ).wait_recv()
             total = total + from_chip[lane, slot].astype(F32)
         if m == 0:
-            o_ref[lane_rows(lane), :] = total.astype(o_ref.dtype)
+            o_ref[rows, :] = total.astype(o_ref.dtype)
             return
-        own[m, lane_rows(lane), :] = total.astype(BF16)
+        own[m, rows, :] = total.astype(BF16)
         bit = orders[lane][last]
         slot = slots[lane, last, m ^ bit]
         copy = pltpu.make_async_remote_copy(
-            src_ref=own.at[m, lane_rows(lane)],
+            src_ref=own.at[m, rows],
             dst_ref=from_chip.at[lane, slot],
             send_sem=chip_send.at[lane, slot],
             recv_sem=chip_recv.at[lane, slot],
@@ -259,46 +289,266 @@
         copy.start()
         waits.append(copy)
 
+    fillers = list(fillers)
     pending = []
     for m, lane in units:
-        pending.append((m, lane, compute(m, lane)))
-        if len(pending) > 1:
+        compute(m, lane)
+        pending.append((m, lane, share(m, lane)))
+        if len(pending) > 1 and sends.get(pending[0][:2]) == 0:
             combine(*pending.pop(0))
-    while pending:
-        combine(*pending.pop(0))
+    for level in range(1, len(orders[0]) + 1):
+        count = -(-len(fillers) // (len(orders[0]) + 1 - level))
+        for filler in fillers[:count]:
+            filler()
+        fillers = fillers[count:]
+        while pending and sends.get(pending[0][:2], len(orders[0])) <= level:
+            combine(*pending.pop(0))
     for copy in waits:
         copy.wait_send()
 
 
-def product_scatter(h, w, chips, ident, transposed):
+def unit_rows(chips, rows, m, lane):
+    c, k = lax.axis_index("ctx"), lax.axis_index("core")
+    half = rows // LANES
+    starts = [(core * chips + (c ^ m)) * rows + lane * half for core in (k, 1 - k)]
+    return [pl.ds(pl.multiple_of(start, half), half) for start in starts]
+
+
+def product_terms(left, w_v, own, theirs, m, lane, transposed, tile):
+    half, cols = left.shape[0] // CORES, own.shape[2]
+    rows = pl.ds(lane * half, half)
+
+    def body(i, carry):
+        span = pl.ds(pl.multiple_of(i * tile, tile), tile)
+        if transposed:
+            part = contract_last(left, w_v[span, :])
+        else:
+            part = jnp.dot(left, w_v[:, span], preferred_element_type=F32)
+        own[m, rows, span] = part[:half].astype(BF16)
+        theirs[m, rows, span] = part[half:].astype(BF16)
+        return carry
+
+    lax.fori_loop(0, cols // tile, body, 0)
+
+
+def core_window(ref, width):
+    stride = ref.shape[1] // CORES
+    first = pl.multiple_of(lax.axis_index("core") * stride, 128)
+    return ref.at[:, pl.ds(first, width)]
+
+
+def product_scatter_kernel(chips, transposed, tile, back, *refs):
+    refs = list(refs)
+    take = lambda count: [refs.pop(0) for _ in range(count)]
+    h_ref, w_ref = take(2)
+    back_in = take(5) if back else None
+    o_ref = take(1)[0]
+    back_out = take(1) if back else None
+    h_v, w_v = take(2)
+    scratch = take(8)
+    w_sem, h_sem = take(2)
+    back_scratch = take(2) if back else None
+    c, k = lax.axis_index("ctx"), lax.axis_index("core")
+    rows = o_ref.shape[0]
+    _, _, _, units = scatter_plan(chips)
+    own, theirs = scratch[:2]
+    if transposed:
+        w_load = pltpu.make_async_copy(core_window(w_ref, w_v.shape[1]), w_v, w_sem)
+    else:
+        w_load = pltpu.make_async_copy(w_ref, w_v, w_sem)
+    w_load.start()
+    loads = {}
+    for m, lane in units:
+        for side, span in enumerate(unit_rows(chips, rows, m, lane)):
+            load = pltpu.make_async_copy(h_ref.at[span], h_v.at[span], h_sem.at[m, lane, side])
+            load.start()
+            loads[m, lane, side] = load
+    greet(chips, c, k)
+    fillers = []
+    if back:
+        fillers = attend_back_parts(*back, *back_in, *back_out, *back_scratch)
+    w_load.wait()
+
+    def compute(m, lane):
+        spans = unit_rows(chips, rows, m, lane)
+        for side in range(CORES):
+            loads[m, lane, side].wait()
+        left = jnp.concatenate([h_v[span, :] for span in spans], axis=0)
+        product_terms(left, w_v, own, theirs, m, lane, transposed, tile)
+
+    exchange(chips, scratch, o_ref, compute, fillers)
+
+
+def product_scatter(h, w, chips, ident, transposed, back=None):
     depth = h.shape[1]
     cols = w.shape[0] if transposed else w.shape[1]
     rows = h.shape[0] // (CORES * chips)
-    half = rows // LANES
-    return pl.pallas_call(
-        functools.partial(product_scatter_kernel, chips, transposed, 512),
+    in_vmem = pl.BlockSpec(memory_space=pltpu.VMEM)
+    in_place = pl.BlockSpec(memory_space=pl.ANY)
+    operands, in_specs = [h, w], [in_place] * 2
+    out_shape = [jax.ShapeDtypeStruct((rows, cols), F32)]
+    back_scratch, sizes = [], None
+    if back is not None:
+        proj, grads, blocks, logsums, heads, size = back
+        operands += [proj, grads, blocks[:, :, None], blocks[:, None, :], logsums]
+        in_specs += [in_vmem] * 5
+        out_shape.append(jax.ShapeDtypeStruct(proj.shape, BF16))
+        back_scratch = [pltpu.VMEM((blocks.shape[1], size), F32)] * 2
+        sizes = (heads, size, 256)
+    result = pl.pallas_call(
+        functools.partial(product_scatter_kernel, chips, transposed, 512, sizes),
         name="product_scatter",
-        out_shape=jax.ShapeDtypeStruct((rows, cols), F32),
-        in_specs=[pl.BlockSpec(memory_space=pl.ANY)] * 2,
-        out_specs=pl.BlockSpec(memory_space=pltpu.VMEM),
+        out_shape=out_shape,
+        in_specs=in_specs,
+        out_specs=[in_vmem] * len(out_shape),
         scratch_shapes=[
             pltpu.VMEM(h.shape, BF16),
-            pltpu.VMEM(w.shape, BF16),
-            pltpu.VMEM((chips, rows, cols), BF16),
-            pltpu.VMEM((chips, rows, cols), BF16),
-            pltpu.VMEM((chips, rows, cols), BF16),
-            pltpu.VMEM((LANES, chips - 1, half, cols), BF16),
-            pltpu.SemaphoreType.DMA((2,)),
-            pltpu.SemaphoreType.DMA((chips, LANES)),
-            pltpu.SemaphoreType.DMA((chips, LANES)),
-            pltpu.SemaphoreType.DMA((LANES, chips - 1)),
-            pltpu.SemaphoreType.DMA((LANES, chips - 1)),
+            pltpu.VMEM((cols, depth) if transposed else w.shape, BF16),
+            *exchange_scratch(chips, rows, cols),
+            pltpu.SemaphoreType.DMA,
+            pltpu.SemaphoreType.DMA((chips, LANES, CORES)),
+            *back_scratch,
         ],
-        cost_estimate=pl.CostEstimate(flops=45_000_000_000, bytes_accessed=0, transcendentals=0),
+        cost_estimate=pl.CostEstimate(flops=1_000_000_000, bytes_accessed=0, transcendentals=0),
         compiler_params=pltpu.CompilerParams(
             collective_id=ident, has_side_effects=True, vmem_limit_bytes=VMEM_LIMIT
         ),
-    )(h, w)
+    )(*operands)
+    return result if len(out_shape) > 1 else result[0]
+
+
+def gelu_slope(u):
+    scale, cubic = math.sqrt(2.0 / math.pi), 0.044715
+    square = u * u
+    bend = jnp.tanh(scale * u * (1.0 + cubic * square))
+    return 0.5 * (1.0 + bend) + 0.5 * u * (1.0 - bend * bend) * scale * (1.0 + 3.0 * cubic * square)
+
+
+def hidden_back_kernel(
+    chips, tile, g_ref, d_ref, p_ref, u_ref, o_ref, e_ref, g_v, p_v, e_v, d_v, u_v, *refs
+):
+    scratch, (w_sem, load_sem, store_sem) = refs[:8], refs[8:]
+    c, k = lax.axis_index("ctx"), lax.axis_index("core")
+    rows = o_ref.shape[0]
+    _, _, _, units = scatter_plan(chips)
+    own, theirs = scratch[:2]
+    d_load = pltpu.make_async_copy(core_window(d_ref, d_v.shape[1]), d_v, w_sem.at[0])
+    u_load = pltpu.make_async_copy(core_window(u_ref, u_v.shape[1]), u_v, w_sem.at[1])
+    d_load.start()
+    loads, stores = {}, []
+    for place, (m, lane) in enumerate(units):
+        if place == 1:
+            u_load.start()
+        for side, span in enumerate(unit_rows(chips, rows, m, lane)):
+            for which, (source, target) in enumerate(((g_ref, g_v), (p_ref, p_v))):
+                load = pltpu.make_async_copy(
+                    source.at[span], target.at[span], load_sem.at[which, m, lane, side]
+                )
+                load.start()
+                loads.setdefault((m, lane), []).append(load)
+    greet(chips, c, k)
+    d_load.wait()
+
+    def compute(m, lane):
+        spans = unit_rows(chips, rows, m, lane)
+        half = rows // LANES
+        for load in loads[m, lane]:
+            load.wait()
+        grads = jnp.concatenate([g_v[span, :] for span in spans], axis=0)
+
+        def body(i, carry):
+            cols = pl.ds(pl.multiple_of(i * tile, tile), tile)
+            part = jnp.dot(grads, d_v[:, cols], preferred_element_type=F32)
+            for side, span in enumerate(spans):
+                slope = gelu_slope(p_v[span, cols])
+                e_v[span, cols] = (part[side * half : (side + 1) * half] * slope).astype(BF16)
+            return carry
+
+        lax.fori_loop(0, e_v.shape[1] // tile, body, 0)
+        for side, span in enumerate(spans):
+            store = pltpu.make_async_copy(e_v.at[span], e_ref.at[span], store_sem.at[m, lane, side])
+            store.start()
+            stores.append(store)
+        if (m, lane) == units[0]:
+            u_load.wait()
+        left = jnp.concatenate([e_v[span, :] for span in spans], axis=0)
+        product_terms(left, u_v, own, theirs, m, lane, True, 512)
+
+    exchange(chips, scratch, o_ref, compute)
+    for store in stores:
+        store.wait()
+
+
+def hidden_back(grads, w_down, pre, w_up, chips, ident):
+    cols, width = w_up.shape[0], pre.shape[1]
+    rows = grads.shape[0] // (CORES * chips)
+    in_place = pl.BlockSpec(memory_space=pl.ANY)
+    return pl.pallas_call(
+        functools.partial(hidden_back_kernel, chips, 256),
+        name="hidden_back",
+        out_shape=[
+            jax.ShapeDtypeStruct((rows, cols), F32),
+            jax.ShapeDtypeStruct((grads.shape[0], width), BF16),
+        ],
+        in_specs=[in_place] * 4,
+        out_specs=[pl.BlockSpec(memory_space=pltpu.VMEM), in_place],
+        scratch_shapes=[
+            pltpu.VMEM(grads.shape, BF16),
+            pltpu.VMEM(pre.shape, pre.dtype),
+            pltpu.VMEM(pre.shape, BF16),
+            pltpu.VMEM((w_down.shape[0], width), BF16),
+            pltpu.VMEM((cols, width), BF16),
+            *exchange_scratch(chips, rows, cols),
+            pltpu.SemaphoreType.DMA((2,)),
+            pltpu.SemaphoreType.DMA((2, chips, LANES, CORES)),
+            pltpu.SemaphoreType.DMA((chips, LANES, CORES)),
+        ],
+        cost_estimate=pl.CostEstimate(flops=1_000_000_000, bytes_accessed=0, transcendentals=0),
+        compiler_params=pltpu.CompilerParams(
+            collective_id=ident, has_side_effects=True, vmem_limit_bytes=VMEM_LIMIT
+        ),
+    )(grads, w_down, pre, w_up)
+
+
+def all_sum_kernel(chips, planes, x_ref, o_ref, landed, send_sem, recv_sem):
+    c, z, k = lax.axis_index("ctx"), lax.axis_index("z"), lax.axis_index("core")
+    partners = [{"ctx": c ^ bit} for bit in chip_bits(chips)] + [{"core": 1 - k}]
+    partners += [{"z": z ^ (2 * bit - 1)} for bit in chip_bits(planes)]
+    barrier = pltpu.get_barrier_semaphore()
+    for partner in partners:
+        pl.semaphore_signal(barrier, inc=1, device_id=partner, device_id_type=MESH)
+    o_ref[...] = x_ref[...]
+    pl.semaphore_wait(barrier, len(partners))
+    for step, partner in enumerate(partners):
+        copy = pltpu.make_async_remote_copy(
+            src_ref=o_ref,
+            dst_ref=landed.at[step],
+            send_sem=send_sem.at[step],
+            recv_sem=recv_sem.at[step],
+            device_id=partner,
+            device_id_type=MESH,
+        )
+        copy.start()
+        copy.wait()
+        o_ref[...] += landed[step]
+
+
+def all_sum(x, chips, planes, ident):
+    in_vmem = pl.BlockSpec(memory_space=pltpu.VMEM)
+    steps = len(chip_bits(chips)) + 1 + len(chip_bits(planes))
+    return pl.pallas_call(
+        functools.partial(all_sum_kernel, chips, planes),
+        name="all_sum",
+        out_shape=jax.ShapeDtypeStruct(x.shape, x.dtype),
+        in_specs=[in_vmem],
+        out_specs=in_vmem,
+        scratch_shapes=[
+            pltpu.VMEM((steps, *x.shape), x.dtype),
+            pltpu.SemaphoreType.DMA((steps,)),
+            pltpu.SemaphoreType.DMA((steps,)),
+        ],
+        compiler_params=pltpu.CompilerParams(collective_id=ident, has_side_effects=True),
+    )(x)
 
 
 def attend_kernel(heads, size, step, p_ref, key_blk, query_blk, o_ref, log_ref):
@@ -323,21 +573,29 @@
             log_ref[0, head : head + 1, span] = top + jnp.log(total)
 
 
-def attend_back_kernel(heads, size, step, p_ref, g_ref, key_blk, query_blk, log_ref, d_ref, dk, dv):
-    length = p_ref.shape[0]
+def attend_back_parts(
+    heads, size, step, p_ref, g_ref, key_blk, query_blk, log_ref, d_ref, dk, dv
+):
+    length = key_blk.shape[1]
     scale = 1.0 / math.sqrt(size)
-    key_block = key_blk[0]
-    for head in range(heads):
-        keys = p_ref[:, (heads + head) * size : (heads + head + 1) * size]
-        values = p_ref[:, (2 * heads + head) * size : (2 * heads + head + 1) * size]
+
+    def part(seq, head):
+        whole = pl.ds(seq * length, length)
+        at_query, at_key, at_value = [
+            slice((j * heads + head) * size, (j * heads + head + 1) * size) for j in range(3)
+        ]
+        keys, values = p_ref[whole, at_key], p_ref[whole, at_value]
         keys_t = keys.T
+        key_block = key_blk[seq]
         for first in range(0, length, step):
-            span = slice(first, first + step)
-            queries = p_ref[span, head * size : (head + 1) * size]
-            grads = g_ref[span, head * size : (head + 1) * size]
+            here = slice(first, first + step)
+            span = pl.ds(seq * length + first, step)
+            queries, grads = p_ref[span, at_query], g_ref[span, at_query]
             scores = contract_last(keys, queries) * scale
             shifted = jnp.where(
-                key_block <= query_blk[0, :, span], scores - log_ref[0, head : head + 1, span], -jnp.inf
+                key_block <= query_blk[seq, :, here],
+                scores - log_ref[seq, head : head + 1, here],
+                -jnp.inf,
             )
             prob = jnp.exp(shifted)
             grad_prob = contract_last(values, grads)
@@ -352,9 +610,15 @@
                 dk[...] += dk_part
                 dv[...] += dv_part
             dq_t = jnp.dot(keys_t, grad_raw, preferred_element_type=F32)
-            d_ref[span, head * size : (head + 1) * size] = dq_t.T.astype(BF16)
-        d_ref[:, (heads + head) * size : (heads + head + 1) * size] = dk[...].astype(BF16)
-        d_ref[:, (2 * heads + head) * size : (2 * heads + head + 1) * size] = dv[...].astype(BF16)
+            d_ref[span, at_query] = dq_t.T.astype(BF16)
+        d_ref[whole, at_key] = dk[...].astype(BF16)
+        d_ref[whole, at_value] = dv[...].astype(BF16)
+
+    return [
+        functools.partial(part, seq, head)
+        for seq in range(key_blk.shape[0])
+        for head in range(heads)
+    ]
 
 
 def attention_specs(length, width, heads):
@@ -380,26 +644,9 @@
         ),
         in_specs=[wide, column, row],
         out_specs=(narrow, logs),
-        cost_estimate=pl.CostEstimate(flops=15_000_000_000, bytes_accessed=0, transcendentals=0),
+        cost_estimate=pl.CostEstimate(flops=1_000_000_000, bytes_accessed=0, transcendentals=0),
         compiler_params=pltpu.CompilerParams(vmem_limit_bytes=VMEM_LIMIT),
     )(proj, blocks[:, :, None], blocks[:, None, :])
-
-
-def attend_back(proj, grads, blocks, logsums, heads, size):
-    length = blocks.shape[1]
-    width = heads * size
-    wide, narrow, column, row, logs = attention_specs(length, width, heads)
-    return pl.pallas_call(
-        functools.partial(attend_back_kernel, heads, size, 256),
-        name="attend_back",
-        grid=(blocks.shape[0],),
-        out_shape=jax.ShapeDtypeStruct(proj.shape, BF16),
-        in_specs=[wide, narrow, column, row, logs],
-        out_specs=wide,
-        scratch_shapes=[pltpu.VMEM((length, size), F32)] * 2,
-        cost_estimate=pl.CostEstimate(flops=30_000_000_000, bytes_accessed=0, transcendentals=0),
-        compiler_params=pltpu.CompilerParams(vmem_limit_bytes=VMEM_LIMIT),
-    )(proj, grads, blocks[:, :, None], blocks[:, None, :], logsums)
 
 
 def shards(
@@ -427,51 +674,44 @@
     ff_cols = hidden_width // team
     fsdp = ("z", "core")
 
-    def chip_cols(w, width):
-        return lax.dynamic_slice_in_dim(w, c * (CORES * width), CORES * width, 1)
-
-    def own_slice(w, width):
-        parts = w.reshape(w.shape[0], -1, CORES, width).transpose(2, 0, 1, 3)
-        parts = parts.reshape(CORES, w.shape[0], -1)
-        full = lax.all_gather(parts, fsdp, axis=0, tiled=False)
-        mine = lax.dynamic_index_in_dim(full, k, 1, keepdims=False)
-        return mine.reshape(model_width, -1)
-
-    qkv_cols = jnp.concatenate(
-        [chip_cols(part, head_cols) for part in jnp.split(w_qkv, 3, axis=1)], axis=1
-    )
-    my_qkv = own_slice(qkv_cols, head_cols)
-    out_cols = model_width // chips
-    out_gathered = lax.all_gather(
-        lax.dynamic_slice_in_dim(w_out, c * out_cols, out_cols, 1), fsdp, axis=0, tiled=True
-    )
-    out_rows = lax.all_to_all(out_gathered, "ctx", split_axis=0, concat_axis=1, tiled=True)
-    my_out = lax.dynamic_slice_in_dim(out_rows, k * head_cols, head_cols, 0)
-    my_up = own_slice(chip_cols(w_up, ff_cols), ff_cols)
-    my_down = own_slice(chip_cols(w_down, ff_cols), ff_cols)
-
-    blocks = stored_blocks(block_ids, piece_order, row_count // 2)
-    blocks = lax.all_gather(blocks, "core", axis=0, tiled=True)
-
+    def core_cols(gathered, width, first=0):
+        return lax.dynamic_slice_in_dim(gathered, first + k * width, width, 1)
+
+    def across_z(w):
+        return lax.all_gather(w, fsdp, axis=0, tiled=True)
+
+    attn_cols, up_cols, down_cols = pick_columns(w_qkv, w_out, w_up, w_down, head_cols, ff_cols)
+    attn_weights = across_z(attn_cols)
     inputs = tokens.reshape(row_count, model_width).astype(F32)
     grad_y = grad_out.reshape(row_count, model_width)
     normed_one, unit_one, inv_one = normalize(inputs, norm1_gain, norm1_bias)
     acts_one = plane_gather(normed_one.astype(BF16), chips, 1)
+    acts_one, block_ids, grad_y = lax.optimization_barrier((acts_one, block_ids, grad_y))
+    up_weights = across_z(up_cols)
+    down_weights = across_z(down_cols)
+    blocks = stored_blocks(block_ids, piece_order, row_count // 2)
+    blocks = lax.all_gather(blocks, "core", axis=0, tiled=True)
+
     grads_y = plane_gather(grad_y, chips, 1)
-    proj = jnp.dot(acts_one, my_qkv, preferred_element_type=F32).astype(BF16)
+    my_attn = core_cols(attn_weights, 4 * head_cols)
+    out_blocks = my_attn[:, 3 * head_cols :]
+    my_out = lax.all_to_all(out_blocks, ("ctx", "core"), split_axis=0, concat_axis=1, tiled=True)
+    proj = jnp.dot(acts_one, my_attn[:, : 3 * head_cols], preferred_element_type=F32).astype(BF16)
     attended, logsums = attend(proj, blocks, heads, size)
     residual = inputs + product_scatter(attended, my_out, chips, 2, False)
     normed_two, unit_two, inv_two = normalize(residual, norm2_gain, norm2_bias)
     acts_two = plane_gather(normed_two.astype(BF16), chips, 1)
+    up_weights, acts_two = lax.optimization_barrier((up_weights, acts_two))
+    my_up = core_cols(up_weights, ff_cols)
     pre_act = jnp.dot(acts_two, my_up, preferred_element_type=F32)
-    gelu_tanh = functools.partial(jax.nn.gelu, approximate=True)
-    hidden_full, gelu_pull = jax.vjp(gelu_tanh, pre_act)
-    hidden = hidden_full.astype(BF16)
-
-    def spread_rows(grad):
-        rounded = grad.astype(BF16).reshape(chips, -1, grad.shape[1])
-        summed = lax.psum_scatter(rounded, "z", scatter_dimension=1, tiled=True)
-        summed = summed.reshape(team, -1, grad.shape[1])
+    hidden = jax.nn.gelu(pre_act, approximate=True).astype(BF16)
+
+    def sum_planes(grad):
+        parts = grad.reshape(chips, -1, grad.shape[1])
+        return lax.psum_scatter(parts, "z", scatter_dimension=1, tiled=True)
+
+    def spread_rows(summed):
+        summed = summed.reshape(team, -1, summed.shape[2])
         return lax.all_to_all(summed, ("ctx", "core"), split_axis=0, concat_axis=0, tiled=True)
 
     def whole_columns(parts, width):
@@ -483,33 +723,47 @@
             .astype(F32)
         )
 
-    grad_down = whole_columns(spread_rows(contract_first(grads_y, hidden)), ff_cols)
-    grad_hidden = jnp.dot(grads_y, my_down, preferred_element_type=F32)
-    grad_pre = gelu_pull(grad_hidden)[0].astype(BF16)
-    grad_up = whole_columns(spread_rows(contract_first(acts_two, grad_pre)), ff_cols)
-    grad_act_two = product_scatter(grad_pre, my_up, chips, 3, True)
+    down_part = contract_first(grads_y, hidden).astype(BF16)
+    down_weights, down_part = lax.optimization_barrier((down_weights, down_part))
+    down_sum = sum_planes(down_part)
+    grad_act_two, grad_pre = hidden_back(grads_y, down_weights, pre_act, up_weights, chips, 3)
+    up_part = contract_first(acts_two, grad_pre).astype(BF16)
+    grad_act_two, up_part = lax.optimization_barrier((grad_act_two, up_part))
+    up_sum = sum_planes(up_part)
     grad_res = grad_y.astype(F32) + normalize_back(grad_act_two, unit_two, inv_two, norm2_gain)
     grads_res = plane_gather(grad_res.astype(BF16), chips, 1)
     grad_attended = contract_last(grads_res, my_out).astype(BF16)
-    grad_proj = attend_back(proj, grad_attended, blocks, logsums, heads, size)
-    grad_qkv = whole_columns(spread_rows(contract_first(acts_one, grad_proj)), head_cols)
-    out_part = lax.psum_scatter(
-        contract_first(attended, grads_res).astype(BF16), "z", scatter_dimension=0, tiled=True
-    )
-    moves = [(z * CORES + core, core * depth + z) for z in range(depth) for core in range(CORES)]
-    grad_wout = lax.ppermute(out_part, fsdp, moves).astype(F32)
-    mixed = residual + product_scatter(hidden, my_down, chips, 3, True)
-    grad_act_one = product_scatter(grad_proj, my_qkv, chips, 4, True)
-    grad_inputs = grad_res + normalize_back(grad_act_one, unit_one, inv_one, norm1_gain)
-    norm_sums = lax.psum(
-        (
+    out_part = contract_first(attended, grads_res).astype(BF16)
+    grad_attended, out_part, down_sum = lax.optimization_barrier(
+        (grad_attended, out_part, down_sum)
+    )
+    grad_down = whole_columns(spread_rows(down_sum), ff_cols)
+    out_sum = lax.psum_scatter(out_part, "z", scatter_dimension=0, tiled=True)
+    mixed_sum, grad_proj = product_scatter(
+        hidden, down_weights, chips, 5, True, back=(proj, grad_attended, blocks, logsums, heads, size)
+    )
+    proj_part = contract_first(acts_one, grad_proj).astype(BF16)
+    grad_proj, proj_part, up_sum, out_sum = lax.optimization_barrier(
+        (grad_proj, proj_part, up_sum, out_sum)
+    )
+    proj_sum = sum_planes(proj_part)
+    grad_act_one = product_scatter(grad_proj, attn_weights, chips, 4, True)
+    mixed = residual + mixed_sum
+    norm_parts = jnp.stack(
+        [
             jnp.sum(grad_act_one * unit_one, axis=0),
             jnp.sum(grad_act_one, axis=0),
             jnp.sum(grad_act_two * unit_two, axis=0),
             jnp.sum(grad_act_two, axis=0),
-        ),
-        ("ctx", "z", "core"),
-    )
+        ]
+        + [jnp.zeros((model_width,), F32)] * 4
+    )
+    norm_sums = all_sum(norm_parts, chips, depth, 6)
+    grad_up = whole_columns(spread_rows(up_sum), ff_cols)
+    moves = [(z * CORES + core, core * depth + z) for z in range(depth) for core in range(CORES)]
+    grad_wout = lax.ppermute(out_sum, fsdp, moves).astype(F32)
+    grad_qkv = whole_columns(spread_rows(proj_sum), head_cols)
+    grad_inputs = grad_res + normalize_back(grad_act_one, unit_one, inv_one, norm1_gain)
     out_shape = (1, row_count, model_width)
     return (
         mixed.reshape(out_shape).astype(BF16),
@@ -518,7 +772,7 @@
         grad_wout,
         grad_up,
         grad_down,
-        *norm_sums,
+        *norm_sums[:4],
     )
 
 

time: 806 us -> 592 us (0.73)
  waiting for transfers between devices: 158 us -> 29.5 us
  blocking collectives: 43.3 us -> 1.91 us
  local copies, waits for them, and re-layouts: 42.3 us -> 15.3 us
  matrix products: 95.8 us -> 79.9 us
    reduce_scatter x4, waiting for transfers between devices: 134 us -> 0.01 us  [the longest x3 0.01 us: sum_planes(): return lax.psum_scatter(parts, 'z', scatter_dimension=1, tiled=True)]
    pallas_call x1 -> x3, Pallas kernels: 16.9 us -> 79.5 us  [the longest x1 58.1 us: hidden_back(): pl.pallas_call(functools.partial(hidden_back_kernel, chips, 256), name='h...]
    pallas_call x4 -> x3, Pallas kernels: 189 us -> 146 us  [product_scatter(): pl.pallas_call(functools.partial(product_scatter_kernel, chips, transpose...]
    psum x1 -> x0, blocking collectives: 41.2 us -> none  [shards(): lax.psum((jnp.sum(grad_act_one * unit_one, axis=0), jnp.sum(grad_act_one,...]
    pallas_call x4, Pallas kernels: 185 us -> 161 us  [plane_gather(): pl.pallas_call(functools.partial(gather_kernel, chips, pieces), name='pla...]
    dot_general x2 -> x1, matrix products: 29.5 us -> 11.2 us  [shards(): jnp.dot(acts_one, my_attn[:, :3 * head_cols], preferred_element_type=F32)]
    all_to_all x3, waiting for transfers between devices: 5.83 us -> 20.7 us  [spread_rows(): lax.all_to_all(summed, ('ctx', 'core'), split_axis=0, concat_axis=0, tile...]
    dynamic_slice x8 -> x0, local copies, waits for them, and re-layouts: 13.5 us -> none  [the longest x2 9 us: own_slice(): mine = lax.dynamic_index_in_dim(full, k, 1, keepdims=False)]
  transfers between devices with their start and end apart: 13 -> 12, of which waited for: 6 -> 3; matrix products, arithmetic and copies ran while one was open for 11% -> 19% of each run, Pallas kernels for 32% -> 68%
where the time goes in v2:
time: 592 us; the launch traced here: 589 us
  Pallas kernels  404 us (68%)
  matrix products  79.9 us (13%)
  waiting for transfers between devices  29.5 us (5%)
  other arithmetic  24.1 us (4%)
  starting transfers between devices  19.9 us (3%)
  local copies, waits for them, and re-layouts  15.3 us (3%)
  between operations  14.8 us (2%)
    pallas_call x4, Pallas kernels, plane_gather(): pl.pallas_call(functools.partial(gather_kernel, chips, pieces), name='pla...  161 us
    pallas_call x3, Pallas kernels, product_scatter(): pl.pallas_call(functools.partial(product_scatter_kernel, chips, transpose...  146 us
    pallas_call x1, Pallas kernels, hidden_back(): pl.pallas_call(functools.partial(hidden_back_kernel, chips, 256), name='h...  58.1 us
    dot_general x4, matrix products, contract_first(): lax.dot_general(left_arr, right_arr, (((0,), (0,)), ((), ())), preferred_...  45.9 us
    all_to_all x3, waiting for transfers between devices, spread_rows(): lax.all_to_all(summed, ('ctx', 'core'), split_axis=0, concat_axis=0, tile...  20.7 us
    pallas_call x1, Pallas kernels, all_sum(): pl.pallas_call(functools.partial(all_sum_kernel, chips, planes), name='al...  17.7 us
    pallas_call x1, Pallas kernels, attend(): pl.pallas_call(functools.partial(attend_kernel, heads, size, 256), name='...  16.2 us
    dot_general x1, matrix products, shards(): pre_act = jnp.dot(acts_two, my_up, preferred_element_type=F32)  15.7 us
  transfers between devices with their start and end apart: 12, of which 3 were waited for; matrix products, arithmetic and copies ran while one was open for 19% of the time, Pallas kernels for 68%

profile of v2, /device:TPU:0, one launch (start us, length us, event | category | flops | bytes accessed | tf_op | source)
XLA Modules:
  0.0 588.8 jit_solution(214293340260333419)
XLA Ops:
  7.2 3.7 pick_columns.1
  14.6 41.9 %plane_gather.4 = bf16[2048,2048]{1,0:T(8,128)(2,1)} custom-call(bf16[256,2048]{1,0:T(8,128)(2,1)} %fusion.20.x_ref), custom_call_target="tpu_custom_call" | custom-call | flops 1000000000 | tf_op jit(solution)/shard_map/plane_gather/pallas_call | solution.py:143
  60.5 39.9 %plane_gather.6.g_ref = bf16[2048,2048]{1,0:T(8,128)(2,1)} custom-call(bf16[256,2048]{1,0:T(8,128)(2,1)} %bitcast.122), custom_call_target="tpu_custom_call" | custom-call | flops 1000000000 | tf_op jit(solution)/shard_map/plane_gather/pallas_call | solution.py:143
  100.5 2.3 constant_dynamic-slice_fusion
  102.8 3.6 all-to-all-start
  106.9 11.2 %convolution_convert_fusion.2.p_ref.refs_2_ = bf16[2048,768]{1,0:T(8,128)(2,1)} fusion(bf16[2048,2048]{1,0:T(8,128)(2,1)} %plane_gather.4, bf16[2048,2048]{1,0:T(8,128)(2,1)} %all-gather.5.cloned.1.call-done.refs_1_, s32[]{:T(128)S(6)} %select_n.22), kind=kOutput, calls=%fused_computation.14 | convolution fusion | flops 6444023808 | bytes 14680068 | tf_op jit(solution)/shard_map/dot_general | solution.py:699
  118.1 16.2 %attend.1 = (bf16[2048,256]{1,0:T(8,128)(2,1)}, f32[2,2,1024]{2,1,0:T(2,128)}) custom-call(bf16[2048,768]{1,0:T(8,128)(2,1)} %convolution_convert_fusion.2.p_ref.refs_2_, s32[2,1024,1]{2,1,0:T(8,128)} %broadcast_in_dim.42.key_blk.refs_4_, s32[2,1,1024]{2,1,0:T(1,128)} %copy-done.8), custom_call_target="tpu_custom_call" | custom-call | flops 1000000000 | tf_op jit(solution)/shard_map/attend/pallas_call | solution.py:637
  135.4 44.2 %product_scatter.3 = f32[256,2048]{1,0:T(8,128)} custom-call(bf16[2048,256]{1,0:T(8,128)(2,1)} %get-tuple-element.38.refs_0_, bf16[256,2048]{1,0:T(8,128)(2,1)} %bitcast.127), custom_call_target="tpu_custom_call" | custom-call | flops 1000000000 | tf_op jit(solution)/shard_map/product_scatter/pallas_call | solution.py:398
  183.8 40.0 %plane_gather.5 = bf16[2048,2048]{1,0:T(8,128)(2,1)} custom-call(bf16[256,2048]{1,0:T(8,128)(2,1)} %add_convert_fusion.1.x_ref), custom_call_target="tpu_custom_call" | custom-call | flops 1000000000 | tf_op jit(solution)/shard_map/plane_gather/pallas_call | solution.py:143
  223.8 15.7 %fusion.7 = (bf16[2048,1024]{1,0:T(8,128)(2,1)S(1)}, f32[2048,1024]{1,0:T(8,128)}) fusion(bf16[2048,2048]{1,0:T(8,128)(2,1)} %plane_gather.5, bf16[2048,2048]{1,0:T(8,128)(2,1)} %all-gather.7.cloned.1.call-done.u_ref, s32[]{:T(128)S(6)} %select_n.22), kind=kOutput, calls=%fused_computation.9 | convolution fusion | flops 8608808960 | bytes 25165828 | tf_op jit(solution)/shard_map/dot_general | solution.py:706
  239.5 1.9 copy-done.5
  241.4 12.9 %convolution_convert_fusion.1 = bf16[2048,1024]{1,0:T(8,128)(2,1)} fusion(bf16[2048,2048]{1,0:T(8,128)(2,1)} %plane_gather.6.g_ref, bf16[2048,1024]{1,0:T(8,128)(2,1)S(1)} %get-tuple-element.76.refs_0_), kind=kOutput, calls=%fused_computation.13 | convolution fusion | flops 8592031744 | bytes 16777216 | tf_op jit(solution)/shard_map/dot_general | solution.py:49
  254.3 7.4 %all-gather.9.cloned.1.call-done.d_ref.refs_1_ = bf16[2048,2048]{1,0:T(8,128)(2,1)} async-done(((bf16[256,2048]{1,0:T(8,128)(2,1)}), bf16[2048,2048]{1,0:T(8,128)(2,1)}) %all-gather.9.cloned.1.call-update) | async-done | bytes 8388624 | tf_op jit(solution)/shard_map/all_gather | solution.py:681
  261.8 58.1 %hidden_back.1 = (f32[256,2048]{1,0:T(8,128)}, bf16[2048,1024]{1,0:T(8,128)(2,1)}) custom-call(bf16[2048,2048]{1,0:T(8,128)(2,1)} %plane_gather.6.g_ref, bf16[2048,2048]{1,0:T(8,128)(2,1)} %all-gather.9.cloned.1.call-done.d_ref.refs_1_, f32[2048,1024]{1,0:T(8,128)} %get-tuple-element.77.p_ref, bf16[2048,2048]{1,0:T(8,128)(2,1)} %all-gather.7.cloned.1.call-done.u_ref), custom_call_target="tpu_custom_call" | custom-call | flops 1000000000 | tf_op jit(solution)/shard_map/hidden_back/pallas_call | solution.py:486
  319.9 14.5 %convolution_convert_fusion = bf16[2048,1024]{1,0:T(8,128)(2,1)} fusion(bf16[2048,2048]{1,0:T(8,128)(2,1)} %plane_gather.5, bf16[2048,1024]{1,0:T(8,128)(2,1)} %get-tuple-element.46), kind=kOutput, calls=%fused_computation.12 | convolution fusion | flops 8592031744 | bytes 16777216 | tf_op jit(solution)/shard_map/dot_general | solution.py:49
  334.5 2.7 multiply_reduce_fusion
  337.3 2.6 fusion.33
  339.9 39.5 %plane_gather.7 = bf16[2048,2048]{1,0:T(8,128)(2,1)} custom-call(bf16[256,2048]{1,0:T(8,128)(2,1)} %get-tuple-element.68.x_ref), custom_call_target="tpu_custom_call" | custom-call | flops 1000000000 | tf_op jit(solution)/shard_map/plane_gather/pallas_call | solution.py:143
  379.4 7.1 %convolution_convert_fusion.4 = bf16[256,2048]{1,0:T(8,128)(2,1)} fusion(bf16[2048,256]{1,0:T(8,128)(2,1)} %get-tuple-element.38.refs_0_, bf16[2048,2048]{1,0:T(8,128)(2,1)} %plane_gather.7), kind=kOutput, calls=%fused_computation.21 | convolution fusion | flops 2148007936 | bytes 10485760 | tf_op jit(solution)/shard_map/dot_general | solution.py:49
  386.4 7.1 %convolution_convert_fusion.5.refs_3_ = bf16[2048,256]{1,0:T(8,128)(2,1)} fusion(bf16[2048,2048]{1,0:T(8,128)(2,1)} %plane_gather.7, bf16[256,2048]{1,0:T(8,128)(2,1)} %bitcast.128), kind=kOutput, calls=%fused_computation.22 | convolution fusion | flops 2148007936 | bytes 10485760 | tf_op jit(solution)/shard_map/dot_general | solution.py:43
  393.6 51.8 %product_scatter.4 = (f32[256,2048]{1,0:T(8,128)}, bf16[2048,768]{1,0:T(8,128)(2,1)}) custom-call(bf16[2048,1024]{1,0:T(8,128)(2,1)} %copy-done.5, bf16[2048,2048]{1,0:T(8,128)(2,1)} %all-gather.9.cloned.1.call-done.d_ref.refs_1_, bf16[2048,768]{1,0:T(8,128)(2,1)} %convolution_convert_fusion.2.p_ref.refs_2_, ...), custom_call_target="tpu_custom_call" | custom-call | flops 1000000000 | tf_op jit(solution)/shard_map/product_scatter/pallas_call | solution.py:398
  445.4 11.4 %convolution_convert_fusion.3 = bf16[2048,768]{1,0:T(8,128)(2,1)} fusion(bf16[2048,2048]{1,0:T(8,128)(2,1)} %plane_gather.4, bf16[2048,768]{1,0:T(8,128)(2,1)} %get-tuple-element.55.refs_0_), kind=kOutput, calls=%fused_computation.15 | convolution fusion | flops 6444023808 | bytes 14680064 | tf_op jit(solution)/shard_map/dot_general | solution.py:49
  456.9 4.3 all-to-all-start.3
  461.1 3.0 fusion.28
  464.1 12.5 %all-to-all-done.3 = bf16[8,64,1024]{2,1,0:T(8,128)(2,1)} async-done(((bf16[8,64,1024]{2,1,0:T(8,128)(2,1)}), bf16[8,64,1024]{2,1,0:T(8,128)(2,1)}, u32[]{:S(2)}, u32[]{:S(2)}) %all-to-all-start.3) | async-done | bytes 1048608 | tf_op jit(solution)/shard_map/all_to_all | solution.py:715
  479.5 4.5 all-to-all-start.2
  484.0 50.4 %product_scatter.5 = f32[256,2048]{1,0:T(8,128)} custom-call(bf16[2048,768]{1,0:T(8,128)(2,1)} %get-tuple-element.55.refs_0_, bf16[2048,2048]{1,0:T(8,128)(2,1)} %all-gather.5.cloned.1.call-done.refs_1_), custom_call_target="tpu_custom_call" | custom-call | flops 1000000000 | tf_op jit(solution)/shard_map/product_scatter/pallas_call | solution.py:398
  534.4 2.7 fusion.26
  537.9 17.7 %all_sum.1 = f32[8,2048]{1,0:T(8,128)} custom-call(f32[8,2048]{1,0:T(8,128)} %stack.23.x_ref), custom_call_target="tpu_custom_call" | custom-call | tf_op jit(solution)/shard_map/all_sum/pallas_call | solution.py:539
  557.1 3.4 fusion.29
  560.6 5.1 all-to-all-start.1
  570.1 8.2 %all-to-all-done.1 = bf16[8,64,768]{2,1,0:T(8,128)(2,1)S(1)} async-done(((bf16[8,64,768]{2,1,0:T(8,128)(2,1)}), bf16[8,64,768]{2,1,0:T(8,128)(2,1)S(1)}, u32[]{:S(2)}, u32[]{:S(2)}) %all-to-all-start.1) | async-done | bytes 786464 | tf_op jit(solution)/shard_map/all_to_all | solution.py:715
  (85 shorter events, 26.5 us)
Async XLA Ops:
  7.2 49.4 %copy-start = (s32[1,1024]{1,0:T(1,128)S(1)}, s32[1,1024]{1,0:T(1,128)}, u32[]{:S(2)}) copy-start(s32[1,1024]{1,0:T(1,128)} %param.13) | copy-start | bytes 12292
  7.2 93.3 %all-gather.5.cloned.1.call-start = ((), (), s32[]{:S(2)}) async-start(), calls=%async_computation.8 | async-start | bytes 9437184 | tf_op jit(solution)/shard_map/all_gather | solution.py:681
  11.0 1.5 copy-start.2
  11.0 212.8 %all-gather.7.cloned.1.call-start = ((), (), s32[]{:S(2)}) async-start(), calls=%async_computation.9 | async-start | bytes 9437184 | tf_op jit(solution)/shard_map/all_gather | solution.py:681
  11.1 2.1 copy-start.10
  11.1 2.1 copy-start.11
  11.8 249.9 %all-gather.9.cloned.1.call-start = ((), (), s32[]{:S(2)}) async-start(), calls=%async_computation.10 | async-start | bytes 9437184 | tf_op jit(solution)/shard_map/all_gather | solution.py:681
  14.6 41.9 %copy-start.13 = (s32[8]{0:T(128)S(1)}, s32[8]{0:T(128)}, u32[]{:S(2)}) copy-start(s32[8]{0:T(128)} %param.14) | copy-start | bytes 100
  59.2 41.3 %copy-start.8 = (s32[2,1,1024]{2,1,0:T(1,128)}, s32[2,1,1024]{2,1,0:T(1,128)S(1)}, u32[]{:S(2)}) copy-start(s32[2,1,1024]{2,1,0:T(1,128)S(1)} %all-gather.query_blk.refs_5_) | copy-start | bytes 24580
  102.8 31.6 %all-to-all-start = ((bf16[8,256,256]{2,1,0:T(8,128)(2,1)}), bf16[8,256,256]{2,1,0:T(8,128)(2,1)S(1)}, u32[]{:S(2)}, u32[]{:S(2)}) async-start(bf16[8,256,256]{2,1,0:T(8,128)(2,1)} %bitcast.5), calls=%async_computation | async-start | bytes 2097152 | tf_op jit(solution)/shard_map/all_to_all | solution.py:698
  106.3 287.2 %reduce-scatter.5.cloned.1.call-start = ((), (), s32[]{:S(2)}) async-start(), calls=%async_computation.11 | async-start | bytes 5242880 | tf_op jit(solution)/shard_map/reduce_scatter | solution.py:711
  181.6 0.7 copy-start.9
  181.6 0.7 copy-start.12
  239.5 1.9 copy-start.5
  261.7 195.1 %reduce-scatter.7.cloned.1.call-start = ((), (), s32[]{:S(2)}) async-start(), calls=%async_computation.12 | async-start | bytes 5242880 | tf_op jit(solution)/shard_map/reduce_scatter | solution.py:711
  334.5 122.4 %reduce-scatter.9.cloned.1.call-start = ((), (), s32[]{:S(2)}) async-start(), calls=%async_computation.13 | async-start | bytes 1310720 | tf_op jit(solution)/shard_map/reduce_scatter | solution.py:741
  334.5 2.7 copy-start.4
  334.5 2.7 copy-start.6
  393.5 167.0 %reduce-scatter.11.cloned.1.call-start = ((), (), s32[]{:S(2)}) async-start(), calls=%async_computation.14 | async-start | bytes 3932160 | tf_op jit(solution)/shard_map/reduce_scatter | solution.py:711
  456.9 19.7 %all-to-all-start.3 = ((bf16[8,64,1024]{2,1,0:T(8,128)(2,1)}), bf16[8,64,1024]{2,1,0:T(8,128)(2,1)}, u32[]{:S(2)}, u32[]{:S(2)}) async-start(bf16[8,64,1024]{2,1,0:T(8,128)(2,1)} %bitcast.133), calls=%async_computation.7 | async-start | bytes 2097152 | tf_op jit(solution)/shard_map/all_to_all | solution.py:715
  479.5 81.1 %all-to-all-start.2 = ((bf16[8,64,1024]{2,1,0:T(8,128)(2,1)}), bf16[8,64,1024]{2,1,0:T(8,128)(2,1)}, u32[]{:S(2)}, u32[]{:S(2)}) async-start(bf16[8,64,1024]{2,1,0:T(8,128)(2,1)} %bitcast.14), calls=%async_computation.6 | async-start | bytes 2097152 | tf_op jit(solution)/shard_map/all_to_all | solution.py:715
  534.4 22.7 %copy-start.3 = (f32[256,2048]{1,0:T(8,128)S(1)}, f32[256,2048]{1,0:T(8,128)}, u32[]{:S(2)}) copy-start(f32[256,2048]{1,0:T(8,128)} %product_scatter.5) | copy-start | bytes 6291460
  555.5 10.8 %collective-permute-start = (bf16[64,2048]{1,0:T(8,128)(2,1)}, bf16[64,2048]{1,0:T(8,128)(2,1)S(1)}, u32[]{:S(2)}, u32[]{:S(2)}) collective-permute-start(bf16[64,2048]{1,0:T(8,128)(2,1)} %reduce-scatter.9.cloned.1.call-done), channel_id=1, source_target_pairs={{0,0},{1,4},{2,1},{3,5},{4,2},{5,6},{6,3},{7,7},{8,8},{9,12},{10,9... | collective-permute-start | bytes 786440 | tf_op jit(solution)/shard_map/ppermute | solution.py:764
  557.1 8.6 %copy-start.7 = (f32[8,2048]{1,0:T(8,128)S(1)}, f32[8,2048]{1,0:T(8,128)}, u32[]{:S(2)}) copy-start(f32[8,2048]{1,0:T(8,128)} %all_sum.1) | copy-start | bytes 196612
  560.6 17.7 %all-to-all-start.1 = ((bf16[8,64,768]{2,1,0:T(8,128)(2,1)}), bf16[8,64,768]{2,1,0:T(8,128)(2,1)S(1)}, u32[]{:S(2)}, u32[]{:S(2)}) async-start(bf16[8,64,768]{2,1,0:T(8,128)(2,1)} %bitcast.134), calls=%async_computation.5 | async-start | bytes 1572864 | tf_op jit(solution)/shard_map/all_to_all | solution.py:715
  579.2 2.6 copy-start.1
Sparse Core Ops, SparseCore 0:
  11.2 84.7 all-gather.4
  98.1 80.7 all-gather.6
  181.1 80.5 all-gather.8
  263.8 75.2 reduce-scatter.4
  341.4 77.2 reduce-scatter.6
  421.5 27.6 reduce-scatter.8
  457.0 57.7 reduce-scatter.10

commit v3 on v2

--- a/solution.py
+++ b/solution.py
@@ -213,11 +213,11 @@
                     count += 1
         for m in range(1, chips):
             sends[m, lane] = min(i for i, b in enumerate(orders[lane]) if m & b)
-    units = sorted(
-        ((m, lane) for m in range(chips) for lane in range(LANES)),
-        key=lambda u: (sends.get(u, len(orders[0])), -bin(u[0]).count("1"), u[1], u[0]),
-    )
-    return orders, slots, sends, units
+    return orders, slots, sends
+
+
+def block_order(chips):
+    return sorted(range(chips), key=lambda m: (-bin(m).count("1"), m))
 
 
 def exchange_scratch(chips, rows, cols):
@@ -238,7 +238,7 @@
     own, theirs, from_core, from_chip, core_send, core_recv, chip_send, chip_recv = scratch
     c, k = lax.axis_index("ctx"), lax.axis_index("core")
     half = o_ref.shape[0] // LANES
-    orders, slots, sends, units = scatter_plan(chips)
+    orders, slots, sends = scatter_plan(chips)
     waits = []
 
     def share(m, lane):
@@ -289,34 +289,37 @@
         copy.start()
         waits.append(copy)
 
-    fillers = list(fillers)
-    pending = []
-    for m, lane in units:
-        compute(m, lane)
-        pending.append((m, lane, share(m, lane)))
-        if len(pending) > 1 and sends.get(pending[0][:2]) == 0:
-            combine(*pending.pop(0))
-    for level in range(1, len(orders[0]) + 1):
-        count = -(-len(fillers) // (len(orders[0]) + 1 - level))
+    fillers, pending, last = list(fillers), [], len(orders[0])
+
+    def settle(level):
+        for unit in [u for u in pending if sends.get(u[:2], last) <= level]:
+            pending.remove(unit)
+            combine(*unit)
+
+    for m in block_order(chips):
+        compute(m)
+        fresh = [(m, lane, share(m, lane)) for lane in range(LANES)]
+        settle(0)
+        pending += fresh
+    settle(0)
+    for level in range(1, last + 1):
+        count = -(-len(fillers) // (last + 1 - level))
         for filler in fillers[:count]:
             filler()
         fillers = fillers[count:]
-        while pending and sends.get(pending[0][:2], len(orders[0])) <= level:
-            combine(*pending.pop(0))
+        settle(level)
     for copy in waits:
         copy.wait_send()
 
 
-def unit_rows(chips, rows, m, lane):
+def block_rows(chips, rows, m):
     c, k = lax.axis_index("ctx"), lax.axis_index("core")
-    half = rows // LANES
-    starts = [(core * chips + (c ^ m)) * rows + lane * half for core in (k, 1 - k)]
-    return [pl.ds(pl.multiple_of(start, half), half) for start in starts]
-
-
-def product_terms(left, w_v, own, theirs, m, lane, transposed, tile):
-    half, cols = left.shape[0] // CORES, own.shape[2]
-    rows = pl.ds(lane * half, half)
+    starts = [(core * chips + (c ^ m)) * rows for core in (k, 1 - k)]
+    return [pl.ds(pl.multiple_of(start, rows), rows) for start in starts]
+
+
+def product_terms(left, w_v, own, theirs, m, transposed, tile):
+    rows, cols = own.shape[1:]
 
     def body(i, carry):
         span = pl.ds(pl.multiple_of(i * tile, tile), tile)
@@ -324,8 +327,8 @@
             part = contract_last(left, w_v[span, :])
         else:
             part = jnp.dot(left, w_v[:, span], preferred_element_type=F32)
-        own[m, rows, span] = part[:half].astype(BF16)
-        theirs[m, rows, span] = part[half:].astype(BF16)
+        own[m, :, span] = part[:rows].astype(BF16)
+        theirs[m, :, span] = part[rows:].astype(BF16)
         return carry
 
     lax.fori_loop(0, cols // tile, body, 0)
@@ -342,15 +345,17 @@
     take = lambda count: [refs.pop(0) for _ in range(count)]
     h_ref, w_ref = take(2)
     back_in = take(5) if back else None
+    a_ref = take(1)[0] if back else None
     o_ref = take(1)[0]
     back_out = take(1) if back else None
+    q_ref = take(1)[0] if back else None
     h_v, w_v = take(2)
     scratch = take(8)
     w_sem, h_sem = take(2)
     back_scratch = take(2) if back else None
+    a_v, a_sem = take(2) if back else (None, None)
     c, k = lax.axis_index("ctx"), lax.axis_index("core")
     rows = o_ref.shape[0]
-    _, _, _, units = scatter_plan(chips)
     own, theirs = scratch[:2]
     if transposed:
         w_load = pltpu.make_async_copy(core_window(w_ref, w_v.shape[1]), w_v, w_sem)
@@ -358,25 +363,39 @@
         w_load = pltpu.make_async_copy(w_ref, w_v, w_sem)
     w_load.start()
     loads = {}
-    for m, lane in units:
-        for side, span in enumerate(unit_rows(chips, rows, m, lane)):
-            load = pltpu.make_async_copy(h_ref.at[span], h_v.at[span], h_sem.at[m, lane, side])
+    for m in block_order(chips):
+        for side, span in enumerate(block_rows(chips, rows, m)):
+            load = pltpu.make_async_copy(h_ref.at[span], h_v.at[span], h_sem.at[m, side])
             load.start()
-            loads[m, lane, side] = load
-    greet(chips, c, k)
+            loads[m, side] = load
     fillers = []
     if back:
+        a_load = pltpu.make_async_copy(a_ref, a_v, a_sem)
+        a_load.start()
         fillers = attend_back_parts(*back, *back_in, *back_out, *back_scratch)
+        fillers.append(a_load.wait)
+        fillers += first_product_parts(a_v, back_out[0], q_ref, tile)
+    greet(chips, c, k)
     w_load.wait()
 
-    def compute(m, lane):
-        spans = unit_rows(chips, rows, m, lane)
+    def compute(m):
+        spans = block_rows(chips, rows, m)
         for side in range(CORES):
-            loads[m, lane, side].wait()
+            loads[m, side].wait()
         left = jnp.concatenate([h_v[span, :] for span in spans], axis=0)
-        product_terms(left, w_v, own, theirs, m, lane, transposed, tile)
+        product_terms(left, w_v, own, theirs, m, transposed, tile)
 
     exchange(chips, scratch, o_ref, compute, fillers)
+
+
+def first_product_parts(left, right, target, tile, after=None):
+    def part(i):
+        span = slice(i * tile, (i + 1) * tile)
+        target[span, :] = contract_first(left[:, span], right[...]).astype(BF16)
+        if after is not None:
+            after(i, span)
+
+    return [functools.partial(part, i) for i in range(left.shape[1] // tile)]
 
 
 def product_scatter(h, w, chips, ident, transposed, back=None):
@@ -389,11 +408,16 @@
     out_shape = [jax.ShapeDtypeStruct((rows, cols), F32)]
     back_scratch, sizes = [], None
     if back is not None:
-        proj, grads, blocks, logsums, heads, size = back
-        operands += [proj, grads, blocks[:, :, None], blocks[:, None, :], logsums]
-        in_specs += [in_vmem] * 5
+        proj, grads, blocks, logsums, heads, size, acts = back
+        operands += [proj, grads, blocks[:, :, None], blocks[:, None, :], logsums, acts]
+        in_specs += [in_vmem] * 5 + [in_place]
         out_shape.append(jax.ShapeDtypeStruct(proj.shape, BF16))
-        back_scratch = [pltpu.VMEM((blocks.shape[1], size), F32)] * 2
+        out_shape.append(jax.ShapeDtypeStruct((acts.shape[1], proj.shape[1]), BF16))
+        back_scratch = [
+            *[pltpu.VMEM((blocks.shape[1], size), F32)] * 2,
+            pltpu.VMEM(acts.shape, BF16),
+            pltpu.SemaphoreType.DMA,
+        ]
         sizes = (heads, size, 256)
     result = pl.pallas_call(
         functools.partial(product_scatter_kernel, chips, transposed, 512, sizes),
@@ -406,7 +430,7 @@
             pltpu.VMEM((cols, depth) if transposed else w.shape, BF16),
             *exchange_scratch(chips, rows, cols),
             pltpu.SemaphoreType.DMA,
-            pltpu.SemaphoreType.DMA((chips, LANES, CORES)),
+            pltpu.SemaphoreType.DMA((chips, CORES)),
             *back_scratch,
         ],
         cost_estimate=pl.CostEstimate(flops=1_000_000_000, bytes_accessed=0, transcendentals=0),
@@ -425,34 +449,32 @@
 
 
 def hidden_back_kernel(
-    chips, tile, g_ref, d_ref, p_ref, u_ref, o_ref, e_ref, g_v, p_v, e_v, d_v, u_v, *refs
+    chips, tile, g_ref, d_ref, p_ref, u_ref, a_ref, o_ref, s_ref, g_v, p_v, e_v, d_v, u_v, *refs
 ):
-    scratch, (w_sem, load_sem, store_sem) = refs[:8], refs[8:]
+    scratch, (w_sem, load_sem, a_sem, store_sem) = refs[:8], refs[8:]
     c, k = lax.axis_index("ctx"), lax.axis_index("core")
     rows = o_ref.shape[0]
-    _, _, _, units = scatter_plan(chips)
     own, theirs = scratch[:2]
     d_load = pltpu.make_async_copy(core_window(d_ref, d_v.shape[1]), d_v, w_sem.at[0])
     u_load = pltpu.make_async_copy(core_window(u_ref, u_v.shape[1]), u_v, w_sem.at[1])
     d_load.start()
     loads, stores = {}, []
-    for place, (m, lane) in enumerate(units):
+    for place, m in enumerate(block_order(chips)):
         if place == 1:
             u_load.start()
-        for side, span in enumerate(unit_rows(chips, rows, m, lane)):
+        for side, span in enumerate(block_rows(chips, rows, m)):
             for which, (source, target) in enumerate(((g_ref, g_v), (p_ref, p_v))):
                 load = pltpu.make_async_copy(
-                    source.at[span], target.at[span], load_sem.at[which, m, lane, side]
+                    source.at[span], target.at[span], load_sem.at[which, m, side]
                 )
                 load.start()
-                loads.setdefault((m, lane), []).append(load)
+                loads.setdefault(m, []).append(load)
     greet(chips, c, k)
     d_load.wait()
 
-    def compute(m, lane):
-        spans = unit_rows(chips, rows, m, lane)
-        half = rows // LANES
-        for load in loads[m, lane]:
+    def compute(m):
+        spans = block_rows(chips, rows, m)
+        for load in loads[m]:
             load.wait()
         grads = jnp.concatenate([g_v[span, :] for span in spans], axis=0)
 
@@ -461,36 +483,41 @@
             part = jnp.dot(grads, d_v[:, cols], preferred_element_type=F32)
             for side, span in enumerate(spans):
                 slope = gelu_slope(p_v[span, cols])
-                e_v[span, cols] = (part[side * half : (side + 1) * half] * slope).astype(BF16)
+                e_v[span, cols] = (part[side * rows : (side + 1) * rows] * slope).astype(BF16)
             return carry
 
         lax.fori_loop(0, e_v.shape[1] // tile, body, 0)
-        for side, span in enumerate(spans):
-            store = pltpu.make_async_copy(e_v.at[span], e_ref.at[span], store_sem.at[m, lane, side])
-            store.start()
-            stores.append(store)
-        if (m, lane) == units[0]:
+        if m == block_order(chips)[0]:
             u_load.wait()
         left = jnp.concatenate([e_v[span, :] for span in spans], axis=0)
-        product_terms(left, u_v, own, theirs, m, lane, True, 512)
-
-    exchange(chips, scratch, o_ref, compute)
-    for store in stores:
-        store.wait()
-
-
-def hidden_back(grads, w_down, pre, w_up, chips, ident):
+        product_terms(left, u_v, own, theirs, m, True, tile)
+
+    a_load = pltpu.make_async_copy(a_ref, g_v, a_sem)
+
+    def store(i, span):
+        copy = pltpu.make_async_copy(d_v.at[span], s_ref.at[span], store_sem.at[i])
+        copy.start()
+        stores.append(copy)
+
+    fillers = [a_load.start, a_load.wait, *first_product_parts(g_v, e_v, d_v, tile, store)]
+    exchange(chips, scratch, o_ref, compute, fillers)
+    for copy in stores:
+        copy.wait()
+
+
+def hidden_back(grads, w_down, pre, w_up, acts, chips, ident):
     cols, width = w_up.shape[0], pre.shape[1]
     rows = grads.shape[0] // (CORES * chips)
+    tile = 512
     in_place = pl.BlockSpec(memory_space=pl.ANY)
     return pl.pallas_call(
-        functools.partial(hidden_back_kernel, chips, 256),
+        functools.partial(hidden_back_kernel, chips, tile),
         name="hidden_back",
         out_shape=[
             jax.ShapeDtypeStruct((rows, cols), F32),
-            jax.ShapeDtypeStruct((grads.shape[0], width), BF16),
+            jax.ShapeDtypeStruct((cols, width), BF16),
         ],
-        in_specs=[in_place] * 4,
+        in_specs=[in_place] * 5,
         out_specs=[pl.BlockSpec(memory_space=pltpu.VMEM), in_place],
         scratch_shapes=[
             pltpu.VMEM(grads.shape, BF16),
@@ -500,55 +527,103 @@
             pltpu.VMEM((cols, width), BF16),
             *exchange_scratch(chips, rows, cols),
             pltpu.SemaphoreType.DMA((2,)),
-            pltpu.SemaphoreType.DMA((2, chips, LANES, CORES)),
-            pltpu.SemaphoreType.DMA((chips, LANES, CORES)),
+            pltpu.SemaphoreType.DMA((2, chips, CORES)),
+            pltpu.SemaphoreType.DMA,
+            pltpu.SemaphoreType.DMA((cols // tile,)),
         ],
         cost_estimate=pl.CostEstimate(flops=1_000_000_000, bytes_accessed=0, transcendentals=0),
         compiler_params=pltpu.CompilerParams(
             collective_id=ident, has_side_effects=True, vmem_limit_bytes=VMEM_LIMIT
         ),
-    )(grads, w_down, pre, w_up)
-
-
-def all_sum_kernel(chips, planes, x_ref, o_ref, landed, send_sem, recv_sem):
+    )(grads, w_down, pre, w_up, acts)
+
+
+def deal_kernel(chips, planes, parts, b_ref, x_ref, o_ref, t_ref, landed, heard, *sems):
+    send_sem, recv_sem, sum_send, sum_recv = sems
     c, z, k = lax.axis_index("ctx"), lax.axis_index("z"), lax.axis_index("core")
-    partners = [{"ctx": c ^ bit} for bit in chip_bits(chips)] + [{"core": 1 - k}]
-    partners += [{"z": z ^ (2 * bit - 1)} for bit in chip_bits(planes)]
+    team, count, width = landed.shape
+    peers = [{"ctx": c ^ m, "core": core} for m in range(1, chips) for core in (k, 1 - k)]
+    peers.append({"core": 1 - k})
+    lines = [{"z": z ^ mask} for mask in range(1, planes)]
+    groups = [[{"ctx": c ^ m} for m in range(1, chips)], [{"core": 1 - k}], lines]
     barrier = pltpu.get_barrier_semaphore()
-    for partner in partners:
-        pl.semaphore_signal(barrier, inc=1, device_id=partner, device_id_type=MESH)
-    o_ref[...] = x_ref[...]
-    pl.semaphore_wait(barrier, len(partners))
-    for step, partner in enumerate(partners):
+    for friend in peers + lines:
+        pl.semaphore_signal(barrier, inc=1, device_id=friend, device_id_type=MESH)
+    me = c * CORES + k
+    landed[me] = b_ref[me]
+    t_ref[...] = x_ref[...]
+    pl.semaphore_wait(barrier, len(peers) + len(lines))
+    copies = []
+    for place, peer in enumerate(peers):
+        target = peer.get("ctx", c) * CORES + peer["core"]
         copy = pltpu.make_async_remote_copy(
-            src_ref=o_ref,
-            dst_ref=landed.at[step],
-            send_sem=send_sem.at[step],
-            recv_sem=recv_sem.at[step],
-            device_id=partner,
+            src_ref=b_ref.at[target],
+            dst_ref=landed.at[me],
+            send_sem=send_sem.at[place],
+            recv_sem=recv_sem.at[place],
+            device_id=peer,
             device_id_type=MESH,
         )
-        copy.start()
+        copies.append(copy)
+    slot = 0
+    for group in groups:
+        sums = []
+        for partner in group:
+            sums.append(
+                pltpu.make_async_remote_copy(
+                    src_ref=t_ref,
+                    dst_ref=heard.at[slot],
+                    send_sem=sum_send.at[slot],
+                    recv_sem=sum_recv.at[slot],
+                    device_id=partner,
+                    device_id_type=MESH,
+                )
+            )
+            slot += 1
+        for total in sums:
+            total.start()
+        if group is groups[0]:
+            for copy in copies:
+                copy.start()
+        for total in sums:
+            total.wait()
+        for place in range(slot - len(sums), slot):
+            t_ref[...] += heard[place]
+    for copy in copies:
         copy.wait()
-        o_ref[...] += landed[step]
-
-
-def all_sum(x, chips, planes, ident):
+    piece = width // parts
+    whole = o_ref.shape[1] // parts
+    for source in range(team):
+        for part in range(parts):
+            first = part * whole + source * piece
+            o_ref[:, first : first + piece] = landed[
+                source, :, part * piece : (part + 1) * piece
+            ].astype(F32)
+
+
+def deal(blocks, parts, x, chips, planes, ident):
+    team, count, width = blocks.shape
     in_vmem = pl.BlockSpec(memory_space=pltpu.VMEM)
-    steps = len(chip_bits(chips)) + 1 + len(chip_bits(planes))
+    steps = chips - 1 + 1 + planes - 1
     return pl.pallas_call(
-        functools.partial(all_sum_kernel, chips, planes),
-        name="all_sum",
-        out_shape=jax.ShapeDtypeStruct(x.shape, x.dtype),
-        in_specs=[in_vmem],
-        out_specs=in_vmem,
+        functools.partial(deal_kernel, chips, planes, parts),
+        name="deal",
+        out_shape=[
+            jax.ShapeDtypeStruct((count, team * width), F32),
+            jax.ShapeDtypeStruct(x.shape, F32),
+        ],
+        in_specs=[in_vmem] * 2,
+        out_specs=[in_vmem] * 2,
         scratch_shapes=[
-            pltpu.VMEM((steps, *x.shape), x.dtype),
+            pltpu.VMEM(blocks.shape, BF16),
+            pltpu.VMEM((steps, *x.shape), F32),
+            pltpu.SemaphoreType.DMA((team - 1,)),
+            pltpu.SemaphoreType.DMA((team - 1,)),
             pltpu.SemaphoreType.DMA((steps,)),
             pltpu.SemaphoreType.DMA((steps,)),
         ],
         compiler_params=pltpu.CompilerParams(collective_id=ident, has_side_effects=True),
-    )(x)
+    )(blocks, x)
 
 
 def attend_kernel(heads, size, step, p_ref, key_blk, query_blk, o_ref, log_ref):
@@ -726,9 +801,9 @@
     down_part = contract_first(grads_y, hidden).astype(BF16)
     down_weights, down_part = lax.optimization_barrier((down_weights, down_part))
     down_sum = sum_planes(down_part)
-    grad_act_two, grad_pre = hidden_back(grads_y, down_weights, pre_act, up_weights, chips, 3)
-    up_part = contract_first(acts_two, grad_pre).astype(BF16)
-    grad_act_two, up_part = lax.optimization_barrier((grad_act_two, up_part))
+    grad_act_two, up_part = hidden_back(
+        grads_y, down_weights, pre_act, up_weights, acts_two, chips, 3
+    )
     up_sum = sum_planes(up_part)
     grad_res = grad_y.astype(F32) + normalize_back(grad_act_two, unit_two, inv_two, norm2_gain)
     grads_res = plane_gather(grad_res.astype(BF16), chips, 1)
@@ -737,18 +812,21 @@
     grad_attended, out_part, down_sum = lax.optimization_barrier(
         (grad_attended, out_part, down_sum)
     )
-    grad_down = whole_columns(spread_rows(down_sum), ff_cols)
+    down_parts = spread_rows(down_sum)
     out_sum = lax.psum_scatter(out_part, "z", scatter_dimension=0, tiled=True)
-    mixed_sum, grad_proj = product_scatter(
-        hidden, down_weights, chips, 5, True, back=(proj, grad_attended, blocks, logsums, heads, size)
-    )
-    proj_part = contract_first(acts_one, grad_proj).astype(BF16)
-    grad_proj, proj_part, up_sum, out_sum = lax.optimization_barrier(
-        (grad_proj, proj_part, up_sum, out_sum)
+    mixed_sum, grad_proj, proj_part = product_scatter(
+        hidden, down_weights, chips, 5, True,
+        back=(proj, grad_attended, blocks, logsums, heads, size, acts_one),
+    )
+    mixed = residual + mixed_sum
+    grad_proj, proj_part, up_sum, out_sum, down_parts, mixed = lax.optimization_barrier(
+        (grad_proj, proj_part, up_sum, out_sum, down_parts, mixed)
     )
     proj_sum = sum_planes(proj_part)
+    up_parts = spread_rows(up_sum)
+    moves = [(z * CORES + core, core * depth + z) for z in range(depth) for core in range(CORES)]
+    out_sum = lax.ppermute(out_sum, fsdp, moves)
     grad_act_one = product_scatter(grad_proj, attn_weights, chips, 4, True)
-    mixed = residual + mixed_sum
     norm_parts = jnp.stack(
         [
             jnp.sum(grad_act_one * unit_one, axis=0),
@@ -756,13 +834,14 @@
             jnp.sum(grad_act_two * unit_two, axis=0),
             jnp.sum(grad_act_two, axis=0),
         ]
-        + [jnp.zeros((model_width,), F32)] * 4
-    )
-    norm_sums = all_sum(norm_parts, chips, depth, 6)
-    grad_up = whole_columns(spread_rows(up_sum), ff_cols)
-    moves = [(z * CORES + core, core * depth + z) for z in range(depth) for core in range(CORES)]
-    grad_wout = lax.ppermute(out_sum, fsdp, moves).astype(F32)
-    grad_qkv = whole_columns(spread_rows(proj_sum), head_cols)
+    ).reshape(8, -1)
+    norm_parts, up_parts, out_sum = lax.optimization_barrier((norm_parts, up_parts, out_sum))
+    grad_down = whole_columns(down_parts, ff_cols)
+    grad_up = whole_columns(up_parts, ff_cols)
+    grad_wout = out_sum.astype(F32)
+    grad_qkv, norm_sums = deal(
+        proj_sum.reshape(team, -1, 3 * head_cols), 3, norm_parts, chips, depth, 6
+    )
     grad_inputs = grad_res + normalize_back(grad_act_one, unit_one, inv_one, norm1_gain)
     out_shape = (1, row_count, model_width)
     return (
@@ -772,7 +851,7 @@
         grad_wout,
         grad_up,
         grad_down,
-        *norm_sums[:4],
+        *norm_sums.reshape(4, model_width),
     )
 
 

time: 592 us -> 553 us (0.934)
  matrix products: 79.9 us -> 53.9 us
  waiting for transfers between devices: 29.5 us -> 15.4 us
    dot_general x4 -> x2, matrix products: 45.9 us -> 20 us  [contract_first(): lax.dot_general(left_arr, right_arr, (((0,), (0,)), ((), ())), preferred_...]
    all_to_all x3 -> x2, waiting for transfers between devices: 20.7 us -> 0.01 us  [spread_rows(): lax.all_to_all(summed, ('ctx', 'core'), split_axis=0, concat_axis=0, tile...]
    reduce_scatter x1, waiting for transfers between devices: 0.01 us -> 6.17 us  [shards(): out_sum = lax.psum_scatter(out_part, 'z', scatter_dimension=0, tiled=True)]
    all_to_all x3 -> x2, starting transfers between devices: 13.9 us -> 8.76 us  [spread_rows(): lax.all_to_all(summed, ('ctx', 'core'), split_axis=0, concat_axis=0, tile...]
  transfers between devices with their start and end apart: 12 -> 11, of which waited for: 3 -> 2; matrix products, arithmetic and copies ran while one was open for 19% -> 16% of each run, Pallas kernels for 68% -> 70%
where the time goes in v3:
time: 553 us; the launch traced here: 550 us
  Pallas kernels  407 us (74%)
  matrix products  53.9 us (10%)
  other arithmetic  24.1 us (4%)
  local copies, waits for them, and re-layouts  17.1 us (3%)
  waiting for transfers between devices  15.4 us (3%)
  starting transfers between devices  14.9 us (3%)
  between operations  14.8 us (3%)
    pallas_call x4, Pallas kernels, plane_gather(): pl.pallas_call(functools.partial(gather_kernel, chips, pieces), name='pla...  161 us
    pallas_call x3, Pallas kernels, product_scatter(): pl.pallas_call(functools.partial(product_scatter_kernel, chips, transpose...  148 us
    pallas_call x1, Pallas kernels, hidden_back(): pl.pallas_call(functools.partial(hidden_back_kernel, chips, tile), name='...  61.2 us
    dot_general x2, matrix products, contract_first(): lax.dot_general(left_arr, right_arr, (((0,), (0,)), ((), ())), preferred_...  20 us
    pallas_call x1, Pallas kernels, deal(): pl.pallas_call(functools.partial(deal_kernel, chips, planes, parts), name...  17.2 us
    pallas_call x1, Pallas kernels, attend(): pl.pallas_call(functools.partial(attend_kernel, heads, size, 256), name='...  16.2 us
    dot_general x1, matrix products, shards(): pre_act = jnp.dot(acts_two, my_up, preferred_element_type=F32)  15.7 us
    unnamed x35, local copies, waits for them, and re-layouts  11.3 us
  transfers between devices with their start and end apart: 11, of which 2 were waited for; matrix products, arithmetic and copies ran while one was open for 16% of the time, Pallas kernels for 70%

profile of v3, /device:TPU:0, one launch (start us, length us, event | category | flops | bytes accessed | tf_op | source)
XLA Modules:
  0.0 549.5 jit_solution(549845684211079733)
XLA Ops:
  7.2 3.7 pick_columns.1
  14.7 41.9 %plane_gather.4.refs_7_ = bf16[2048,2048]{1,0:T(8,128)(2,1)} custom-call(bf16[256,2048]{1,0:T(8,128)(2,1)} %fusion.20.x_ref), custom_call_target="tpu_custom_call" | custom-call | flops 1000000000 | tf_op jit(solution)/shard_map/plane_gather/pallas_call | solution.py:143
  57.3 1.9 all-gather.query_blk.refs_5_
  60.5 39.9 %plane_gather.6.g_ref = bf16[2048,2048]{1,0:T(8,128)(2,1)} custom-call(bf16[256,2048]{1,0:T(8,128)(2,1)} %bitcast.129), custom_call_target="tpu_custom_call" | custom-call | flops 1000000000 | tf_op jit(solution)/shard_map/plane_gather/pallas_call | solution.py:143
  100.5 2.3 constant_dynamic-slice_fusion
  102.8 3.6 all-to-all-start
  106.7 11.2 %convolution_convert_fusion.1.p_ref.refs_2_ = bf16[2048,768]{1,0:T(8,128)(2,1)} fusion(bf16[2048,2048]{1,0:T(8,128)(2,1)} %plane_gather.4.refs_7_, bf16[2048,2048]{1,0:T(8,128)(2,1)} %all-gather.7.cloned.1.call-done.refs_1_, s32[]{:T(128)S(6)} %select_n.22), kind=kOutput, calls=%fused_computation.13 | convolution fusion | flops 6444023808 | bytes 14680068 | tf_op jit(solution)/shard_map/dot_general | solution.py:774
  117.9 16.2 %attend.1 = (bf16[2048,256]{1,0:T(8,128)(2,1)}, f32[2,2,1024]{2,1,0:T(2,128)}) custom-call(bf16[2048,768]{1,0:T(8,128)(2,1)} %convolution_convert_fusion.1.p_ref.refs_2_, s32[2,1024,1]{2,1,0:T(8,128)} %broadcast_in_dim.42.key_blk.refs_4_, s32[2,1,1024]{2,1,0:T(1,128)} %copy-done.7), custom_call_target="tpu_custom_call" | custom-call | flops 1000000000 | tf_op jit(solution)/shard_map/attend/pallas_call | solution.py:712
  135.2 44.1 %product_scatter.3 = f32[256,2048]{1,0:T(8,128)} custom-call(bf16[2048,256]{1,0:T(8,128)(2,1)} %get-tuple-element.45.refs_0_, bf16[256,2048]{1,0:T(8,128)(2,1)} %bitcast.134), custom_call_target="tpu_custom_call" | custom-call | flops 1000000000 | tf_op jit(solution)/shard_map/product_scatter/pallas_call | solution.py:422
  179.4 1.9 fusion.33
  183.4 40.0 %plane_gather.5.a_ref = bf16[2048,2048]{1,0:T(8,128)(2,1)} custom-call(bf16[256,2048]{1,0:T(8,128)(2,1)} %add_convert_fusion.x_ref), custom_call_target="tpu_custom_call" | custom-call | flops 1000000000 | tf_op jit(solution)/shard_map/plane_gather/pallas_call | solution.py:143
  223.4 15.7 %fusion.7 = (bf16[2048,1024]{1,0:T(8,128)(2,1)S(1)}, f32[2048,1024]{1,0:T(8,128)}) fusion(bf16[2048,2048]{1,0:T(8,128)(2,1)} %plane_gather.5.a_ref, bf16[2048,2048]{1,0:T(8,128)(2,1)} %all-gather.5.cloned.1.call-done.u_ref, s32[]{:T(128)S(6)} %select_n.22), kind=kOutput, calls=%fused_computation.9 | convolution fusion | flops 8608808960 | bytes 25165828 | tf_op jit(solution)/shard_map/dot_general | solution.py:781
  239.1 1.9 copy-done.6
  241.0 12.9 %convolution_convert_fusion = bf16[2048,1024]{1,0:T(8,128)(2,1)} fusion(bf16[2048,2048]{1,0:T(8,128)(2,1)} %plane_gather.6.g_ref, bf16[2048,1024]{1,0:T(8,128)(2,1)S(1)} %get-tuple-element.88.refs_0_), kind=kOutput, calls=%fused_computation.12 | convolution fusion | flops 8592031744 | bytes 16777216 | tf_op jit(solution)/shard_map/dot_general | solution.py:49
  253.9 7.8 %all-gather.9.cloned.1.call-done.d_ref.refs_1_ = bf16[2048,2048]{1,0:T(8,128)(2,1)} async-done(((bf16[256,2048]{1,0:T(8,128)(2,1)}), bf16[2048,2048]{1,0:T(8,128)(2,1)}) %all-gather.9.cloned.1.call-update) | async-done | bytes 8388624 | tf_op jit(solution)/shard_map/all_gather | solution.py:756
  261.8 61.2 %hidden_back.1 = (f32[256,2048]{1,0:T(8,128)}, bf16[2048,1024]{1,0:T(8,128)(2,1)}) custom-call(bf16[2048,2048]{1,0:T(8,128)(2,1)} %plane_gather.6.g_ref, bf16[2048,2048]{1,0:T(8,128)(2,1)} %all-gather.9.cloned.1.call-done.d_ref.refs_1_, f32[2048,1024]{1,0:T(8,128)} %get-tuple-element.89.p_ref, bf16[2048,2048]{1,0:T(8,128)(2,1)} %all-gather.5.cloned.1.call-done.u_ref, ...), custom_call_target="tpu_custom_call" | custom-call | flops 1000000000 | tf_op jit(solution)/shard_map/hidden_back/pallas_call | solution.py:513
  323.5 2.7 multiply_reduce_fusion
  326.2 2.6 fusion.32
  328.8 39.5 %plane_gather.7 = bf16[2048,2048]{1,0:T(8,128)(2,1)} custom-call(bf16[256,2048]{1,0:T(8,128)(2,1)} %get-tuple-element.80.x_ref), custom_call_target="tpu_custom_call" | custom-call | flops 1000000000 | tf_op jit(solution)/shard_map/plane_gather/pallas_call | solution.py:143
  368.3 7.1 %convolution_convert_fusion.2 = bf16[256,2048]{1,0:T(8,128)(2,1)} fusion(bf16[2048,256]{1,0:T(8,128)(2,1)} %get-tuple-element.45.refs_0_, bf16[2048,2048]{1,0:T(8,128)(2,1)} %plane_gather.7), kind=kOutput, calls=%fused_computation.19 | convolution fusion | flops 2148007936 | bytes 10485760 | tf_op jit(solution)/shard_map/dot_general | solution.py:49
  375.4 7.1 %convolution_convert_fusion.3.refs_3_ = bf16[2048,256]{1,0:T(8,128)(2,1)} fusion(bf16[2048,2048]{1,0:T(8,128)(2,1)} %plane_gather.7, bf16[256,2048]{1,0:T(8,128)(2,1)} %bitcast.135), kind=kOutput, calls=%fused_computation.20 | convolution fusion | flops 2148007936 | bytes 10485760 | tf_op jit(solution)/shard_map/dot_general | solution.py:43
  382.5 4.3 all-to-all-start.1
  386.8 53.2 %product_scatter.4 = (f32[256,2048]{1,0:T(8,128)}, bf16[2048,768]{1,0:T(8,128)(2,1)}, bf16[2048,768]{1,0:T(8,128)(2,1)}) custom-call(bf16[2048,1024]{1,0:T(8,128)(2,1)} %copy-done.6, bf16[2048,2048]{1,0:T(8,128)(2,1)} %all-gather.9.cloned.1.call-done.d_ref.refs_1_, bf16[2048,768]{1,0:T(8,128)(2,1)} %convolution_convert_fusion.1.p_ref.refs_2_, ...), custom_call_target="tpu_custom_call" | custom-call | flops 1000000000 | tf_op jit(solution)/shard_map/product_scatter/pallas_call | solution.py:422
  440.0 3.0 add.82
  442.9 6.2 %reduce-scatter.9.cloned.1.call-done = bf16[64,2048]{1,0:T(8,128)(2,1)} async-done(((bf16[256,2048]{1,0:T(8,128)(2,1)}), bf16[64,2048]{1,0:T(8,128)(2,1)}) %reduce-scatter.9.cloned.1.call-update) | async-done | bytes 262160 | tf_op jit(solution)/shard_map/reduce_scatter | solution.py:816
  449.1 4.5 all-to-all-start.2
  453.6 50.3 %product_scatter.5 = f32[256,2048]{1,0:T(8,128)} custom-call(bf16[2048,768]{1,0:T(8,128)(2,1)} %get-tuple-element.62.refs_0_, bf16[2048,2048]{1,0:T(8,128)(2,1)} %all-gather.7.cloned.1.call-done.refs_1_), custom_call_target="tpu_custom_call" | custom-call | flops 1000000000 | tf_op jit(solution)/shard_map/product_scatter/pallas_call | solution.py:422
  504.0 2.7 fusion.26
  507.4 1.6 collective-permute-start
  509.0 3.4 fusion.28
  519.1 17.2 %deal.1 = (f32[64,6144]{1,0:T(8,128)}, f32[8,1024]{1,0:T(8,128)}) custom-call(bf16[8,64,768]{2,1,0:T(8,128)(2,1)} %bitcast.141, f32[8,1024]{1,0:T(8,128)} %reshape.159.x_ref), custom_call_target="tpu_custom_call" | custom-call | tf_op jit(solution)/shard_map/deal/pallas_call | solution.py:608
  539.7 2.7 copy.55
  (81 shorter events, 20.5 us)
Async XLA Ops:
  7.2 49.4 %copy-start = (s32[1,1024]{1,0:T(1,128)S(1)}, s32[1,1024]{1,0:T(1,128)}, u32[]{:S(2)}) copy-start(s32[1,1024]{1,0:T(1,128)} %param.13) | copy-start | bytes 12292
  7.2 93.3 %all-gather.7.cloned.1.call-start = ((), (), s32[]{:S(2)}) async-start(), calls=%async_computation.8 | async-start | bytes 9437184 | tf_op jit(solution)/shard_map/all_gather | solution.py:756
  11.0 1.5 copy-start.2
  11.0 212.4 %all-gather.5.cloned.1.call-start = ((), (), s32[]{:S(2)}) async-start(), calls=%async_computation.7 | async-start | bytes 9437184 | tf_op jit(solution)/shard_map/all_gather | solution.py:756
  11.1 2.1 copy-start.9
  11.1 2.1 copy-start.10
  11.8 249.9 %all-gather.9.cloned.1.call-start = ((), (), s32[]{:S(2)}) async-start(), calls=%async_computation.9 | async-start | bytes 9437184 | tf_op jit(solution)/shard_map/all_gather | solution.py:756
  14.6 41.9 %copy-start.12 = (s32[8]{0:T(128)S(1)}, s32[8]{0:T(128)}, u32[]{:S(2)}) copy-start(s32[8]{0:T(128)} %param.14) | copy-start | bytes 100
  59.2 41.3 %copy-start.7 = (s32[2,1,1024]{2,1,0:T(1,128)}, s32[2,1,1024]{2,1,0:T(1,128)S(1)}, u32[]{:S(2)}) copy-start(s32[2,1,1024]{2,1,0:T(1,128)S(1)} %all-gather.query_blk.refs_5_) | copy-start | bytes 24580
  102.8 31.4 %all-to-all-start = ((bf16[8,256,256]{2,1,0:T(8,128)(2,1)}), bf16[8,256,256]{2,1,0:T(8,128)(2,1)S(1)}, u32[]{:S(2)}, u32[]{:S(2)}) async-start(bf16[8,256,256]{2,1,0:T(8,128)(2,1)} %bitcast.5), calls=%async_computation | async-start | bytes 2097152 | tf_op jit(solution)/shard_map/all_to_all | solution.py:773
  106.3 276.1 %reduce-scatter.5.cloned.1.call-start = ((), (), s32[]{:S(2)}) async-start(), calls=%async_computation.10 | async-start | bytes 5242880 | tf_op jit(solution)/shard_map/reduce_scatter | solution.py:786
  181.3 0.7 copy-start.8
  181.3 0.7 copy-start.11
  239.1 1.9 copy-start.6
  261.7 181.2 %reduce-scatter.7.cloned.1.call-start = ((), (), s32[]{:S(2)}) async-start(), calls=%async_computation.11 | async-start | bytes 5242880 | tf_op jit(solution)/shard_map/reduce_scatter | solution.py:786
  323.0 126.1 %reduce-scatter.9.cloned.1.call-start = ((), (), s32[]{:S(2)}) async-start(), calls=%async_computation.12 | async-start | bytes 1310720 | tf_op jit(solution)/shard_map/reduce_scatter | solution.py:816
  323.5 2.7 copy-start.4
  323.5 2.7 copy-start.5
  382.5 60.5 %all-to-all-start.1 = ((bf16[8,64,1024]{2,1,0:T(8,128)(2,1)}), bf16[8,64,1024]{2,1,0:T(8,128)(2,1)}, u32[]{:S(2)}, u32[]{:S(2)}) async-start(bf16[8,64,1024]{2,1,0:T(8,128)(2,1)} %bitcast.140), calls=%async_computation.4 | async-start | bytes 2097152 | tf_op jit(solution)/shard_map/all_to_all | solution.py:790
  386.7 132.4 %reduce-scatter.11.cloned.1.call-start = ((), (), s32[]{:S(2)}) async-start(), calls=%async_computation.13 | async-start | bytes 3932160 | tf_op jit(solution)/shard_map/reduce_scatter | solution.py:786
  449.1 66.2 %all-to-all-start.2 = ((bf16[8,64,1024]{2,1,0:T(8,128)(2,1)}), bf16[8,64,1024]{2,1,0:T(8,128)(2,1)}, u32[]{:S(2)}, u32[]{:S(2)}) async-start(bf16[8,64,1024]{2,1,0:T(8,128)(2,1)} %bitcast.18), calls=%async_computation.6 | async-start | bytes 2097152 | tf_op jit(solution)/shard_map/all_to_all | solution.py:790
  504.0 5.0 copy-start.3
  507.4 7.9 %collective-permute-start = (bf16[64,2048]{1,0:T(8,128)(2,1)}, bf16[64,2048]{1,0:T(8,128)(2,1)S(1)}, u32[]{:S(2)}, u32[]{:S(2)}) collective-permute-start(bf16[64,2048]{1,0:T(8,128)(2,1)} %reduce-scatter.9.cloned.1.call-done), channel_id=1, source_target_pairs={{0,0},{1,4},{2,1},{3,5},{4,2},{5,6},{6,3},{7,7},{8,8},{9,12},{10,9... | collective-permute-start | bytes 786440 | tf_op jit(solution)/shard_map/ppermute | solution.py:828
  517.7 24.7 %copy-start.1 = (s32[1,1024]{1,0:T(1,128)S(1)}, s32[1,1024]{1,0:T(1,128)}, u32[]{:S(2)}) copy-start(s32[1,1024]{1,0:T(1,128)} %param.13) | copy-start | bytes 12292
Sparse Core Ops, SparseCore 0:
  11.2 84.7 all-gather.6
  98.1 80.7 all-gather.4
  181.1 80.5 all-gather.8
  263.8 75.2 reduce-scatter.4
  341.4 77.2 reduce-scatter.6
  421.5 27.6 reduce-scatter.8
  451.5 58.9 reduce-scatter.10

commit v4 on v3

--- a/solution.py
+++ b/solution.py
@@ -69,19 +69,24 @@
     pl.semaphore_wait(barrier, len(friends))
 
 
-def gather_kernel(chips, pieces, x_ref, o_ref, own_sem, send_sem, recv_sem):
+def gather_scratch(chips, pieces):
+    bits = len(chip_bits(chips))
+    return [
+        pltpu.SemaphoreType.DMA((bits + 1, chips, LANES, pieces)),
+        pltpu.SemaphoreType.DMA((2, chips, LANES, pieces)),
+    ]
+
+
+def gather(chips, pieces, sems, x_ref, o_ref, fillers=(), on_block=None):
+    send_sem, recv_sem = sems
     c, k = lax.axis_index("ctx"), lax.axis_index("core")
     rows = x_ref.shape[0]
     piece_rows = rows // (LANES * pieces)
     bits, orders = chip_bits(chips), lane_orders(chips)
+    fillers, started = list(fillers), []
 
     def place(core, chip, lane, piece):
         return pl.ds((core * chips + chip) * rows + (lane * pieces + piece) * piece_rows, piece_rows)
-
-    local = pltpu.make_async_copy(x_ref, o_ref.at[pl.ds((k * chips + c) * rows, rows)], own_sem)
-    local.start()
-    greet(chips, c, k)
-    started = []
 
     def send(source, m, lane, piece, step):
         if step < len(bits):
@@ -111,6 +116,14 @@
             device_id_type=MESH,
         ).wait_recv()
 
+    def finish(m):
+        if on_block is not None and m:
+            on_block(k, m)
+        for piece, lane in own:
+            arrived(1, m, lane, piece)
+        if on_block is not None:
+            on_block(1 - k, m)
+
     own = [(p, l) for p in range(pieces) for l in range(LANES)]
     for piece, lane in own:
         source = x_ref.at[pl.ds((lane * pieces + piece) * piece_rows, piece_rows)]
@@ -120,40 +133,105 @@
         source = x_ref.at[pl.ds((lane * pieces + piece) * piece_rows, piece_rows)]
         send(source, 0, lane, piece, len(bits))
     items = sorted(
-        (max(i for i, b in enumerate(orders[lane]) if m & b), piece, lane, m)
+        (max(i for i, b in enumerate(orders[lane]) if m & b), bin(m).count("1"), piece, lane, m)
         for m in range(1, chips)
         for piece, lane in own
     )
-    for step, piece, lane, m in items:
+    left = {m: len(own) for m in range(1, chips)}
+    if on_block is not None:
+        on_block(k, 0)
+    done = [0]
+    for count, (step, _, piece, lane, m) in enumerate(items):
+        if fillers and count % max(1, len(items) // len(fillers)) == 0:
+            fillers.pop(0)()
         arrived(0, m, lane, piece)
         source = o_ref.at[place(k, c ^ m, lane, piece)]
         for later in range(step + 1, len(bits) + 1):
             send(source, m, lane, piece, later)
-    for m in range(chips):
-        for piece, lane in own:
-            arrived(1, m, lane, piece)
+        left[m] -= 1
+        if left[m] == 0:
+            done.append(m)
+            finish(done.pop(0))
+    for filler in fillers:
+        filler()
+    for m in done:
+        finish(m)
     for copy in started:
         copy.wait_send()
+
+
+def gather_kernel(chips, pieces, x_ref, o_ref, own_sem, *sems):
+    c, k = lax.axis_index("ctx"), lax.axis_index("core")
+    rows = x_ref.shape[0]
+    local = pltpu.make_async_copy(x_ref, o_ref.at[pl.ds((k * chips + c) * rows, rows)], own_sem)
+    local.start()
+    greet(chips, c, k)
+    gather(chips, pieces, sems, x_ref, o_ref)
     local.wait()
 
 
 def plane_gather(x, chips, ident, pieces=2):
     rows, cols = x.shape
-    bits = len(chip_bits(chips))
     return pl.pallas_call(
         functools.partial(gather_kernel, chips, pieces),
         name="plane_gather",
         out_shape=jax.ShapeDtypeStruct((CORES * chips * rows, cols), x.dtype),
         in_specs=[pl.BlockSpec(memory_space=pl.ANY)],
         out_specs=pl.BlockSpec(memory_space=pl.ANY),
-        scratch_shapes=[
-            pltpu.SemaphoreType.DMA,
-            pltpu.SemaphoreType.DMA((bits + 1, chips, LANES, pieces)),
-            pltpu.SemaphoreType.DMA((2, chips, LANES, pieces)),
-        ],
+        scratch_shapes=[pltpu.SemaphoreType.DMA, *gather_scratch(chips, pieces)],
         cost_estimate=pl.CostEstimate(flops=1_000_000_000, bytes_accessed=0, transcendentals=0),
         compiler_params=pltpu.CompilerParams(collective_id=ident, has_side_effects=True),
     )(x)
+
+
+def attended_back_kernel(
+    chips, pieces, x_ref, w_ref, h_ref, g_ref, s_ref, x_v, own_sem, *sems
+):
+    c, k = lax.axis_index("ctx"), lax.axis_index("core")
+    rows = x_ref.shape[0]
+
+    def span_of(core, m):
+        return pl.ds(pl.multiple_of((core * chips + (c ^ m)) * rows, rows), rows)
+
+    local = pltpu.make_async_copy(x_ref, x_v.at[span_of(k, 0)], own_sem)
+    local.start()
+    greet(chips, c, k)
+    local.wait()
+
+    def on_block(core, m):
+        span = span_of(core, m)
+        g_ref[span, :] = contract_last(x_v[span, :], w_ref[...]).astype(BF16)
+
+    gather(chips, pieces, sems, x_ref, x_v, (), on_block)
+    tile = 512
+    for i in range(x_v.shape[1] // tile):
+        span = slice(i * tile, (i + 1) * tile)
+        s_ref[:, span] = contract_first(h_ref[...], x_v[:, span]).astype(BF16)
+
+
+def attended_back(x, w, attended, chips, ident, pieces=2):
+    rows, cols = x.shape
+    total = CORES * chips * rows
+    in_place, in_vmem = pl.BlockSpec(memory_space=pl.ANY), pl.BlockSpec(memory_space=pltpu.VMEM)
+    return pl.pallas_call(
+        functools.partial(attended_back_kernel, chips, pieces),
+        name="attended_back",
+        out_shape=[
+            jax.ShapeDtypeStruct((total, w.shape[0]), BF16),
+            jax.ShapeDtypeStruct((attended.shape[1], cols), BF16),
+        ],
+        in_specs=[in_place] + [in_vmem] * 2,
+        out_specs=[in_vmem] * 2,
+        scratch_shapes=[
+            pltpu.VMEM((total, cols), BF16),
+            pltpu.SemaphoreType.DMA,
+            *gather_scratch(chips, pieces),
+        ],
+        cost_estimate=pl.CostEstimate(flops=1_000_000_000, bytes_accessed=0, transcendentals=0),
+        compiler_params=pltpu.CompilerParams(
+            collective_id=ident, has_side_effects=True, vmem_limit_bytes=VMEM_LIMIT
+        ),
+    )(x, w, attended)
 
 
 def pick_kernel(head_cols, ff_cols, q_ref, o_ref, u_ref, d_ref, attn_ref, up_ref, down_ref, sem):
@@ -538,7 +616,7 @@
     )(grads, w_down, pre, w_up, acts)
 
 
-def deal_kernel(chips, planes, parts, b_ref, x_ref, o_ref, t_ref, landed, heard, *sems):
+def deal_kernel(chips, planes, b_ref, x_ref, landed, t_ref, heard, *sems):
     send_sem, recv_sem, sum_send, sum_recv = sems
     c, z, k = lax.axis_index("ctx"), lax.axis_index("z"), lax.axis_index("core")
     team, count, width = landed.shape
@@ -591,31 +669,54 @@
             t_ref[...] += heard[place]
     for copy in copies:
         copy.wait()
-    piece = width // parts
-    whole = o_ref.shape[1] // parts
-    for source in range(team):
-        for part in range(parts):
-            first = part * whole + source * piece
-            o_ref[:, first : first + piece] = landed[
-                source, :, part * piece : (part + 1) * piece
+
+
+def columns_kernel(counts, *refs):
+    blocks, targets = refs[: len(counts)], refs[len(counts) :]
+    source = pl.program_id(0)
+    for count, block, target in zip(counts, blocks, targets):
+        piece = block.shape[2] // count
+        whole = target.shape[1] // count
+        for part in range(count):
+            first = pl.multiple_of(part * whole + source * piece, piece) if count > 1 else 0
+            target[:, pl.ds(first, piece)] = block[
+                0, :, part * piece : (part + 1) * piece
             ].astype(F32)
 
 
-def deal(blocks, parts, x, chips, planes, ident):
+def whole_columns(arrays, counts):
+    team = arrays[0].shape[0]
+    specs = []
+    for array, count in zip(arrays, counts):
+        rows, width = array.shape[1:]
+        if count > 1:
+            specs.append(pl.BlockSpec((rows, team * width), lambda i: (0, 0)))
+        else:
+            specs.append(pl.BlockSpec((rows, width), lambda i: (0, i)))
+    return pl.pallas_call(
+        functools.partial(columns_kernel, counts),
+        name="whole_columns",
+        grid=(team,),
+        out_shape=[jax.ShapeDtypeStruct((a.shape[1], team * a.shape[2]), F32) for a in arrays],
+        in_specs=[pl.BlockSpec((1, *a.shape[1:]), lambda i: (i, 0, 0)) for a in arrays],
+        out_specs=specs,
+    )(*arrays)
+
+
+def deal(blocks, x, chips, planes, ident):
     team, count, width = blocks.shape
     in_vmem = pl.BlockSpec(memory_space=pltpu.VMEM)
     steps = chips - 1 + 1 + planes - 1
     return pl.pallas_call(
-        functools.partial(deal_kernel, chips, planes, parts),
+        functools.partial(deal_kernel, chips, planes),
         name="deal",
         out_shape=[
-            jax.ShapeDtypeStruct((count, team * width), F32),
+            jax.ShapeDtypeStruct(blocks.shape, BF16),
             jax.ShapeDtypeStruct(x.shape, F32),
         ],
         in_specs=[in_vmem] * 2,
         out_specs=[in_vmem] * 2,
         scratch_shapes=[
-            pltpu.VMEM(blocks.shape, BF16),
             pltpu.VMEM((steps, *x.shape), F32),
             pltpu.SemaphoreType.DMA((team - 1,)),
             pltpu.SemaphoreType.DMA((team - 1,)),
@@ -789,15 +890,6 @@
         summed = summed.reshape(team, -1, summed.shape[2])
         return lax.all_to_all(summed, ("ctx", "core"), split_axis=0, concat_axis=0, tiled=True)
 
-    def whole_columns(parts, width):
-        count = parts.shape[1]
-        return (
-            parts.reshape(team, count, -1, width)
-            .transpose(1, 2, 0, 3)
-            .reshape(count, -1)
-            .astype(F32)
-        )
-
     down_part = contract_first(grads_y, hidden).astype(BF16)
     down_weights, down_part = lax.optimization_barrier((down_weights, down_part))
     down_sum = sum_planes(down_part)
@@ -806,27 +898,36 @@
     )
     up_sum = sum_planes(up_part)
     grad_res = grad_y.astype(F32) + normalize_back(grad_act_two, unit_two, inv_two, norm2_gain)
-    grads_res = plane_gather(grad_res.astype(BF16), chips, 1)
-    grad_attended = contract_last(grads_res, my_out).astype(BF16)
-    out_part = contract_first(attended, grads_res).astype(BF16)
+    grad_attended, out_part = attended_back(grad_res.astype(BF16), my_out, attended, chips, 7)
     grad_attended, out_part, down_sum = lax.optimization_barrier(
         (grad_attended, out_part, down_sum)
     )
     down_parts = spread_rows(down_sum)
-    out_sum = lax.psum_scatter(out_part, "z", scatter_dimension=0, tiled=True)
     mixed_sum, grad_proj, proj_part = product_scatter(
         hidden, down_weights, chips, 5, True,
         back=(proj, grad_attended, blocks, logsums, heads, size, acts_one),
     )
+    grad_proj, proj_part, up_sum, out_part, down_parts = lax.optimization_barrier(
+        (grad_proj, proj_part, up_sum, out_part, down_parts)
+    )
+    proj_sum = sum_planes(proj_part)
+    out_part = out_part.reshape(depth // CORES, CORES, -1, model_width)
+    kept, given = [
+        lax.dynamic_index_in_dim(out_part, core, 1, keepdims=False) for core in (k, 1 - k)
+    ]
+    taken = lax.ppermute(given, "core", [(0, 1), (1, 0)])
+    up_parts = spread_rows(up_sum)
+    kept_first = k == 0
+    out_mine = jnp.concatenate(
+        [jnp.where(kept_first, kept, taken), jnp.where(kept_first, taken, kept)]
+    )
+    grad_act_one = product_scatter(grad_proj, attn_weights, chips, 4, True)
+    grad_act_one, out_mine, up_parts, proj_sum = lax.optimization_barrier(
+        (grad_act_one, out_mine, up_parts, proj_sum)
+    )
+    grad_wout = lax.psum_scatter(out_mine, "z", scatter_dimension=0, tiled=True)
+    grad_wout = grad_wout.reshape(-1, model_width).astype(F32)
     mixed = residual + mixed_sum
-    grad_proj, proj_part, up_sum, out_sum, down_parts, mixed = lax.optimization_barrier(
-        (grad_proj, proj_part, up_sum, out_sum, down_parts, mixed)
-    )
-    proj_sum = sum_planes(proj_part)
-    up_parts = spread_rows(up_sum)
-    moves = [(z * CORES + core, core * depth + z) for z in range(depth) for core in range(CORES)]
-    out_sum = lax.ppermute(out_sum, fsdp, moves)
-    grad_act_one = product_scatter(grad_proj, attn_weights, chips, 4, True)
     norm_parts = jnp.stack(
         [
             jnp.sum(grad_act_one * unit_one, axis=0),
@@ -835,13 +936,10 @@
             jnp.sum(grad_act_two, axis=0),
         ]
     ).reshape(8, -1)
-    norm_parts, up_parts, out_sum = lax.optimization_barrier((norm_parts, up_parts, out_sum))
-    grad_down = whole_columns(down_parts, ff_cols)
-    grad_up = whole_columns(up_parts, ff_cols)
-    grad_wout = out_sum.astype(F32)
-    grad_qkv, norm_sums = deal(
-        proj_sum.reshape(team, -1, 3 * head_cols), 3, norm_parts, chips, depth, 6
-    )
+    proj_parts, norm_sums = deal(
+        proj_sum.reshape(team, -1, 3 * head_cols), norm_parts, chips, depth, 6
+    )
+    grad_qkv, grad_up, grad_down = whole_columns((proj_parts, up_parts, down_parts), (3, 1, 1))
     grad_inputs = grad_res + normalize_back(grad_act_one, unit_one, inv_one, norm1_gain)
     out_shape = (1, row_count, model_width)
     return (

time: 553 us -> 539 us (0.975)
  matrix products: 53.9 us -> 40 us
  Pallas kernels: 407 us -> 420 us
    pallas_call x1 -> x3, Pallas kernels: 17.2 us -> 70 us  [the longest x1 45.6 us: attended_back(): pl.pallas_call(functools.partial(attended_back_kernel, chips, pieces), na...]
    pallas_call x4 -> x3, Pallas kernels: 161 us -> 120 us  [plane_gather(): pl.pallas_call(functools.partial(gather_kernel, chips, pieces), name='pla...]
    dot_general x1 -> x0, matrix products: 7.06 us -> none  [contract_last(): lax.dot_general(left_arr, right_arr, (((1,), (1,)), ((), ())), preferred_...]
    dot_general x2 -> x1, matrix products: 20 us -> 12.9 us  [contract_first(): lax.dot_general(left_arr, right_arr, (((0,), (0,)), ((), ())), preferred_...]
    reduce_scatter x1, waiting for transfers between devices: 6.17 us -> 0.01 us  [shards(): grad_wout = lax.psum_scatter(out_mine, 'z', scatter_dimension=0, tiled=True)]
    unnamed x35 -> x36, local copies, waits for them, and re-layouts: 11.3 us -> 5.72 us
  transfers between devices with their start and end apart: 11 -> 11, of which waited for: 2 -> 1; matrix products, arithmetic and copies ran while one was open for 16% -> 13% of each run, Pallas kernels for 70% -> 78%
where the time goes in v4:
time: 539 us; the launch traced here: 535 us
  Pallas kernels  420 us (78%)
  matrix products  40 us (7%)
  other arithmetic  22.7 us (4%)
  between operations  14.8 us (3%)
  local copies, waits for them, and re-layouts  13.5 us (3%)
  starting transfers between devices  12.6 us (2%)
  waiting for transfers between devices  10 us (2%)
    pallas_call x3, Pallas kernels, product_scatter(): pl.pallas_call(functools.partial(product_scatter_kernel, chips, transpose...  148 us
    pallas_call x3, Pallas kernels, plane_gather(): pl.pallas_call(functools.partial(gather_kernel, chips, pieces), name='pla...  120 us
    pallas_call x1, Pallas kernels, hidden_back(): pl.pallas_call(functools.partial(hidden_back_kernel, chips, tile), name='...  61.5 us
    pallas_call x1, Pallas kernels, attended_back(): pl.pallas_call(functools.partial(attended_back_kernel, chips, pieces), na...  45.6 us
    pallas_call x1, Pallas kernels, deal(): pl.pallas_call(functools.partial(deal_kernel, chips, planes), name='deal'...  17.4 us
    pallas_call x1, Pallas kernels, attend(): pl.pallas_call(functools.partial(attend_kernel, heads, size, 256), name='...  16.2 us
    dot_general x1, matrix products, shards(): pre_act = jnp.dot(acts_two, my_up, preferred_element_type=F32)  15.7 us
    dot_general x1, matrix products, contract_first(): lax.dot_general(left_arr, right_arr, (((0,), (0,)), ((), ())), preferred_...  12.9 us
  transfers between devices with their start and end apart: 11, of which 1 were waited for; matrix products, arithmetic and copies ran while one was open for 13% of the time, Pallas kernels for 78%

profile of v4, /device:TPU:0, one launch (start us, length us, event | category | flops | bytes accessed | tf_op | source)
XLA Modules:
  0.0 535.2 jit_solution(6741025322459718313)
XLA Ops:
  7.2 3.7 pick_columns.1
  13.2 1.4 fusion.20.x_ref
  14.7 41.5 %plane_gather.3.refs_7_ = bf16[2048,2048]{1,0:T(8,128)(2,1)} custom-call(bf16[256,2048]{1,0:T(8,128)(2,1)} %fusion.20.x_ref), custom_call_target="tpu_custom_call" | custom-call | flops 1000000000 | tf_op jit(solution)/shard_map/plane_gather/pallas_call | solution.py:175
  56.9 1.9 all-gather.query_blk.refs_5_
  58.8 1.3 broadcast_in_dim.42.key_blk.refs_4_
  60.1 39.6 %plane_gather.5.g_ref = bf16[2048,2048]{1,0:T(8,128)(2,1)} custom-call(bf16[256,2048]{1,0:T(8,128)(2,1)} %bitcast.103), custom_call_target="tpu_custom_call" | custom-call | flops 1000000000 | tf_op jit(solution)/shard_map/plane_gather/pallas_call | solution.py:175
  99.7 2.3 constant_dynamic-slice_fusion
  102.0 3.6 all-to-all-start
  105.9 11.4 %convolution_convert_fusion.1.p_ref.refs_2_ = bf16[2048,768]{1,0:T(8,128)(2,1)} fusion(bf16[2048,2048]{1,0:T(8,128)(2,1)} %plane_gather.3.refs_7_, bf16[2048,2048]{1,0:T(8,128)(2,1)} %all-gather.5.cloned.1.call-done.refs_1_, s32[]{:T(128)S(6)} %select_n.41), kind=kOutput, calls=%fused_computation.13 | convolution fusion | flops 6444023808 | bytes 14680068 | tf_op jit(solution)/shard_map/dot_general | solution.py:875
  117.2 16.2 %attend.1 = (bf16[2048,256]{1,0:T(8,128)(2,1)}, f32[2,2,1024]{2,1,0:T(2,128)}) custom-call(bf16[2048,768]{1,0:T(8,128)(2,1)} %convolution_convert_fusion.1.p_ref.refs_2_, s32[2,1024,1]{2,1,0:T(8,128)} %broadcast_in_dim.42.key_blk.refs_4_, s32[2,1,1024]{2,1,0:T(1,128)} %copy-done.9), custom_call_target="tpu_custom_call" | custom-call | flops 1000000000 | tf_op jit(solution)/shard_map/attend/pallas_call | solution.py:813
  134.6 44.3 %product_scatter.3 = f32[256,2048]{1,0:T(8,128)} custom-call(bf16[2048,256]{1,0:T(8,128)(2,1)} %get-tuple-element.49.refs_0_.h_ref, bf16[256,2048]{1,0:T(8,128)(2,1)} %bitcast.108), custom_call_target="tpu_custom_call" | custom-call | flops 1000000000 | tf_op jit(solution)/shard_map/product_scatter/pallas_call | solution.py:500
  178.9 1.9 fusion.34
  181.5 1.4 add_convert_fusion.1.x_ref
  183.0 39.4 %plane_gather.4.a_ref = bf16[2048,2048]{1,0:T(8,128)(2,1)} custom-call(bf16[256,2048]{1,0:T(8,128)(2,1)} %add_convert_fusion.1.x_ref), custom_call_target="tpu_custom_call" | custom-call | flops 1000000000 | tf_op jit(solution)/shard_map/plane_gather/pallas_call | solution.py:175
  222.4 15.7 %fusion.7 = (bf16[2048,1024]{1,0:T(8,128)(2,1)S(1)}, f32[2048,1024]{1,0:T(8,128)}) fusion(bf16[2048,2048]{1,0:T(8,128)(2,1)} %plane_gather.4.a_ref, bf16[2048,2048]{1,0:T(8,128)(2,1)} %all-gather.7.cloned.1.call-done.u_ref, s32[]{:T(128)S(6)} %select_n.41), kind=kOutput, calls=%fused_computation.9 | convolution fusion | flops 8608808960 | bytes 25165828 | tf_op jit(solution)/shard_map/dot_general | solution.py:882
  238.1 1.9 copy-done.7
  240.1 12.9 %convolution_convert_fusion = bf16[2048,1024]{1,0:T(8,128)(2,1)} fusion(bf16[2048,2048]{1,0:T(8,128)(2,1)} %plane_gather.5.g_ref, bf16[2048,1024]{1,0:T(8,128)(2,1)S(1)} %get-tuple-element.100.refs_0_), kind=kOutput, calls=%fused_computation.12 | convolution fusion | flops 8592031744 | bytes 16777216 | tf_op jit(solution)/shard_map/dot_general | solution.py:49
  253.0 8.5 %all-gather.9.cloned.1.call-done.d_ref.refs_1_ = bf16[2048,2048]{1,0:T(8,128)(2,1)} async-done(((bf16[256,2048]{1,0:T(8,128)(2,1)}), bf16[2048,2048]{1,0:T(8,128)(2,1)}) %all-gather.9.cloned.1.call-update) | async-done | bytes 8388624 | tf_op jit(solution)/shard_map/all_gather | solution.py:857
  261.6 61.5 %hidden_back.1 = (f32[256,2048]{1,0:T(8,128)}, bf16[2048,1024]{1,0:T(8,128)(2,1)}) custom-call(bf16[2048,2048]{1,0:T(8,128)(2,1)} %plane_gather.5.g_ref, bf16[2048,2048]{1,0:T(8,128)(2,1)} %all-gather.9.cloned.1.call-done.d_ref.refs_1_, f32[2048,1024]{1,0:T(8,128)} %get-tuple-element.101.p_ref, bf16[2048,2048]{1,0:T(8,128)(2,1)} %all-gather.7.cloned.1.call-done.u_ref, ...), custom_call_target="tpu_custom_call" | custom-call | flops 1000000000 | tf_op jit(solution)/shard_map/hidden_back/pallas_call | solution.py:591
  323.1 2.7 multiply_reduce_fusion
  325.8 2.6 fusion.33
  328.4 45.6 %attended_back.1 = (bf16[2048,256]{1,0:T(8,128)(2,1)}, bf16[256,2048]{1,0:T(8,128)(2,1)}) custom-call(bf16[256,2048]{1,0:T(8,128)(2,1)} %get-tuple-element.90.x_ref, bf16[256,2048]{1,0:T(8,128)(2,1)} %bitcast.109, bf16[2048,256]{1,0:T(8,128)(2,1)} %get-tuple-element.49.refs_0_.h_ref), custom_call_target="tpu_custom_call" | custom-call | flops 1000000000 | tf_op jit(solution)/shard_map/attended_back/pallas_call | solution.py:216
  374.1 4.3 all-to-all-start.1
  378.4 53.1 %product_scatter.4 = (f32[256,2048]{1,0:T(8,128)}, bf16[2048,768]{1,0:T(8,128)(2,1)}, bf16[2048,768]{1,0:T(8,128)(2,1)}) custom-call(bf16[2048,1024]{1,0:T(8,128)(2,1)} %copy-done.7, bf16[2048,2048]{1,0:T(8,128)(2,1)} %all-gather.9.cloned.1.call-done.d_ref.refs_1_, bf16[2048,768]{1,0:T(8,128)(2,1)} %convolution_convert_fusion.1.p_ref.refs_2_, ...), custom_call_target="tpu_custom_call" | custom-call | flops 1000000000 | tf_op jit(solution)/shard_map/product_scatter/pallas_call | solution.py:500
  431.6 1.9 dynamic-slice_bitcast_fusion
  433.4 4.3 all-to-all-start.2
  437.8 50.2 %product_scatter.5 = f32[256,2048]{1,0:T(8,128)} custom-call(bf16[2048,768]{1,0:T(8,128)(2,1)} %get-tuple-element.68.refs_0_, bf16[2048,2048]{1,0:T(8,128)(2,1)} %all-gather.5.cloned.1.call-done.refs_1_), custom_call_target="tpu_custom_call" | custom-call | flops 1000000000 | tf_op jit(solution)/shard_map/product_scatter/pallas_call | solution.py:500
  490.4 3.1 fusion.28
  495.2 17.4 %deal.1 = (bf16[8,64,768]{2,1,0:T(8,128)(2,1)}, f32[8,1024]{1,0:T(8,128)}) custom-call(bf16[8,64,768]{2,1,0:T(8,128)(2,1)} %bitcast.115, f32[8,1024]{1,0:T(8,128)} %reshape.155.x_ref), custom_call_target="tpu_custom_call" | custom-call | tf_op jit(solution)/shard_map/deal/pallas_call | solution.py:710
  515.9 7.0 %whole_columns.1 = (f32[64,6144]{1,0:T(8,128)}, f32[64,8192]{1,0:T(8,128)}, f32[64,8192]{1,0:T(8,128)}) custom-call(bf16[8,64,768]{2,1,0:T(8,128)(2,1)} %get-tuple-element.74.refs_0_, bf16[8,64,1024]{2,1,0:T(8,128)(2,1)} %all-to-all-done.2.refs_1_, bf16[8,64,1024]{2,1,0:T(8,128)(2,1)} %all-to-all-done.1.refs_2_), custom_call_target="tpu_custom_call" | custom-call | tf_op jit(solution)/shard_map/whole_columns/pallas_call | solution.py:696
  523.0 3.4 fusion.29
  526.4 1.8 bitcast_convert_fusion
  (82 shorter events, 12.5 us)
Async XLA Ops:
  7.2 49.0 %copy-start = (s32[1,1024]{1,0:T(1,128)S(1)}, s32[1,1024]{1,0:T(1,128)}, u32[]{:S(2)}) copy-start(s32[1,1024]{1,0:T(1,128)} %param.13) | copy-start | bytes 12292
  7.2 92.5 %all-gather.5.cloned.1.call-start = ((), (), s32[]{:S(2)}) async-start(), calls=%async_computation.7 | async-start | bytes 9437184 | tf_op jit(solution)/shard_map/all_gather | solution.py:857
  11.0 1.5 copy-start.2
  11.0 211.4 %all-gather.7.cloned.1.call-start = ((), (), s32[]{:S(2)}) async-start(), calls=%async_computation.8 | async-start | bytes 9437184 | tf_op jit(solution)/shard_map/all_gather | solution.py:857
  11.1 2.1 copy-start.11
  11.1 2.1 copy-start.12
  11.8 249.8 %all-gather.9.cloned.1.call-start = ((), (), s32[]{:S(2)}) async-start(), calls=%async_computation.9 | async-start | bytes 9437184 | tf_op jit(solution)/shard_map/all_gather | solution.py:857
  14.7 41.5 %copy-start.14 = (s32[8]{0:T(128)S(1)}, s32[8]{0:T(128)}, u32[]{:S(2)}) copy-start(s32[8]{0:T(128)} %param.14) | copy-start | bytes 100
  58.8 40.9 %copy-start.9 = (s32[2,1,1024]{2,1,0:T(1,128)}, s32[2,1,1024]{2,1,0:T(1,128)S(1)}, u32[]{:S(2)}) copy-start(s32[2,1,1024]{2,1,0:T(1,128)S(1)} %all-gather.query_blk.refs_5_) | copy-start | bytes 24580
  102.0 31.5 %all-to-all-start = ((bf16[8,256,256]{2,1,0:T(8,128)(2,1)}), bf16[8,256,256]{2,1,0:T(8,128)(2,1)S(1)}, u32[]{:S(2)}, u32[]{:S(2)}) async-start(bf16[8,256,256]{2,1,0:T(8,128)(2,1)} %bitcast.5), calls=%async_computation | async-start | bytes 2097152 | tf_op jit(solution)/shard_map/all_to_all | solution.py:874
  105.6 268.4 %reduce-scatter.5.cloned.1.call-start = ((), (), s32[]{:S(2)}) async-start(), calls=%async_computation.10 | async-start | bytes 5242880 | tf_op jit(solution)/shard_map/reduce_scatter | solution.py:887
  180.8 0.7 copy-start.10
  180.8 0.7 copy-start.13
  238.1 1.9 copy-start.7
  261.6 169.9 %reduce-scatter.7.cloned.1.call-start = ((), (), s32[]{:S(2)}) async-start(), calls=%async_computation.11 | async-start | bytes 5242880 | tf_op jit(solution)/shard_map/reduce_scatter | solution.py:887
  323.1 2.7 copy-start.5
  323.1 2.7 copy-start.6
  374.1 57.5 %all-to-all-start.1 = ((bf16[8,64,1024]{2,1,0:T(8,128)(2,1)}), bf16[8,64,1024]{2,1,0:T(8,128)(2,1)}, u32[]{:S(2)}, u32[]{:S(2)}) async-start(bf16[8,64,1024]{2,1,0:T(8,128)(2,1)} %bitcast.112), calls=%async_computation.3 | async-start | bytes 2097152 | tf_op jit(solution)/shard_map/all_to_all | solution.py:891
  378.3 112.0 %reduce-scatter.9.cloned.1.call-start = ((), (), s32[]{:S(2)}) async-start(), calls=%async_computation.12 | async-start | bytes 3932160 | tf_op jit(solution)/shard_map/reduce_scatter | solution.py:887
  433.4 54.6 %collective-permute-start = (bf16[2,64,2048]{2,1,0:T(8,128)(2,1)}, bf16[2,64,2048]{2,1,0:T(8,128)(2,1)}, u32[]{:S(2)}, u32[]{:S(2)}) collective-permute-start(bf16[2,64,2048]{2,1,0:T(8,128)(2,1)} %dynamic-slice_bitcast_fusion), channel_id=1, source_target_pairs={{0,1},{1,0},{2,3},{3,2},{4,5},{5,4},{6,7},{7,6},{8,9},{9,8},{10,11... | collective-permute-start | bytes 1572872 | tf_op jit(solution)/shard_map/ppermute | solution.py:918
  433.4 56.9 %all-to-all-start.2 = ((bf16[8,64,1024]{2,1,0:T(8,128)(2,1)}), bf16[8,64,1024]{2,1,0:T(8,128)(2,1)}, u32[]{:S(2)}, u32[]{:S(2)}) async-start(bf16[8,64,1024]{2,1,0:T(8,128)(2,1)} %bitcast.111), calls=%async_computation.4 | async-start | bytes 2097152 | tf_op jit(solution)/shard_map/all_to_all | solution.py:891
  437.7 88.6 %reduce-scatter.11.cloned.1.call-start = ((), (), s32[]{:S(2)}) async-start(), calls=%async_computation.13 | async-start | bytes 1310720 | tf_op jit(solution)/shard_map/reduce_scatter | solution.py:928
  437.8 50.3 %copy-start.8 = (bf16[256,2048]{1,0:T(8,128)(2,1)S(1)}, bf16[256,2048]{1,0:T(8,128)(2,1)}, u32[]{:S(2)}) copy-start(bf16[256,2048]{1,0:T(8,128)(2,1)} %get-tuple-element.69) | copy-start | bytes 3145732
  490.4 3.1 copy-start.3
  494.5 28.4 %copy-start.4 = (f32[256,2048]{1,0:T(8,128)S(1)}, f32[256,2048]{1,0:T(8,128)}, u32[]{:S(2)}) copy-start(f32[256,2048]{1,0:T(8,128)} %product_scatter.5) | copy-start | bytes 6291460
  522.9 5.2 copy-start.1
Sparse Core Ops, SparseCore 0:
  11.2 84.7 all-gather.4
  98.1 80.5 all-gather.6
  180.9 80.5 all-gather.8
  263.7 75.2 reduce-scatter.4
  341.2 77.2 reduce-scatter.6
  431.7 57.9 reduce-scatter.8
  491.9 29.2 reduce-scatter.10

commit v5 on v4

--- a/solution.py
+++ b/solution.py
@@ -234,48 +234,33 @@
     )(x, w, attended)
 
 
-def pick_kernel(head_cols, ff_cols, q_ref, o_ref, u_ref, d_ref, attn_ref, up_ref, down_ref, sem):
+def pick_kernel(pieces, *refs):
+    sources, (target, sem) = refs[:-2], refs[-2:]
     c = lax.axis_index("ctx")
-    width = o_ref.shape[1]
-    copies = []
-
-    def move(source, first, target, landing, count):
-        first = pl.multiple_of(first, 128)
+    copies, landing = [], 0
+    for place, (which, first, step, count) in enumerate(pieces):
+        first = pl.multiple_of(first + c * step, 128)
         copy = pltpu.make_async_copy(
-            source.at[:, pl.ds(first, count)],
+            sources[which].at[:, pl.ds(first, count)],
             target.at[:, pl.ds(landing, count)],
-            sem.at[len(copies)],
+            sem.at[place],
         )
         copy.start()
         copies.append(copy)
-
-    for core in range(CORES):
-        first = (c * CORES + core) * head_cols
-        for part in range(3):
-            landing = (core * 4 + part) * head_cols
-            move(q_ref, part * width + first, attn_ref, landing, head_cols)
-        move(o_ref, first, attn_ref, (core * 4 + 3) * head_cols, head_cols)
-    for source, target in ((u_ref, up_ref), (d_ref, down_ref)):
-        move(source, c * (CORES * ff_cols), target, 0, CORES * ff_cols)
+        landing += count
     for copy in copies:
         copy.wait()
 
 
-def pick_columns(w_qkv, w_out, w_up, w_down, head_cols, ff_cols):
-    rows = w_qkv.shape[0]
-    in_place = pl.BlockSpec(memory_space=pl.ANY)
-    in_vmem = pl.BlockSpec(memory_space=pltpu.VMEM)
+def pick_columns(weights, pieces):
     return pl.pallas_call(
-        functools.partial(pick_kernel, head_cols, ff_cols),
+        functools.partial(pick_kernel, pieces),
         name="pick_columns",
-        out_shape=[
-            jax.ShapeDtypeStruct((rows, CORES * count), BF16)
-            for count in (4 * head_cols, ff_cols, ff_cols)
-        ],
-        in_specs=[in_place] * 4,
-        out_specs=[in_vmem] * 3,
-        scratch_shapes=[pltpu.SemaphoreType.DMA((4 * CORES + 2,))],
-    )(w_qkv, w_out, w_up, w_down)
+        out_shape=jax.ShapeDtypeStruct((weights[0].shape[0], sum(p[3] for p in pieces)), BF16),
+        in_specs=[pl.BlockSpec(memory_space=pl.ANY)] * len(weights),
+        out_specs=pl.BlockSpec(memory_space=pltpu.VMEM),
+        scratch_shapes=[pltpu.SemaphoreType.DMA((len(pieces),))],
+    )(*weights)
 
 
 def scatter_plan(chips):
@@ -375,6 +360,8 @@
             combine(*unit)
 
     for m in block_order(chips):
+        if m == 0:
+            settle(0)
         compute(m)
         fresh = [(m, lane, share(m, lane)) for lane in range(LANES)]
         settle(0)
@@ -396,6 +383,12 @@
     return [pl.ds(pl.multiple_of(start, rows), rows) for start in starts]
 
 
+def block_place(rows, m, side=None):
+    if side is None:
+        return slice(m * CORES * rows, (m + 1) * CORES * rows)
+    return pl.ds((m * CORES + side) * rows, rows)
+
+
 def product_terms(left, w_v, own, theirs, m, transposed, tile):
     rows, cols = own.shape[1:]
 
@@ -422,16 +415,13 @@
     refs = list(refs)
     take = lambda count: [refs.pop(0) for _ in range(count)]
     h_ref, w_ref = take(2)
-    back_in = take(5) if back else None
-    a_ref = take(1)[0] if back else None
+    back_in = take(6) if back else None
     o_ref = take(1)[0]
-    back_out = take(1) if back else None
-    q_ref = take(1)[0] if back else None
+    back_out = take(2) if back else None
     h_v, w_v = take(2)
     scratch = take(8)
     w_sem, h_sem = take(2)
-    back_scratch = take(2) if back else None
-    a_v, a_sem = take(2) if back else (None, None)
+    back_scratch = take(8) if back else None
     c, k = lax.axis_index("ctx"), lax.axis_index("core")
     rows = o_ref.shape[0]
     own, theirs = scratch[:2]
@@ -443,27 +433,53 @@
     loads = {}
     for m in block_order(chips):
         for side, span in enumerate(block_rows(chips, rows, m)):
-            load = pltpu.make_async_copy(h_ref.at[span], h_v.at[span], h_sem.at[m, side])
+            load = pltpu.make_async_copy(
+                h_ref.at[span], h_v.at[block_place(rows, m, side)], h_sem.at[m, side]
+            )
             load.start()
             loads[m, side] = load
-    fillers = []
+    fillers, stores = [], []
     if back:
-        a_load = pltpu.make_async_copy(a_ref, a_v, a_sem)
-        a_load.start()
-        fillers = attend_back_parts(*back, *back_in, *back_out, *back_scratch)
-        fillers.append(a_load.wait)
-        fillers += first_product_parts(a_v, back_out[0], q_ref, tile)
+        p_ref, g_ref, key_blk, query_blk, log_ref, a_ref = back_in
+        p_v, g_v, a_v, d_v, q_v, dk, dv, back_sem = back_scratch
+        copies = [
+            pltpu.make_async_copy(source, target, back_sem.at[place])
+            for place, (source, target) in enumerate(
+                ((p_ref, p_v), (g_ref, g_v), (a_ref, a_v), (d_v, back_out[0]), (q_v, back_out[1]))
+            )
+        ]
+        stores = copies[3:]
+        for copy in copies[:3]:
+            copy.start()
+        parts = attend_back_parts(*back, p_v, g_v, key_blk, query_blk, log_ref, d_v, dk, dv)
+        products = first_product_parts(a_v, d_v, q_v, tile)
+
+        def first_part():
+            copies[0].wait()
+            copies[1].wait()
+            parts[0]()
+
+        def first_product():
+            copies[2].wait()
+            stores[0].start()
+            products[0]()
+
+        def last_product():
+            products[-1]()
+            stores[1].start()
+
+        fillers = [first_part, *parts[1:], first_product, *products[1:-1], last_product]
     greet(chips, c, k)
     w_load.wait()
 
     def compute(m):
-        spans = block_rows(chips, rows, m)
         for side in range(CORES):
             loads[m, side].wait()
-        left = jnp.concatenate([h_v[span, :] for span in spans], axis=0)
-        product_terms(left, w_v, own, theirs, m, transposed, tile)
+        product_terms(h_v[block_place(rows, m), :], w_v, own, theirs, m, transposed, tile)
 
     exchange(chips, scratch, o_ref, compute, fillers)
+    for store in stores:
+        store.wait()
 
 
 def first_product_parts(left, right, target, tile, after=None):
@@ -484,17 +500,22 @@
     in_place = pl.BlockSpec(memory_space=pl.ANY)
     operands, in_specs = [h, w], [in_place] * 2
     out_shape = [jax.ShapeDtypeStruct((rows, cols), F32)]
-    back_scratch, sizes = [], None
+    out_specs, back_scratch, sizes = [in_vmem], [], None
     if back is not None:
         proj, grads, blocks, logsums, heads, size, acts = back
         operands += [proj, grads, blocks[:, :, None], blocks[:, None, :], logsums, acts]
-        in_specs += [in_vmem] * 5 + [in_place]
+        in_specs += [in_place] * 2 + [in_vmem] * 3 + [in_place]
+        out_specs += [in_place] * 2
         out_shape.append(jax.ShapeDtypeStruct(proj.shape, BF16))
         out_shape.append(jax.ShapeDtypeStruct((acts.shape[1], proj.shape[1]), BF16))
         back_scratch = [
+            pltpu.VMEM(proj.shape, BF16),
+            pltpu.VMEM(grads.shape, BF16),
+            pltpu.VMEM(acts.shape, BF16),
+            pltpu.VMEM(proj.shape, BF16),
+            pltpu.VMEM((acts.shape[1], proj.shape[1]), BF16),
             *[pltpu.VMEM((blocks.shape[1], size), F32)] * 2,
-            pltpu.VMEM(acts.shape, BF16),
-            pltpu.SemaphoreType.DMA,
+            pltpu.SemaphoreType.DMA((5,)),
         ]
         sizes = (heads, size, 256)
     result = pl.pallas_call(
@@ -502,7 +523,7 @@
         name="product_scatter",
         out_shape=out_shape,
         in_specs=in_specs,
-        out_specs=[in_vmem] * len(out_shape),
+        out_specs=out_specs,
         scratch_shapes=[
             pltpu.VMEM(h.shape, BF16),
             pltpu.VMEM((cols, depth) if transposed else w.shape, BF16),
@@ -527,9 +548,14 @@
 
 
 def hidden_back_kernel(
-    chips, tile, g_ref, d_ref, p_ref, u_ref, a_ref, o_ref, s_ref, g_v, p_v, e_v, d_v, u_v, *refs
+    chips, tile, g_ref, d_ref, p_ref, u_ref, a_ref, y_ref, unit_ref, inv_ref, gain_ref,
+    o_ref, low_ref, sum_ref, s_ref, g_v, p_v, e_v, d_v, u_v, y_v, unit_v, *refs
 ):
     scratch, (w_sem, load_sem, a_sem, store_sem) = refs[:8], refs[8:]
+    own_loads = [
+        pltpu.make_async_copy(y_ref, y_v, w_sem.at[2]),
+        pltpu.make_async_copy(unit_ref, unit_v, w_sem.at[3]),
+    ]
     c, k = lax.axis_index("ctx"), lax.axis_index("core")
     rows = o_ref.shape[0]
     own, theirs = scratch[:2]
@@ -543,7 +569,9 @@
         for side, span in enumerate(block_rows(chips, rows, m)):
             for which, (source, target) in enumerate(((g_ref, g_v), (p_ref, p_v))):
                 load = pltpu.make_async_copy(
-                    source.at[span], target.at[span], load_sem.at[which, m, side]
+                    source.at[span],
+                    target.at[block_place(rows, m, side)],
+                    load_sem.at[which, m, side],
                 )
                 load.start()
                 loads.setdefault(m, []).append(load)
@@ -551,69 +579,97 @@
     d_load.wait()
 
     def compute(m):
-        spans = block_rows(chips, rows, m)
+        block = block_place(rows, m)
         for load in loads[m]:
             load.wait()
-        grads = jnp.concatenate([g_v[span, :] for span in spans], axis=0)
 
         def body(i, carry):
             cols = pl.ds(pl.multiple_of(i * tile, tile), tile)
-            part = jnp.dot(grads, d_v[:, cols], preferred_element_type=F32)
-            for side, span in enumerate(spans):
-                slope = gelu_slope(p_v[span, cols])
-                e_v[span, cols] = (part[side * rows : (side + 1) * rows] * slope).astype(BF16)
+            part = jnp.dot(g_v[block, :], d_v[:, cols], preferred_element_type=F32)
+            e_v[block, cols] = (part * gelu_slope(p_v[block, cols])).astype(BF16)
             return carry
 
         lax.fori_loop(0, e_v.shape[1] // tile, body, 0)
         if m == block_order(chips)[0]:
             u_load.wait()
-        left = jnp.concatenate([e_v[span, :] for span in spans], axis=0)
-        product_terms(left, u_v, own, theirs, m, True, tile)
-
-    a_load = pltpu.make_async_copy(a_ref, g_v, a_sem)
+        product_terms(e_v[block, :], u_v, own, theirs, m, True, tile)
+
+    a_loads = [
+        pltpu.make_async_copy(
+            a_ref.at[span], g_v.at[block_place(rows, m, side)], a_sem.at[m, side]
+        )
+        for m in range(chips)
+        for side, span in enumerate(block_rows(chips, rows, m))
+    ]
+
+    def load_acts():
+        for load in a_loads + own_loads:
+            load.start()
+
+    def await_acts():
+        for load in a_loads:
+            load.wait()
 
     def store(i, span):
         copy = pltpu.make_async_copy(d_v.at[span], s_ref.at[span], store_sem.at[i])
         copy.start()
         stores.append(copy)
 
-    fillers = [a_load.start, a_load.wait, *first_product_parts(g_v, e_v, d_v, tile, store)]
+    fillers = [load_acts, await_acts, *first_product_parts(g_v, e_v, d_v, tile, store)]
     exchange(chips, scratch, o_ref, compute, fillers)
+    for load in own_loads:
+        load.wait()
+    total = [jnp.zeros((1, o_ref.shape[1]), F32)] * 2
+    step = math.gcd(rows, 64)
+    for first in range(0, rows, step):
+        span = slice(first, first + step)
+        grad, unit = o_ref[span, :], unit_v[span, :]
+        total[0] += jnp.sum(grad * unit, axis=0, keepdims=True)
+        total[1] += jnp.sum(grad, axis=0, keepdims=True)
+        back = normalize_back(grad, unit, inv_ref[span, :], gain_ref[...])
+        result = y_v[span, :].astype(F32) + back
+        o_ref[span, :] = result
+        low_ref[span, :] = result.astype(BF16)
+    sum_ref[...] = jnp.concatenate(total)
     for copy in stores:
         copy.wait()
 
 
-def hidden_back(grads, w_down, pre, w_up, acts, chips, ident):
+def hidden_back(grads, w_down, pre, w_up, acts, grad_y, unit, inv, gain, chips, ident):
     cols, width = w_up.shape[0], pre.shape[1]
     rows = grads.shape[0] // (CORES * chips)
     tile = 512
-    in_place = pl.BlockSpec(memory_space=pl.ANY)
+    in_place, in_vmem = pl.BlockSpec(memory_space=pl.ANY), pl.BlockSpec(memory_space=pltpu.VMEM)
     return pl.pallas_call(
         functools.partial(hidden_back_kernel, chips, tile),
         name="hidden_back",
         out_shape=[
             jax.ShapeDtypeStruct((rows, cols), F32),
+            jax.ShapeDtypeStruct((rows, cols), BF16),
+            jax.ShapeDtypeStruct((2, cols), F32),
             jax.ShapeDtypeStruct((cols, width), BF16),
         ],
-        in_specs=[in_place] * 5,
-        out_specs=[pl.BlockSpec(memory_space=pltpu.VMEM), in_place],
+        in_specs=[in_place] * 7 + [in_vmem] * 2,
+        out_specs=[in_vmem] * 3 + [in_place],
         scratch_shapes=[
             pltpu.VMEM(grads.shape, BF16),
             pltpu.VMEM(pre.shape, pre.dtype),
             pltpu.VMEM(pre.shape, BF16),
             pltpu.VMEM((w_down.shape[0], width), BF16),
             pltpu.VMEM((cols, width), BF16),
+            pltpu.VMEM((rows, cols), BF16),
+            pltpu.VMEM((rows, cols), F32),
             *exchange_scratch(chips, rows, cols),
-            pltpu.SemaphoreType.DMA((2,)),
+            pltpu.SemaphoreType.DMA((4,)),
             pltpu.SemaphoreType.DMA((2, chips, CORES)),
-            pltpu.SemaphoreType.DMA,
+            pltpu.SemaphoreType.DMA((chips, CORES)),
             pltpu.SemaphoreType.DMA((cols // tile,)),
         ],
         cost_estimate=pl.CostEstimate(flops=1_000_000_000, bytes_accessed=0, transcendentals=0),
         compiler_params=pltpu.CompilerParams(
             collective_id=ident, has_side_effects=True, vmem_limit_bytes=VMEM_LIMIT
         ),
-    )(grads, w_down, pre, w_up, acts)
+    )(grads, w_down, pre, w_up, acts, grad_y, unit, inv, gain)
 
 
 def deal_kernel(chips, planes, b_ref, x_ref, landed, t_ref, heard, *sems):
@@ -856,15 +912,24 @@
     def across_z(w):
         return lax.all_gather(w, fsdp, axis=0, tiled=True)
 
-    attn_cols, up_cols, down_cols = pick_columns(w_qkv, w_out, w_up, w_down, head_cols, ff_cols)
-    attn_weights = across_z(attn_cols)
+    chip_heads = CORES * head_cols
+    pieces = []
+    for core in range(CORES):
+        pieces += [
+            (0, part * model_width + core * head_cols, chip_heads, head_cols) for part in range(3)
+        ]
+        pieces.append((1, core * head_cols, chip_heads, head_cols))
+    attn_weights = across_z(pick_columns((w_qkv, w_out), pieces))
     inputs = tokens.reshape(row_count, model_width).astype(F32)
     grad_y = grad_out.reshape(row_count, model_width)
     normed_one, unit_one, inv_one = normalize(inputs, norm1_gain, norm1_bias)
     acts_one = plane_gather(normed_one.astype(BF16), chips, 1)
-    acts_one, block_ids, grad_y = lax.optimization_barrier((acts_one, block_ids, grad_y))
-    up_weights = across_z(up_cols)
-    down_weights = across_z(down_cols)
+    acts_one, block_ids, grad_y, w_up, w_down = lax.optimization_barrier(
+        (acts_one, block_ids, grad_y, w_up, w_down)
+    )
+    chip_ff = [(0, 0, CORES * ff_cols, CORES * ff_cols)]
+    up_weights = across_z(pick_columns((w_up,), chip_ff))
+    down_weights = across_z(pick_columns((w_down,), chip_ff))
     blocks = stored_blocks(block_ids, piece_order, row_count // 2)
     blocks = lax.all_gather(blocks, "core", axis=0, tiled=True)
 
@@ -893,12 +958,12 @@
     down_part = contract_first(grads_y, hidden).astype(BF16)
     down_weights, down_part = lax.optimization_barrier((down_weights, down_part))
     down_sum = sum_planes(down_part)
-    grad_act_two, up_part = hidden_back(
-        grads_y, down_weights, pre_act, up_weights, acts_two, chips, 3
+    grad_res, grad_res_low, norm_two, up_part = hidden_back(
+        grads_y, down_weights, pre_act, up_weights, acts_two,
+        grad_y, unit_two, inv_two, norm2_gain[None], chips, 3,
     )
     up_sum = sum_planes(up_part)
-    grad_res = grad_y.astype(F32) + normalize_back(grad_act_two, unit_two, inv_two, norm2_gain)
-    grad_attended, out_part = attended_back(grad_res.astype(BF16), my_out, attended, chips, 7)
+    grad_attended, out_part = attended_back(grad_res_low, my_out, attended, chips, 7)
     grad_attended, out_part, down_sum = lax.optimization_barrier(
         (grad_attended, out_part, down_sum)
     )
@@ -932,8 +997,8 @@
         [
             jnp.sum(grad_act_one * unit_one, axis=0),
             jnp.sum(grad_act_one, axis=0),
-            jnp.sum(grad_act_two * unit_two, axis=0),
-            jnp.sum(grad_act_two, axis=0),
+            norm_two[0],
+            norm_two[1],
         ]
     ).reshape(8, -1)
     proj_parts, norm_sums = deal(

time: 539 us -> 530 us (0.983)
  waiting for transfers between devices: 10 us -> 4.42 us
    convert_element_type x2 -> x0, other arithmetic: 5.69 us -> none  [the longest x1 3.1 us: shards(): mixed.reshape(out_shape).astype(BF16)]
  transfers between devices with their start and end apart: 11 -> 11, of which waited for: 1 -> 1; matrix products, arithmetic and copies ran while one was open for 13% -> 13% of each run, Pallas kernels for 78% -> 80%
where the time goes in v5:
time: 530 us; the launch traced here: 526 us
  Pallas kernels  422 us (80%)
  matrix products  40 us (8%)
  other arithmetic  18.9 us (4%)
  between operations  14.8 us (3%)
  starting transfers between devices  12.6 us (2%)
  local copies, waits for them, and re-layouts  12.2 us (2%)
    pallas_call x3, Pallas kernels, product_scatter(): pl.pallas_call(functools.partial(product_scatter_kernel, chips, transpose...  147 us
    pallas_call x3, Pallas kernels, plane_gather(): pl.pallas_call(functools.partial(gather_kernel, chips, pieces), name='pla...  120 us
    pallas_call x1, Pallas kernels, hidden_back(): pl.pallas_call(functools.partial(hidden_back_kernel, chips, tile), name='...  62.1 us
    pallas_call x1, Pallas kernels, attended_back(): pl.pallas_call(functools.partial(attended_back_kernel, chips, pieces), na...  45.6 us
    pallas_call x1, Pallas kernels, deal(): pl.pallas_call(functools.partial(deal_kernel, chips, planes), name='deal'...  16.9 us
    pallas_call x1, Pallas kernels, attend(): pl.pallas_call(functools.partial(attend_kernel, heads, size, 256), name='...  16.2 us
    dot_general x1, matrix products, shards(): pre_act = jnp.dot(acts_two, my_up, preferred_element_type=F32)  15.8 us
    dot_general x1, matrix products, contract_first(): lax.dot_general(left_arr, right_arr, (((0,), (0,)), ((), ())), preferred_...  13 us
  transfers between devices with their start and end apart: 11, of which 1 were waited for; matrix products, arithmetic and copies ran while one was open for 13% of the time, Pallas kernels for 80%

profile of v5, /device:TPU:0, one launch (start us, length us, event | category | flops | bytes accessed | tf_op | source)
XLA Modules:
  0.0 526.5 jit_solution(10302745996546875662)
XLA Ops:
  7.2 2.4 pick_columns.3
  10.5 1.4 fusion.20.x_ref
  11.9 41.5 %plane_gather.3.refs_7_ = bf16[2048,2048]{1,0:T(8,128)(2,1)} custom-call(bf16[256,2048]{1,0:T(8,128)(2,1)} %fusion.20.x_ref), custom_call_target="tpu_custom_call" | custom-call | flops 1000000000 | tf_op jit(solution)/shard_map/plane_gather/pallas_call | solution.py:175
  53.4 2.2 pick_columns.4
  55.8 2.3 pick_columns.5
  58.8 1.9 all-gather.query_blk.refs_5_
  60.7 1.3 broadcast_in_dim.43.key_blk.refs_4_
  62.0 39.7 %plane_gather.5.g_ref = bf16[2048,2048]{1,0:T(8,128)(2,1)} custom-call(bf16[256,2048]{1,0:T(8,128)(2,1)} %bitcast.107), custom_call_target="tpu_custom_call" | custom-call | flops 1000000000 | tf_op jit(solution)/shard_map/plane_gather/pallas_call | solution.py:175
  101.8 2.4 constant_dynamic-slice_fusion
  104.2 3.6 all-to-all-start
  108.0 11.2 %convolution_convert_fusion.1.p_ref.refs_2_ = bf16[2048,768]{1,0:T(8,128)(2,1)} fusion(bf16[2048,2048]{1,0:T(8,128)(2,1)} %plane_gather.3.refs_7_, bf16[2048,2048]{1,0:T(8,128)(2,1)} %all-gather.5.cloned.1.call-done.refs_1_, s32[]{:T(128)S(6)} %select_n.41), kind=kOutput, calls=%fused_computation.13 | convolution fusion | flops 6444023808 | bytes 14680068 | tf_op jit(solution)/shard_map/dot_general | solution.py:940
  119.2 16.2 %attend.1 = (bf16[2048,256]{1,0:T(8,128)(2,1)}, f32[2,2,1024]{2,1,0:T(2,128)}) custom-call(bf16[2048,768]{1,0:T(8,128)(2,1)} %convolution_convert_fusion.1.p_ref.refs_2_, s32[2,1024,1]{2,1,0:T(8,128)} %broadcast_in_dim.43.key_blk.refs_4_, s32[2,1,1024]{2,1,0:T(1,128)} %copy-done.6), custom_call_target="tpu_custom_call" | custom-call | flops 1000000000 | tf_op jit(solution)/shard_map/attend/pallas_call | solution.py:869
  136.5 44.4 %product_scatter.3 = f32[256,2048]{1,0:T(8,128)} custom-call(bf16[2048,256]{1,0:T(8,128)(2,1)} %get-tuple-element.49.refs_0_.h_ref, bf16[256,2048]{1,0:T(8,128)(2,1)} %bitcast.112), custom_call_target="tpu_custom_call" | custom-call | flops 1000000000 | tf_op jit(solution)/shard_map/product_scatter/pallas_call | solution.py:521
  181.0 2.1 fusion.30
  183.8 2.2 add_convert_fusion.1
  186.0 39.1 %plane_gather.4.a_ref = bf16[2048,2048]{1,0:T(8,128)(2,1)} custom-call(bf16[256,2048]{1,0:T(8,128)(2,1)} %get-tuple-element.88.x_ref), custom_call_target="tpu_custom_call" | custom-call | flops 1000000000 | tf_op jit(solution)/shard_map/plane_gather/pallas_call | solution.py:175
  225.1 15.8 %fusion.7 = (bf16[2048,1024]{1,0:T(8,128)(2,1)S(1)}, f32[2048,1024]{1,0:T(8,128)}) fusion(bf16[2048,2048]{1,0:T(8,128)(2,1)} %plane_gather.4.a_ref, bf16[2048,2048]{1,0:T(8,128)(2,1)} %all-gather.7.cloned.1.call-done.u_ref, s32[]{:T(128)S(6)} %select_n.41), kind=kOutput, calls=%fused_computation.9 | convolution fusion | flops 8608808960 | bytes 25165828 | tf_op jit(solution)/shard_map/dot_general | solution.py:947
  241.0 1.9 copy-done.4
  242.9 13.0 %convolution_convert_fusion = bf16[2048,1024]{1,0:T(8,128)(2,1)} fusion(bf16[2048,2048]{1,0:T(8,128)(2,1)} %plane_gather.5.g_ref, bf16[2048,1024]{1,0:T(8,128)(2,1)S(1)} %get-tuple-element.98.refs_0_), kind=kOutput, calls=%fused_computation.12 | convolution fusion | flops 8592031744 | bytes 16777216 | tf_op jit(solution)/shard_map/dot_general | solution.py:49
  255.9 4.2 all-gather.9.cloned.1.call-done.d_ref.refs_1_
  261.0 62.1 %hidden_back.1 = (f32[256,2048]{1,0:T(8,128)}, bf16[256,2048]{1,0:T(8,128)(2,1)}, f32[2,2048]{1,0:T(2,128)}, bf16[2048,1024]{1,0:T(8,128)(2,1)}) custom-call(bf16[2048,2048]{1,0:T(8,128)(2,1)} %plane_gather.5.g_ref, bf16[2048,2048]{1,0:T(8,128)(2,1)} %all-gather.9.cloned.1.call-done.d_ref.refs_1_, f32[2048,1024]{1,0:T(8,128)} %get-tuple-element.99.p_ref, ...), custom_call_target="tpu_custom_call" | custom-call | flops 1000000000 | tf_op jit(solution)/shard_map/hidden_back/pallas_call | solution.py:643
  323.1 45.6 %attended_back.1 = (bf16[2048,256]{1,0:T(8,128)(2,1)}, bf16[256,2048]{1,0:T(8,128)(2,1)}) custom-call(bf16[256,2048]{1,0:T(8,128)(2,1)} %get-tuple-element.56.x_ref, bf16[256,2048]{1,0:T(8,128)(2,1)} %bitcast.113, bf16[2048,256]{1,0:T(8,128)(2,1)} %get-tuple-element.49.refs_0_.h_ref), custom_call_target="tpu_custom_call" | custom-call | flops 1000000000 | tf_op jit(solution)/shard_map/attended_back/pallas_call | solution.py:216
  368.8 4.2 all-to-all-start.1
  373.1 51.8 %product_scatter.4 = (f32[256,2048]{1,0:T(8,128)}, bf16[2048,768]{1,0:T(8,128)(2,1)}, bf16[2048,768]{1,0:T(8,128)(2,1)}) custom-call(bf16[2048,1024]{1,0:T(8,128)(2,1)} %copy-done.4, bf16[2048,2048]{1,0:T(8,128)(2,1)} %all-gather.9.cloned.1.call-done.d_ref.refs_1_, bf16[2048,768]{1,0:T(8,128)(2,1)} %convolution_convert_fusion.1.p_ref.refs_2_, ...), custom_call_target="tpu_custom_call" | custom-call | flops 1000000000 | tf_op jit(solution)/shard_map/product_scatter/pallas_call | solution.py:521
  425.0 1.9 dynamic-slice_bitcast_fusion
  426.9 4.3 all-to-all-start.2
  431.2 50.2 %product_scatter.5 = f32[256,2048]{1,0:T(8,128)} custom-call(bf16[2048,768]{1,0:T(8,128)(2,1)} %get-tuple-element.69.refs_0_, bf16[2048,2048]{1,0:T(8,128)(2,1)} %all-gather.5.cloned.1.call-done.refs_1_), custom_call_target="tpu_custom_call" | custom-call | flops 1000000000 | tf_op jit(solution)/shard_map/product_scatter/pallas_call | solution.py:521
  483.8 2.6 fusion.26
  487.0 16.9 %deal.1 = (bf16[8,64,768]{2,1,0:T(8,128)(2,1)}, f32[8,1024]{1,0:T(8,128)}) custom-call(bf16[8,64,768]{2,1,0:T(8,128)(2,1)} %bitcast.119, f32[8,1024]{1,0:T(8,128)} %reshape.160.x_ref), custom_call_target="tpu_custom_call" | custom-call | tf_op jit(solution)/shard_map/deal/pallas_call | solution.py:766
  504.0 7.0 %whole_columns.1 = (f32[64,6144]{1,0:T(8,128)}, f32[64,8192]{1,0:T(8,128)}, f32[64,8192]{1,0:T(8,128)}) custom-call(bf16[8,64,768]{2,1,0:T(8,128)(2,1)} %get-tuple-element.76.refs_0_, bf16[8,64,1024]{2,1,0:T(8,128)(2,1)} %all-to-all-done.2.refs_1_, bf16[8,64,1024]{2,1,0:T(8,128)(2,1)} %all-to-all-done.1.refs_2_), custom_call_target="tpu_custom_call" | custom-call | tf_op jit(solution)/shard_map/whole_columns/pallas_call | solution.py:752
  512.2 5.4 %fusion.29 = (bf16[1,256,2048]{2,1,0:T(8,128)(2,1)}, bf16[1,256,2048]{2,1,0:T(8,128)(2,1)}) fusion(f32[256,2048]{1,0:T(8,128)} %get-tuple-element.63, bf16[1,256,2048]{2,1,0:T(8,128)(2,1)S(1)} %copy-done.2, f32[256,2048]{1,0:T(8,128)} %product_scatter.5, f32[256]{0:T(256)S(1)} %get-tuple-element.100, f32[256]{0:T(256)S(1)} %get-tuple-element.101, ...), kind=kLoop, calls=%fused_computation.40 | loop fusion | flops 6815744 | bytes 11546624 | tf_op jit(solution)/shard_map/convert_element_type | solution.py:1012
  517.6 1.8 bitcast_convert_fusion
  (76 shorter events, 8.9 us)
Async XLA Ops:
  7.2 50.9 %copy-start = (s32[1,1024]{1,0:T(1,128)S(1)}, s32[1,1024]{1,0:T(1,128)}, u32[]{:S(2)}) copy-start(s32[1,1024]{1,0:T(1,128)} %param.13) | copy-start | bytes 12292
  7.2 2.6 copy-start.2
  7.2 94.6 %all-gather.5.cloned.1.call-start = ((), (), s32[]{:S(2)}) async-start(), calls=%async_computation.7 | async-start | bytes 9437184 | tf_op jit(solution)/shard_map/all_gather | solution.py:913
  9.7 0.8 copy-start.7
  9.7 0.8 copy-start.11
  9.7 215.4 %all-gather.7.cloned.1.call-start = ((), (), s32[]{:S(2)}) async-start(), calls=%async_computation.8 | async-start | bytes 9437184 | tf_op jit(solution)/shard_map/all_gather | solution.py:913
  55.7 2.4 copy-start.13
  55.7 204.4 %all-gather.9.cloned.1.call-start = ((), (), s32[]{:S(2)}) async-start(), calls=%async_computation.9 | async-start | bytes 9437184 | tf_op jit(solution)/shard_map/all_gather | solution.py:913
  60.7 41.1 %copy-start.6 = (s32[2,1,1024]{2,1,0:T(1,128)}, s32[2,1,1024]{2,1,0:T(1,128)S(1)}, u32[]{:S(2)}) copy-start(s32[2,1,1024]{2,1,0:T(1,128)S(1)} %all-gather.query_blk.refs_5_) | copy-start | bytes 24580
  104.2 31.2 %all-to-all-start = ((bf16[8,256,256]{2,1,0:T(8,128)(2,1)}), bf16[8,256,256]{2,1,0:T(8,128)(2,1)S(1)}, u32[]{:S(2)}, u32[]{:S(2)}) async-start(bf16[8,256,256]{2,1,0:T(8,128)(2,1)} %bitcast.5), calls=%async_computation | async-start | bytes 2097152 | tf_op jit(solution)/shard_map/all_to_all | solution.py:939
  107.7 261.0 %reduce-scatter.5.cloned.1.call-start = ((), (), s32[]{:S(2)}) async-start(), calls=%async_computation.10 | async-start | bytes 5242880 | tf_op jit(solution)/shard_map/reduce_scatter | solution.py:952
  181.0 2.2 copy-start.3
  183.0 0.7 copy-start.8
  183.0 0.7 copy-start.12
  241.0 1.9 copy-start.4
  260.1 164.8 %reduce-scatter.7.cloned.1.call-start = ((), (), s32[]{:S(2)}) async-start(), calls=%async_computation.11 | async-start | bytes 5242880 | tf_op jit(solution)/shard_map/reduce_scatter | solution.py:952
  368.8 56.2 %all-to-all-start.1 = ((bf16[8,64,1024]{2,1,0:T(8,128)(2,1)}), bf16[8,64,1024]{2,1,0:T(8,128)(2,1)}, u32[]{:S(2)}, u32[]{:S(2)}) async-start(bf16[8,64,1024]{2,1,0:T(8,128)(2,1)} %bitcast.116), calls=%async_computation.3 | async-start | bytes 2097152 | tf_op jit(solution)/shard_map/all_to_all | solution.py:956
  373.0 110.7 %reduce-scatter.9.cloned.1.call-start = ((), (), s32[]{:S(2)}) async-start(), calls=%async_computation.12 | async-start | bytes 3932160 | tf_op jit(solution)/shard_map/reduce_scatter | solution.py:952
  426.9 54.6 %collective-permute-start = (bf16[2,64,2048]{2,1,0:T(8,128)(2,1)}, bf16[2,64,2048]{2,1,0:T(8,128)(2,1)}, u32[]{:S(2)}, u32[]{:S(2)}) collective-permute-start(bf16[2,64,2048]{2,1,0:T(8,128)(2,1)} %dynamic-slice_bitcast_fusion), channel_id=1, source_target_pairs={{0,1},{1,0},{2,3},{3,2},{4,5},{5,4},{6,7},{7,6},{8,9},{9,8},{10,11... | collective-permute-start | bytes 1572872 | tf_op jit(solution)/shard_map/ppermute | solution.py:983
  426.9 56.9 %all-to-all-start.2 = ((bf16[8,64,1024]{2,1,0:T(8,128)(2,1)}), bf16[8,64,1024]{2,1,0:T(8,128)(2,1)}, u32[]{:S(2)}, u32[]{:S(2)}) async-start(bf16[8,64,1024]{2,1,0:T(8,128)(2,1)} %bitcast.115), calls=%async_computation.4 | async-start | bytes 2097152 | tf_op jit(solution)/shard_map/all_to_all | solution.py:956
  431.2 86.5 %reduce-scatter.11.cloned.1.call-start = ((), (), s32[]{:S(2)}) async-start(), calls=%async_computation.13 | async-start | bytes 1310720 | tf_op jit(solution)/shard_map/reduce_scatter | solution.py:993
  431.2 50.3 %copy-start.5 = (bf16[256,2048]{1,0:T(8,128)(2,1)S(1)}, bf16[256,2048]{1,0:T(8,128)(2,1)}, u32[]{:S(2)}) copy-start(bf16[256,2048]{1,0:T(8,128)(2,1)} %get-tuple-element.70) | copy-start | bytes 3145732
  483.7 2.6 copy-start.10
  504.0 7.0 %copy-start.9 = (f32[8,1024]{1,0:T(8,128)S(1)}, f32[8,1024]{1,0:T(8,128)}, u32[]{:S(2)}) copy-start(f32[8,1024]{1,0:T(8,128)} %get-tuple-element.83) | copy-start | bytes 98308
  512.2 7.2 %copy-start.1 = (s32[1,1024]{1,0:T(1,128)S(1)}, s32[1,1024]{1,0:T(1,128)}, u32[]{:S(2)}) copy-start(s32[1,1024]{1,0:T(1,128)} %param.13) | copy-start | bytes 12292
Sparse Core Ops, SparseCore 0:
  10.2 84.7 all-gather.4
  96.6 80.6 all-gather.6
  179.5 80.5 all-gather.8
  262.3 75.2 reduce-scatter.4
  339.8 77.2 reduce-scatter.6
  425.1 57.4 reduce-scatter.8
  484.9 29.2 reduce-scatter.10

commit v6 on v5

--- a/solution.py
+++ b/solution.py
@@ -548,14 +548,11 @@
 
 
 def hidden_back_kernel(
-    chips, tile, g_ref, d_ref, p_ref, u_ref, a_ref, y_ref, unit_ref, inv_ref, gain_ref,
-    o_ref, low_ref, sum_ref, s_ref, g_v, p_v, e_v, d_v, u_v, y_v, unit_v, *refs
+    chips, tile, g_ref, d_ref, p_ref, u_ref, a_ref, unit_ref, inv_ref, gain_ref,
+    o_ref, low_ref, sum_ref, s_ref, g_v, p_v, e_v, d_v, u_v, a_v, unit_v, *refs
 ):
     scratch, (w_sem, load_sem, a_sem, store_sem) = refs[:8], refs[8:]
-    own_loads = [
-        pltpu.make_async_copy(y_ref, y_v, w_sem.at[2]),
-        pltpu.make_async_copy(unit_ref, unit_v, w_sem.at[3]),
-    ]
+    unit_load = pltpu.make_async_copy(unit_ref, unit_v, w_sem.at[2])
     c, k = lax.axis_index("ctx"), lax.axis_index("core")
     rows = o_ref.shape[0]
     own, theirs = scratch[:2]
@@ -586,7 +583,7 @@
         def body(i, carry):
             cols = pl.ds(pl.multiple_of(i * tile, tile), tile)
             part = jnp.dot(g_v[block, :], d_v[:, cols], preferred_element_type=F32)
-            e_v[block, cols] = (part * gelu_slope(p_v[block, cols])).astype(BF16)
+            e_v[block, cols] = (part * gelu_slope(p_v[block, cols].astype(F32))).astype(BF16)
             return carry
 
         lax.fori_loop(0, e_v.shape[1] // tile, body, 0)
@@ -596,15 +593,14 @@
 
     a_loads = [
         pltpu.make_async_copy(
-            a_ref.at[span], g_v.at[block_place(rows, m, side)], a_sem.at[m, side]
+            a_ref.at[span], a_v.at[block_place(rows, m, side)], a_sem.at[m, side]
         )
         for m in range(chips)
         for side, span in enumerate(block_rows(chips, rows, m))
     ]
 
-    def load_acts():
-        for load in a_loads + own_loads:
-            load.start()
+    for load in a_loads + [unit_load]:
+        load.start()
 
     def await_acts():
         for load in a_loads:
@@ -615,10 +611,10 @@
         copy.start()
         stores.append(copy)
 
-    fillers = [load_acts, await_acts, *first_product_parts(g_v, e_v, d_v, tile, store)]
+    fillers = [await_acts, *first_product_parts(a_v, e_v, d_v, tile, store)]
     exchange(chips, scratch, o_ref, compute, fillers)
-    for load in own_loads:
-        load.wait()
+    unit_load.wait()
+    mine = block_place(rows, 0, 0).start
     total = [jnp.zeros((1, o_ref.shape[1]), F32)] * 2
     step = math.gcd(rows, 64)
     for first in range(0, rows, step):
@@ -627,7 +623,7 @@
         total[0] += jnp.sum(grad * unit, axis=0, keepdims=True)
         total[1] += jnp.sum(grad, axis=0, keepdims=True)
         back = normalize_back(grad, unit, inv_ref[span, :], gain_ref[...])
-        result = y_v[span, :].astype(F32) + back
+        result = g_v[pl.ds(mine + first, step), :].astype(F32) + back
         o_ref[span, :] = result
         low_ref[span, :] = result.astype(BF16)
     sum_ref[...] = jnp.concatenate(total)
@@ -635,7 +631,7 @@
         copy.wait()
 
 
-def hidden_back(grads, w_down, pre, w_up, acts, grad_y, unit, inv, gain, chips, ident):
+def hidden_back(grads, w_down, pre, w_up, acts, unit, inv, gain, chips, ident):
     cols, width = w_up.shape[0], pre.shape[1]
     rows = grads.shape[0] // (CORES * chips)
     tile = 512
@@ -649,7 +645,7 @@
             jax.ShapeDtypeStruct((2, cols), F32),
             jax.ShapeDtypeStruct((cols, width), BF16),
         ],
-        in_specs=[in_place] * 7 + [in_vmem] * 2,
+        in_specs=[in_place] * 6 + [in_vmem] * 2,
         out_specs=[in_vmem] * 3 + [in_place],
         scratch_shapes=[
             pltpu.VMEM(grads.shape, BF16),
@@ -657,10 +653,10 @@
             pltpu.VMEM(pre.shape, BF16),
             pltpu.VMEM((w_down.shape[0], width), BF16),
             pltpu.VMEM((cols, width), BF16),
-            pltpu.VMEM((rows, cols), BF16),
+            pltpu.VMEM(acts.shape, BF16),
             pltpu.VMEM((rows, cols), F32),
             *exchange_scratch(chips, rows, cols),
-            pltpu.SemaphoreType.DMA((4,)),
+            pltpu.SemaphoreType.DMA((3,)),
             pltpu.SemaphoreType.DMA((2, chips, CORES)),
             pltpu.SemaphoreType.DMA((chips, CORES)),
             pltpu.SemaphoreType.DMA((cols // tile,)),
@@ -669,7 +665,7 @@
         compiler_params=pltpu.CompilerParams(
             collective_id=ident, has_side_effects=True, vmem_limit_bytes=VMEM_LIMIT
         ),
-    )(grads, w_down, pre, w_up, acts, grad_y, unit, inv, gain)
+    )(grads, w_down, pre, w_up, acts, unit, inv, gain)
 
 
 def deal_kernel(chips, planes, b_ref, x_ref, landed, t_ref, heard, *sems):
@@ -959,8 +955,8 @@
     down_weights, down_part = lax.optimization_barrier((down_weights, down_part))
     down_sum = sum_planes(down_part)
     grad_res, grad_res_low, norm_two, up_part = hidden_back(
-        grads_y, down_weights, pre_act, up_weights, acts_two,
-        grad_y, unit_two, inv_two, norm2_gain[None], chips, 3,
+        grads_y, down_weights, pre_act.astype(BF16), up_weights, acts_two,
+        unit_two, inv_two, norm2_gain[None], chips, 3,
     )
     up_sum = sum_planes(up_part)
     grad_attended, out_part = attended_back(grad_res_low, my_out, attended, chips, 7)

time: 530 us -> 528 us (level)
  no operation moved by 1% of the time
where the time goes in v6:
time: 528 us; the launch traced here: 525 us
  Pallas kernels  420 us (80%)
  matrix products  39.6 us (8%)
  other arithmetic  18.8 us (4%)
  between operations  14.8 us (3%)
  starting transfers between devices  12.6 us (2%)
  local copies, waits for them, and re-layouts  12.3 us (2%)
    pallas_call x3, Pallas kernels, product_scatter(): pl.pallas_call(functools.partial(product_scatter_kernel, chips, transpose...  146 us
    pallas_call x3, Pallas kernels, plane_gather(): pl.pallas_call(functools.partial(gather_kernel, chips, pieces), name='pla...  120 us
    pallas_call x1, Pallas kernels, hidden_back(): pl.pallas_call(functools.partial(hidden_back_kernel, chips, tile), name='...  60.7 us
    pallas_call x1, Pallas kernels, attended_back(): pl.pallas_call(functools.partial(attended_back_kernel, chips, pieces), na...  45.7 us
    pallas_call x1, Pallas kernels, deal(): pl.pallas_call(functools.partial(deal_kernel, chips, planes), name='deal'...  17 us
    pallas_call x1, Pallas kernels, attend(): pl.pallas_call(functools.partial(attend_kernel, heads, size, 256), name='...  16.2 us
    dot_general x1, matrix products, shards(): pre_act = jnp.dot(acts_two, my_up, preferred_element_type=F32)  15.4 us
    dot_general x1, matrix products, contract_first(): lax.dot_general(left_arr, right_arr, (((0,), (0,)), ((), ())), preferred_...  12.9 us
  transfers between devices with their start and end apart: 11, of which 1 were waited for; matrix products, arithmetic and copies ran while one was open for 13% of the time, Pallas kernels for 80%

profile of v6, /device:TPU:0, one launch (start us, length us, event | category | flops | bytes accessed | tf_op | source)
XLA Modules:
  0.0 524.9 jit_solution(8477030067172654785)
XLA Ops:
  7.2 2.4 pick_columns.3
  10.5 1.4 fusion.20.x_ref
  11.9 41.5 %plane_gather.3.refs_7_ = bf16[2048,2048]{1,0:T(8,128)(2,1)} custom-call(bf16[256,2048]{1,0:T(8,128)(2,1)} %fusion.20.x_ref), custom_call_target="tpu_custom_call" | custom-call | flops 1000000000 | tf_op jit(solution)/shard_map/plane_gather/pallas_call | solution.py:175
  53.4 2.2 pick_columns.4
  55.8 2.3 pick_columns.5
  58.8 1.9 all-gather.query_blk.refs_5_
  60.7 1.3 broadcast_in_dim.43.key_blk.refs_4_
  62.0 39.7 %plane_gather.5.g_ref = bf16[2048,2048]{1,0:T(8,128)(2,1)} custom-call(bf16[256,2048]{1,0:T(8,128)(2,1)} %bitcast.113), custom_call_target="tpu_custom_call" | custom-call | flops 1000000000 | tf_op jit(solution)/shard_map/plane_gather/pallas_call | solution.py:175
  101.8 2.4 constant_dynamic-slice_fusion
  104.2 3.6 all-to-all-start
  108.0 11.2 %convolution_convert_fusion.1.p_ref.refs_2_ = bf16[2048,768]{1,0:T(8,128)(2,1)} fusion(bf16[2048,2048]{1,0:T(8,128)(2,1)} %plane_gather.3.refs_7_, bf16[2048,2048]{1,0:T(8,128)(2,1)} %all-gather.5.cloned.1.call-done.refs_1_, s32[]{:T(128)S(6)} %select_n.41), kind=kOutput, calls=%fused_computation.13 | convolution fusion | flops 6444023808 | bytes 14680068 | tf_op jit(solution)/shard_map/dot_general | solution.py:936
  119.2 16.2 %attend.1 = (bf16[2048,256]{1,0:T(8,128)(2,1)}, f32[2,2,1024]{2,1,0:T(2,128)}) custom-call(bf16[2048,768]{1,0:T(8,128)(2,1)} %convolution_convert_fusion.1.p_ref.refs_2_, s32[2,1024,1]{2,1,0:T(8,128)} %broadcast_in_dim.43.key_blk.refs_4_, s32[2,1,1024]{2,1,0:T(1,128)} %copy-done.6), custom_call_target="tpu_custom_call" | custom-call | flops 1000000000 | tf_op jit(solution)/shard_map/attend/pallas_call | solution.py:865
  136.6 44.4 %product_scatter.3 = f32[256,2048]{1,0:T(8,128)} custom-call(bf16[2048,256]{1,0:T(8,128)(2,1)} %get-tuple-element.49.refs_0_.h_ref, bf16[256,2048]{1,0:T(8,128)(2,1)} %bitcast.110), custom_call_target="tpu_custom_call" | custom-call | flops 1000000000 | tf_op jit(solution)/shard_map/product_scatter/pallas_call | solution.py:521
  181.0 2.1 fusion.30
  183.8 2.2 add_convert_fusion.1
  186.0 39.1 %plane_gather.4.a_ref = bf16[2048,2048]{1,0:T(8,128)(2,1)} custom-call(bf16[256,2048]{1,0:T(8,128)(2,1)} %get-tuple-element.88.x_ref), custom_call_target="tpu_custom_call" | custom-call | flops 1000000000 | tf_op jit(solution)/shard_map/plane_gather/pallas_call | solution.py:175
  225.2 15.4 %fusion.34 = (bf16[2048,1024]{1,0:T(8,128)(2,1)}, bf16[2048,1024]{1,0:T(8,128)(2,1)S(1)}) fusion(bf16[2048,2048]{1,0:T(8,128)(2,1)} %plane_gather.4.a_ref, bf16[2048,2048]{1,0:T(8,128)(2,1)} %all-gather.7.cloned.1.call-done.u_ref, s32[]{:T(128)S(6)} %select_n.41), kind=kOutput, calls=%fused_computation.71 | convolution fusion | flops 8610906112 | bytes 20971524 | tf_op jit(solution)/shard_map/dot_general | solution.py:943
  240.6 2.1 copy-done.4
  242.6 12.9 %convolution_convert_fusion = bf16[2048,1024]{1,0:T(8,128)(2,1)} fusion(bf16[2048,2048]{1,0:T(8,128)(2,1)} %plane_gather.5.g_ref, bf16[2048,1024]{1,0:T(8,128)(2,1)S(1)} %get-tuple-element.91.refs_0_), kind=kOutput, calls=%fused_computation.12 | convolution fusion | flops 8592031744 | bytes 16777216 | tf_op jit(solution)/shard_map/dot_general | solution.py:49
  255.6 4.5 all-gather.9.cloned.1.call-done.d_ref.refs_1_
  261.0 60.7 %hidden_back.1 = (f32[256,2048]{1,0:T(8,128)}, bf16[256,2048]{1,0:T(8,128)(2,1)}, f32[2,2048]{1,0:T(2,128)}, bf16[2048,1024]{1,0:T(8,128)(2,1)}) custom-call(bf16[2048,2048]{1,0:T(8,128)(2,1)} %plane_gather.5.g_ref, bf16[2048,2048]{1,0:T(8,128)(2,1)} %all-gather.9.cloned.1.call-done.d_ref.refs_1_, bf16[2048,1024]{1,0:T(8,128)(2,1)} %get-tuple-element.90.p_ref, ...), custom_call_target="tpu_custom_call" | custom-call | flops 1000000000 | tf_op jit(solution)/shard_map/hidden_back/pallas_call | solution.py:639
  321.7 45.7 %attended_back.1 = (bf16[2048,256]{1,0:T(8,128)(2,1)}, bf16[256,2048]{1,0:T(8,128)(2,1)}) custom-call(bf16[256,2048]{1,0:T(8,128)(2,1)} %get-tuple-element.56.x_ref, bf16[256,2048]{1,0:T(8,128)(2,1)} %bitcast.111, bf16[2048,256]{1,0:T(8,128)(2,1)} %get-tuple-element.49.refs_0_.h_ref), custom_call_target="tpu_custom_call" | custom-call | flops 1000000000 | tf_op jit(solution)/shard_map/attended_back/pallas_call | solution.py:216
  367.4 4.3 all-to-all-start.1
  371.7 51.7 %product_scatter.4 = (f32[256,2048]{1,0:T(8,128)}, bf16[2048,768]{1,0:T(8,128)(2,1)}, bf16[2048,768]{1,0:T(8,128)(2,1)}) custom-call(bf16[2048,1024]{1,0:T(8,128)(2,1)} %copy-done.4, bf16[2048,2048]{1,0:T(8,128)(2,1)} %all-gather.9.cloned.1.call-done.d_ref.refs_1_, bf16[2048,768]{1,0:T(8,128)(2,1)} %convolution_convert_fusion.1.p_ref.refs_2_, ...), custom_call_target="tpu_custom_call" | custom-call | flops 1000000000 | tf_op jit(solution)/shard_map/product_scatter/pallas_call | solution.py:521
  423.4 1.9 dynamic-slice_bitcast_fusion
  425.3 4.3 all-to-all-start.2
  429.7 50.2 %product_scatter.5 = f32[256,2048]{1,0:T(8,128)} custom-call(bf16[2048,768]{1,0:T(8,128)(2,1)} %get-tuple-element.69.refs_0_, bf16[2048,2048]{1,0:T(8,128)(2,1)} %all-gather.5.cloned.1.call-done.refs_1_), custom_call_target="tpu_custom_call" | custom-call | flops 1000000000 | tf_op jit(solution)/shard_map/product_scatter/pallas_call | solution.py:521
  482.2 2.6 fusion.26
  485.5 17.0 %deal.1 = (bf16[8,64,768]{2,1,0:T(8,128)(2,1)}, f32[8,1024]{1,0:T(8,128)}) custom-call(bf16[8,64,768]{2,1,0:T(8,128)(2,1)} %bitcast.118, f32[8,1024]{1,0:T(8,128)} %reshape.160.x_ref), custom_call_target="tpu_custom_call" | custom-call | tf_op jit(solution)/shard_map/deal/pallas_call | solution.py:762
  502.5 7.0 %whole_columns.1 = (f32[64,6144]{1,0:T(8,128)}, f32[64,8192]{1,0:T(8,128)}, f32[64,8192]{1,0:T(8,128)}) custom-call(bf16[8,64,768]{2,1,0:T(8,128)(2,1)} %get-tuple-element.76.refs_0_, bf16[8,64,1024]{2,1,0:T(8,128)(2,1)} %all-to-all-done.2.refs_1_, bf16[8,64,1024]{2,1,0:T(8,128)(2,1)} %all-to-all-done.1.refs_2_), custom_call_target="tpu_custom_call" | custom-call | tf_op jit(solution)/shard_map/whole_columns/pallas_call | solution.py:748
  510.7 5.3 %fusion.29 = (bf16[1,256,2048]{2,1,0:T(8,128)(2,1)}, bf16[1,256,2048]{2,1,0:T(8,128)(2,1)}) fusion(f32[256,2048]{1,0:T(8,128)} %get-tuple-element.63, bf16[1,256,2048]{2,1,0:T(8,128)(2,1)S(1)} %copy-done.2, f32[256,2048]{1,0:T(8,128)} %product_scatter.5, f32[256]{0:T(256)S(1)} %get-tuple-element.100, f32[256]{0:T(256)S(1)} %get-tuple-element.101, ...), kind=kLoop, calls=%fused_computation.40 | loop fusion | flops 6815744 | bytes 11546624 | tf_op jit(solution)/shard_map/convert_element_type | solution.py:1008
  516.0 1.8 bitcast_convert_fusion
  (76 shorter events, 8.9 us)
Async XLA Ops:
  7.2 50.9 %copy-start = (s32[1,1024]{1,0:T(1,128)S(1)}, s32[1,1024]{1,0:T(1,128)}, u32[]{:S(2)}) copy-start(s32[1,1024]{1,0:T(1,128)} %param.13) | copy-start | bytes 12292
  7.2 2.6 copy-start.2
  7.2 94.6 %all-gather.5.cloned.1.call-start = ((), (), s32[]{:S(2)}) async-start(), calls=%async_computation.7 | async-start | bytes 9437184 | tf_op jit(solution)/shard_map/all_gather | solution.py:909
  9.7 0.8 copy-start.7
  9.7 0.8 copy-start.11
  9.7 215.4 %all-gather.7.cloned.1.call-start = ((), (), s32[]{:S(2)}) async-start(), calls=%async_computation.8 | async-start | bytes 9437184 | tf_op jit(solution)/shard_map/all_gather | solution.py:909
  55.7 2.4 copy-start.13
  55.7 204.4 %all-gather.9.cloned.1.call-start = ((), (), s32[]{:S(2)}) async-start(), calls=%async_computation.9 | async-start | bytes 9437184 | tf_op jit(solution)/shard_map/all_gather | solution.py:909
  60.7 41.1 %copy-start.6 = (s32[2,1,1024]{2,1,0:T(1,128)}, s32[2,1,1024]{2,1,0:T(1,128)S(1)}, u32[]{:S(2)}) copy-start(s32[2,1,1024]{2,1,0:T(1,128)S(1)} %all-gather.query_blk.refs_5_) | copy-start | bytes 24580
  104.2 31.3 %all-to-all-start = ((bf16[8,256,256]{2,1,0:T(8,128)(2,1)}), bf16[8,256,256]{2,1,0:T(8,128)(2,1)S(1)}, u32[]{:S(2)}, u32[]{:S(2)}) async-start(bf16[8,256,256]{2,1,0:T(8,128)(2,1)} %bitcast.5), calls=%async_computation | async-start | bytes 2097152 | tf_op jit(solution)/shard_map/all_to_all | solution.py:935
  107.7 259.6 %reduce-scatter.5.cloned.1.call-start = ((), (), s32[]{:S(2)}) async-start(), calls=%async_computation.10 | async-start | bytes 5242880 | tf_op jit(solution)/shard_map/reduce_scatter | solution.py:948
  181.0 2.2 copy-start.3
  183.0 0.7 copy-start.9
  183.0 0.7 copy-start.12
  240.6 2.1 copy-start.4
  260.1 163.3 %reduce-scatter.7.cloned.1.call-start = ((), (), s32[]{:S(2)}) async-start(), calls=%async_computation.11 | async-start | bytes 5242880 | tf_op jit(solution)/shard_map/reduce_scatter | solution.py:948
  367.4 56.0 %all-to-all-start.1 = ((bf16[8,64,1024]{2,1,0:T(8,128)(2,1)}), bf16[8,64,1024]{2,1,0:T(8,128)(2,1)}, u32[]{:S(2)}, u32[]{:S(2)}) async-start(bf16[8,64,1024]{2,1,0:T(8,128)(2,1)} %bitcast.115), calls=%async_computation.3 | async-start | bytes 2097152 | tf_op jit(solution)/shard_map/all_to_all | solution.py:952
  371.6 110.5 %reduce-scatter.9.cloned.1.call-start = ((), (), s32[]{:S(2)}) async-start(), calls=%async_computation.12 | async-start | bytes 3932160 | tf_op jit(solution)/shard_map/reduce_scatter | solution.py:948
  425.3 54.6 %collective-permute-start = (bf16[2,64,2048]{2,1,0:T(8,128)(2,1)}, bf16[2,64,2048]{2,1,0:T(8,128)(2,1)}, u32[]{:S(2)}, u32[]{:S(2)}) collective-permute-start(bf16[2,64,2048]{2,1,0:T(8,128)(2,1)} %dynamic-slice_bitcast_fusion), channel_id=1, source_target_pairs={{0,1},{1,0},{2,3},{3,2},{4,5},{5,4},{6,7},{7,6},{8,9},{9,8},{10,11... | collective-permute-start | bytes 1572872 | tf_op jit(solution)/shard_map/ppermute | solution.py:979
  425.3 56.8 %all-to-all-start.2 = ((bf16[8,64,1024]{2,1,0:T(8,128)(2,1)}), bf16[8,64,1024]{2,1,0:T(8,128)(2,1)}, u32[]{:S(2)}, u32[]{:S(2)}) async-start(bf16[8,64,1024]{2,1,0:T(8,128)(2,1)} %bitcast.114), calls=%async_computation.4 | async-start | bytes 2097152 | tf_op jit(solution)/shard_map/all_to_all | solution.py:952
  429.6 86.4 %reduce-scatter.11.cloned.1.call-start = ((), (), s32[]{:S(2)}) async-start(), calls=%async_computation.13 | async-start | bytes 1310720 | tf_op jit(solution)/shard_map/reduce_scatter | solution.py:989
  429.7 50.3 %copy-start.5 = (bf16[256,2048]{1,0:T(8,128)(2,1)S(1)}, bf16[256,2048]{1,0:T(8,128)(2,1)}, u32[]{:S(2)}) copy-start(bf16[256,2048]{1,0:T(8,128)(2,1)} %get-tuple-element.70) | copy-start | bytes 3145732
  482.2 2.6 copy-start.10
  502.5 7.0 %copy-start.8 = (f32[8,1024]{1,0:T(8,128)S(1)}, f32[8,1024]{1,0:T(8,128)}, u32[]{:S(2)}) copy-start(f32[8,1024]{1,0:T(8,128)} %get-tuple-element.83) | copy-start | bytes 98308
  510.7 7.1 %copy-start.1 = (s32[1,1024]{1,0:T(1,128)S(1)}, s32[1,1024]{1,0:T(1,128)}, u32[]{:S(2)}) copy-start(s32[1,1024]{1,0:T(1,128)} %param.13) | copy-start | bytes 12292
Sparse Core Ops, SparseCore 0:
  10.2 84.7 all-gather.4
  96.6 80.6 all-gather.6
  179.5 80.5 all-gather.8
  262.3 75.2 reduce-scatter.4
  339.8 77.3 reduce-scatter.6
  423.6 57.5 reduce-scatter.8
  483.5 29.2 reduce-scatter.10

commit v7 on v6

--- a/solution.py
+++ b/solution.py
@@ -185,7 +185,7 @@
 
 
 def attended_back_kernel(
-    chips, pieces, x_ref, w_ref, h_ref, g_ref, s_ref, x_v, own_sem, *sems
+    chips, pieces, x_ref, w_ref, h_ref, g_ref, s_ref, x_v, total, own_sem, *sems
 ):
     c, k = lax.axis_index("ctx"), lax.axis_index("core")
     rows = x_ref.shape[0]
@@ -201,12 +201,11 @@
     def on_block(core, m):
         span = span_of(core, m)
         g_ref[span, :] = contract_last(x_v[span, :], w_ref[...]).astype(BF16)
-
+        total[...] += contract_first(h_ref[span, :], x_v[span, :])
+
+    total[...] = jnp.zeros_like(total)
     gather(chips, pieces, sems, x_ref, x_v, (), on_block)
-    tile = 512
-    for i in range(x_v.shape[1] // tile):
-        span = slice(i * tile, (i + 1) * tile)
-        s_ref[:, span] = contract_first(h_ref[...], x_v[:, span]).astype(BF16)
+    s_ref[...] = total[...].astype(BF16)
 
 
 def attended_back(x, w, attended, chips, ident, pieces=2):
@@ -224,6 +223,7 @@
         out_specs=[in_vmem] * 2,
         scratch_shapes=[
             pltpu.VMEM((total, cols), BF16),
+            pltpu.VMEM((attended.shape[1], cols), F32),
             pltpu.SemaphoreType.DMA,
             *gather_scratch(chips, pieces),
         ],

time: 528 us -> 528 us (level)
  no operation moved by 1% of the time
where the time goes in v7:
time: 528 us; the launch traced here: 524 us
  Pallas kernels  419 us (79%)
  matrix products  39.6 us (8%)
  other arithmetic  18.8 us (4%)
  between operations  14.8 us (3%)
  starting transfers between devices  12.6 us (2%)
  local copies, waits for them, and re-layouts  12.3 us (2%)
    pallas_call x3, Pallas kernels, product_scatter(): pl.pallas_call(functools.partial(product_scatter_kernel, chips, transpose...  146 us
    pallas_call x3, Pallas kernels, plane_gather(): pl.pallas_call(functools.partial(gather_kernel, chips, pieces), name='pla...  120 us
    pallas_call x1, Pallas kernels, hidden_back(): pl.pallas_call(functools.partial(hidden_back_kernel, chips, tile), name='...  60.7 us
    pallas_call x1, Pallas kernels, attended_back(): pl.pallas_call(functools.partial(attended_back_kernel, chips, pieces), na...  44 us
    pallas_call x1, Pallas kernels, deal(): pl.pallas_call(functools.partial(deal_kernel, chips, planes), name='deal'...  17.6 us
    pallas_call x1, Pallas kernels, attend(): pl.pallas_call(functools.partial(attend_kernel, heads, size, 256), name='...  16.2 us
    dot_general x1, matrix products, shards(): pre_act = jnp.dot(acts_two, my_up, preferred_element_type=F32)  15.4 us
    dot_general x1, matrix products, contract_first(): lax.dot_general(left_arr, right_arr, (((0,), (0,)), ((), ())), preferred_...  12.9 us
  transfers between devices with their start and end apart: 11, of which 1 were waited for; matrix products, arithmetic and copies ran while one was open for 13% of the time, Pallas kernels for 80%

profile of v7, /device:TPU:0, one launch (start us, length us, event | category | flops | bytes accessed | tf_op | source)
XLA Modules:
  0.0 523.8 jit_solution(15696540459314138454)
XLA Ops:
  7.2 2.4 pick_columns.3
  10.5 1.4 fusion.20.x_ref
  11.9 41.5 %plane_gather.3.refs_7_ = bf16[2048,2048]{1,0:T(8,128)(2,1)} custom-call(bf16[256,2048]{1,0:T(8,128)(2,1)} %fusion.20.x_ref), custom_call_target="tpu_custom_call" | custom-call | flops 1000000000 | tf_op jit(solution)/shard_map/plane_gather/pallas_call | solution.py:175
  53.4 2.2 pick_columns.4
  55.8 2.3 pick_columns.5
  58.8 1.9 all-gather.query_blk.refs_5_
  60.7 1.3 broadcast_in_dim.43.key_blk.refs_4_
  62.0 39.7 %plane_gather.5.g_ref = bf16[2048,2048]{1,0:T(8,128)(2,1)} custom-call(bf16[256,2048]{1,0:T(8,128)(2,1)} %bitcast.113), custom_call_target="tpu_custom_call" | custom-call | flops 1000000000 | tf_op jit(solution)/shard_map/plane_gather/pallas_call | solution.py:175
  101.8 2.4 constant_dynamic-slice_fusion
  104.2 3.6 all-to-all-start
  108.0 11.2 %convolution_convert_fusion.1.p_ref.refs_2_ = bf16[2048,768]{1,0:T(8,128)(2,1)} fusion(bf16[2048,2048]{1,0:T(8,128)(2,1)} %plane_gather.3.refs_7_, bf16[2048,2048]{1,0:T(8,128)(2,1)} %all-gather.5.cloned.1.call-done.refs_1_, s32[]{:T(128)S(6)} %select_n.41), kind=kOutput, calls=%fused_computation.13 | convolution fusion | flops 6444023808 | bytes 14680068 | tf_op jit(solution)/shard_map/dot_general | solution.py:936
  119.2 16.2 %attend.1 = (bf16[2048,256]{1,0:T(8,128)(2,1)}, f32[2,2,1024]{2,1,0:T(2,128)}) custom-call(bf16[2048,768]{1,0:T(8,128)(2,1)} %convolution_convert_fusion.1.p_ref.refs_2_, s32[2,1024,1]{2,1,0:T(8,128)} %broadcast_in_dim.43.key_blk.refs_4_, s32[2,1,1024]{2,1,0:T(1,128)} %copy-done.6), custom_call_target="tpu_custom_call" | custom-call | flops 1000000000 | tf_op jit(solution)/shard_map/attend/pallas_call | solution.py:865
  136.6 44.4 %product_scatter.3 = f32[256,2048]{1,0:T(8,128)} custom-call(bf16[2048,256]{1,0:T(8,128)(2,1)} %get-tuple-element.49.refs_0_.h_ref, bf16[256,2048]{1,0:T(8,128)(2,1)} %bitcast.110), custom_call_target="tpu_custom_call" | custom-call | flops 1000000000 | tf_op jit(solution)/shard_map/product_scatter/pallas_call | solution.py:521
  181.0 2.1 fusion.30
  183.8 2.2 add_convert_fusion.1
  186.0 39.1 %plane_gather.4.a_ref = bf16[2048,2048]{1,0:T(8,128)(2,1)} custom-call(bf16[256,2048]{1,0:T(8,128)(2,1)} %get-tuple-element.88.x_ref), custom_call_target="tpu_custom_call" | custom-call | flops 1000000000 | tf_op jit(solution)/shard_map/plane_gather/pallas_call | solution.py:175
  225.2 15.4 %fusion.34 = (bf16[2048,1024]{1,0:T(8,128)(2,1)}, bf16[2048,1024]{1,0:T(8,128)(2,1)S(1)}) fusion(bf16[2048,2048]{1,0:T(8,128)(2,1)} %plane_gather.4.a_ref, bf16[2048,2048]{1,0:T(8,128)(2,1)} %all-gather.7.cloned.1.call-done.u_ref, s32[]{:T(128)S(6)} %select_n.41), kind=kOutput, calls=%fused_computation.71 | convolution fusion | flops 8610906112 | bytes 20971524 | tf_op jit(solution)/shard_map/dot_general | solution.py:943
  240.6 2.1 copy-done.4
  242.6 12.9 %convolution_convert_fusion = bf16[2048,1024]{1,0:T(8,128)(2,1)} fusion(bf16[2048,2048]{1,0:T(8,128)(2,1)} %plane_gather.5.g_ref, bf16[2048,1024]{1,0:T(8,128)(2,1)S(1)} %get-tuple-element.91.refs_0_), kind=kOutput, calls=%fused_computation.12 | convolution fusion | flops 8592031744 | bytes 16777216 | tf_op jit(solution)/shard_map/dot_general | solution.py:49
  255.6 4.5 all-gather.9.cloned.1.call-done.d_ref.refs_1_
  261.0 60.7 %hidden_back.1 = (f32[256,2048]{1,0:T(8,128)}, bf16[256,2048]{1,0:T(8,128)(2,1)}, f32[2,2048]{1,0:T(2,128)}, bf16[2048,1024]{1,0:T(8,128)(2,1)}) custom-call(bf16[2048,2048]{1,0:T(8,128)(2,1)} %plane_gather.5.g_ref, bf16[2048,2048]{1,0:T(8,128)(2,1)} %all-gather.9.cloned.1.call-done.d_ref.refs_1_, bf16[2048,1024]{1,0:T(8,128)(2,1)} %get-tuple-element.90.p_ref, ...), custom_call_target="tpu_custom_call" | custom-call | flops 1000000000 | tf_op jit(solution)/shard_map/hidden_back/pallas_call | solution.py:639
  321.7 44.0 %attended_back.1 = (bf16[2048,256]{1,0:T(8,128)(2,1)}, bf16[256,2048]{1,0:T(8,128)(2,1)}) custom-call(bf16[256,2048]{1,0:T(8,128)(2,1)} %get-tuple-element.56.x_ref, bf16[256,2048]{1,0:T(8,128)(2,1)} %bitcast.111, bf16[2048,256]{1,0:T(8,128)(2,1)} %get-tuple-element.49.refs_0_.h_ref), custom_call_target="tpu_custom_call" | custom-call | flops 1000000000 | tf_op jit(solution)/shard_map/attended_back/pallas_call | solution.py:215
  365.7 4.3 all-to-all-start.1
  370.0 51.6 %product_scatter.4 = (f32[256,2048]{1,0:T(8,128)}, bf16[2048,768]{1,0:T(8,128)(2,1)}, bf16[2048,768]{1,0:T(8,128)(2,1)}) custom-call(bf16[2048,1024]{1,0:T(8,128)(2,1)} %copy-done.4, bf16[2048,2048]{1,0:T(8,128)(2,1)} %all-gather.9.cloned.1.call-done.d_ref.refs_1_, bf16[2048,768]{1,0:T(8,128)(2,1)} %convolution_convert_fusion.1.p_ref.refs_2_, ...), custom_call_target="tpu_custom_call" | custom-call | flops 1000000000 | tf_op jit(solution)/shard_map/product_scatter/pallas_call | solution.py:521
  421.7 1.9 dynamic-slice_bitcast_fusion
  423.6 4.3 all-to-all-start.2
  428.0 50.2 %product_scatter.5 = f32[256,2048]{1,0:T(8,128)} custom-call(bf16[2048,768]{1,0:T(8,128)(2,1)} %get-tuple-element.69.refs_0_, bf16[2048,2048]{1,0:T(8,128)(2,1)} %all-gather.5.cloned.1.call-done.refs_1_), custom_call_target="tpu_custom_call" | custom-call | flops 1000000000 | tf_op jit(solution)/shard_map/product_scatter/pallas_call | solution.py:521
  480.5 2.6 fusion.26
  483.8 17.6 %deal.1 = (bf16[8,64,768]{2,1,0:T(8,128)(2,1)}, f32[8,1024]{1,0:T(8,128)}) custom-call(bf16[8,64,768]{2,1,0:T(8,128)(2,1)} %bitcast.118, f32[8,1024]{1,0:T(8,128)} %reshape.160.x_ref), custom_call_target="tpu_custom_call" | custom-call | tf_op jit(solution)/shard_map/deal/pallas_call | solution.py:762
  501.4 7.0 %whole_columns.1 = (f32[64,6144]{1,0:T(8,128)}, f32[64,8192]{1,0:T(8,128)}, f32[64,8192]{1,0:T(8,128)}) custom-call(bf16[8,64,768]{2,1,0:T(8,128)(2,1)} %get-tuple-element.76.refs_0_, bf16[8,64,1024]{2,1,0:T(8,128)(2,1)} %all-to-all-done.2.refs_1_, bf16[8,64,1024]{2,1,0:T(8,128)(2,1)} %all-to-all-done.1.refs_2_), custom_call_target="tpu_custom_call" | custom-call | tf_op jit(solution)/shard_map/whole_columns/pallas_call | solution.py:748
  509.7 5.3 %fusion.29 = (bf16[1,256,2048]{2,1,0:T(8,128)(2,1)}, bf16[1,256,2048]{2,1,0:T(8,128)(2,1)}) fusion(f32[256,2048]{1,0:T(8,128)} %get-tuple-element.63, bf16[1,256,2048]{2,1,0:T(8,128)(2,1)S(1)} %copy-done.2, f32[256,2048]{1,0:T(8,128)} %product_scatter.5, f32[256]{0:T(256)S(1)} %get-tuple-element.100, f32[256]{0:T(256)S(1)} %get-tuple-element.101, ...), kind=kLoop, calls=%fused_computation.40 | loop fusion | flops 6815744 | bytes 11546624 | tf_op jit(solution)/shard_map/convert_element_type | solution.py:1008
  515.0 1.8 bitcast_convert_fusion
  (76 shorter events, 8.9 us)
Async XLA Ops:
  7.2 50.9 %copy-start = (s32[1,1024]{1,0:T(1,128)S(1)}, s32[1,1024]{1,0:T(1,128)}, u32[]{:S(2)}) copy-start(s32[1,1024]{1,0:T(1,128)} %param.13) | copy-start | bytes 12292
  7.2 2.6 copy-start.2
  7.2 94.6 %all-gather.5.cloned.1.call-start = ((), (), s32[]{:S(2)}) async-start(), calls=%async_computation.7 | async-start | bytes 9437184 | tf_op jit(solution)/shard_map/all_gather | solution.py:909
  9.7 0.8 copy-start.7
  9.7 0.8 copy-start.11
  9.7 215.4 %all-gather.7.cloned.1.call-start = ((), (), s32[]{:S(2)}) async-start(), calls=%async_computation.8 | async-start | bytes 9437184 | tf_op jit(solution)/shard_map/all_gather | solution.py:909
  55.7 2.4 copy-start.13
  55.7 204.4 %all-gather.9.cloned.1.call-start = ((), (), s32[]{:S(2)}) async-start(), calls=%async_computation.9 | async-start | bytes 9437184 | tf_op jit(solution)/shard_map/all_gather | solution.py:909
  60.7 41.1 %copy-start.6 = (s32[2,1,1024]{2,1,0:T(1,128)}, s32[2,1,1024]{2,1,0:T(1,128)S(1)}, u32[]{:S(2)}) copy-start(s32[2,1,1024]{2,1,0:T(1,128)S(1)} %all-gather.query_blk.refs_5_) | copy-start | bytes 24580
  104.2 31.3 %all-to-all-start = ((bf16[8,256,256]{2,1,0:T(8,128)(2,1)}), bf16[8,256,256]{2,1,0:T(8,128)(2,1)S(1)}, u32[]{:S(2)}, u32[]{:S(2)}) async-start(bf16[8,256,256]{2,1,0:T(8,128)(2,1)} %bitcast.5), calls=%async_computation | async-start | bytes 2097152 | tf_op jit(solution)/shard_map/all_to_all | solution.py:935
  107.7 258.0 %reduce-scatter.5.cloned.1.call-start = ((), (), s32[]{:S(2)}) async-start(), calls=%async_computation.10 | async-start | bytes 5242880 | tf_op jit(solution)/shard_map/reduce_scatter | solution.py:948
  181.0 2.2 copy-start.3
  183.0 0.7 copy-start.9
  183.0 0.7 copy-start.12
  240.6 2.1 copy-start.4
  260.1 161.5 %reduce-scatter.7.cloned.1.call-start = ((), (), s32[]{:S(2)}) async-start(), calls=%async_computation.11 | async-start | bytes 5242880 | tf_op jit(solution)/shard_map/reduce_scatter | solution.py:948
  365.7 56.0 %all-to-all-start.1 = ((bf16[8,64,1024]{2,1,0:T(8,128)(2,1)}), bf16[8,64,1024]{2,1,0:T(8,128)(2,1)}, u32[]{:S(2)}, u32[]{:S(2)}) async-start(bf16[8,64,1024]{2,1,0:T(8,128)(2,1)} %bitcast.115), calls=%async_computation.3 | async-start | bytes 2097152 | tf_op jit(solution)/shard_map/all_to_all | solution.py:952
  370.0 110.5 %reduce-scatter.9.cloned.1.call-start = ((), (), s32[]{:S(2)}) async-start(), calls=%async_computation.12 | async-start | bytes 3932160 | tf_op jit(solution)/shard_map/reduce_scatter | solution.py:948
  423.6 54.6 %collective-permute-start = (bf16[2,64,2048]{2,1,0:T(8,128)(2,1)}, bf16[2,64,2048]{2,1,0:T(8,128)(2,1)}, u32[]{:S(2)}, u32[]{:S(2)}) collective-permute-start(bf16[2,64,2048]{2,1,0:T(8,128)(2,1)} %dynamic-slice_bitcast_fusion), channel_id=1, source_target_pairs={{0,1},{1,0},{2,3},{3,2},{4,5},{5,4},{6,7},{7,6},{8,9},{9,8},{10,11... | collective-permute-start | bytes 1572872 | tf_op jit(solution)/shard_map/ppermute | solution.py:979
  423.6 56.9 %all-to-all-start.2 = ((bf16[8,64,1024]{2,1,0:T(8,128)(2,1)}), bf16[8,64,1024]{2,1,0:T(8,128)(2,1)}, u32[]{:S(2)}, u32[]{:S(2)}) async-start(bf16[8,64,1024]{2,1,0:T(8,128)(2,1)} %bitcast.114), calls=%async_computation.4 | async-start | bytes 2097152 | tf_op jit(solution)/shard_map/all_to_all | solution.py:952
  427.9 87.1 %reduce-scatter.11.cloned.1.call-start = ((), (), s32[]{:S(2)}) async-start(), calls=%async_computation.13 | async-start | bytes 1310720 | tf_op jit(solution)/shard_map/reduce_scatter | solution.py:989
  428.0 50.3 %copy-start.5 = (bf16[256,2048]{1,0:T(8,128)(2,1)S(1)}, bf16[256,2048]{1,0:T(8,128)(2,1)}, u32[]{:S(2)}) copy-start(bf16[256,2048]{1,0:T(8,128)(2,1)} %get-tuple-element.70) | copy-start | bytes 3145732
  480.5 2.6 copy-start.10
  501.4 7.0 %copy-start.8 = (f32[8,1024]{1,0:T(8,128)S(1)}, f32[8,1024]{1,0:T(8,128)}, u32[]{:S(2)}) copy-start(f32[8,1024]{1,0:T(8,128)} %get-tuple-element.83) | copy-start | bytes 98308
  509.7 7.1 %copy-start.1 = (s32[1,1024]{1,0:T(1,128)S(1)}, s32[1,1024]{1,0:T(1,128)}, u32[]{:S(2)}) copy-start(s32[1,1024]{1,0:T(1,128)} %param.13) | copy-start | bytes 12292
Sparse Core Ops, SparseCore 0:
  10.2 84.7 all-gather.4
  96.6 80.6 all-gather.6
  179.5 80.5 all-gather.8
  262.3 75.2 reduce-scatter.4
  339.8 77.2 reduce-scatter.6
  421.8 58.1 reduce-scatter.8
  482.4 29.2 reduce-scatter.10
